TPU v7x, 32 devices: a whole 2x2x4 slice. The times are simulated.
32 devices in a mesh: gx: 2 (over x), gy: 4 (over z), gz: 4 (over y, core).
Axes of the slice: x: 2, y: 2, z: 4, core: 2. Of those that a mesh axis runs over, the one named last changes fastest.
Arguments:
- perturb: float32 [27, 16, 64, 512], P(None, 'gx', 'gy', 'gz'), may hold values from -2.5 to 2.5
- density: float32 [16, 64, 512], P('gx', 'gy', 'gz'), may hold values from 0.9 to 1.1
- velocity: float32 [3, 16, 64, 512], P(None, 'gx', 'gy', 'gz'), may hold values from -0.12 to 0.12
- excitation: float32 [16, 64, 512], P('gx', 'gy', 'gz'), may hold values from 0.0001 to 0.2
- solid_flag: int32 [16, 64, 512], P('gx', 'gy', 'gz'), may hold values 0 or 1
- panel_cell: int32 [8192], P(('gx', 'gy', 'gz')), may hold values from 0 to 16383
- panel_owner: int32 [8192], P(('gx', 'gy', 'gz')), may hold values from 0 to 7, as said below
- panel_area: float32 [3, 8192], P(None, ('gx', 'gy', 'gz')), may hold values from -4 to 4
- weights: bfloat16 [4, 16384, 1024], P(None, ('gx', 'gy', 'gz')), may hold values from -1.796875 to 1.796875
- bin_offset: int32 [256, 8], P(('gx', 'gy', 'gz')), may hold values from 0 to 124
Outputs:
- final_density: float32 [16, 64, 512], P('gx', 'gy', 'gz')
- final_velocity: float32 [3, 16, 64, 512], P(None, 'gx', 'gy', 'gz')
- signal: float32 [1024, 128], P(('gx', 'gy', 'gz'))
Inputs may be any that keep to these rules, and one draw needn't show every extreme that they name: `panel_owner`: the slots of a device name owners of its vertical layer; at most 64 slots of one device name the same owner, and in each vertical layer one owner is named by exactly 64 slots of every device of the layer.
All inputs are finite; a program needn't handle non-finite values. No bound on the sum of `solid_flag` on one device may be relied on, other than what follows from the above.
Results may differ from a plain program's by a relative error of at most 0.0029.
Values may be sent and summed in bfloat16 or wider, within the bound.
No kernel may reach another device: no remote copies, remote signals or barrier semaphores. Data moves between devices by JAX's collectives and lax.ppermute only.
A program may use at most 128 MiB of HBM per device.

v0:
```python
import functools
import jax
import jax.numpy as jnp
from jax import lax
from jax.experimental import pallas as pl
from jax.experimental.pallas import tpu as pltpu
from jax.sharding import PartitionSpec as P


STEPS = 4
NB = 128
BETA = 0.99
FLOOR = 1e-06
LANES = 128
ROWS = 160
FIRST = 16
TILES = 18
HALO_ROWS = 8 * TILES
HALO_TYPE = jnp.bfloat16
F32 = jnp.float32


VELS = [(i // 9 - 1, (i // 3) % 3 - 1, i % 3 - 1) for i in range(27)]
WEIGHT = [float([8 / 27, 2 / 27, 1 / 54, 1 / 216][sum(abs(a) for a in c)]) for c in VELS]


def pop(cx, cy, cz):
    return (cx + 1) * 9 + (cy + 1) * 3 + cz + 1


def x_place(cx, cy, cz):
    j = (cy + 1) * 3 + cz + 1
    if j < 8:
        return (0 if cx > 0 else 1), 16 * j
    return 2, (0 if cx > 0 else 64)


def x_flag_place(cx):
    return 2, (16 if cx > 0 else 80)


def y_slot(cx, cz):
    return (cx + 1) * 3 + cz + 1


def y_flag_slot(cx):
    return 9 + cx + 1


def lane_iota():
    return lax.broadcasted_iota(jnp.int32, (8, LANES), 1)


def turn(v, shift):
    shift %= LANES
    return v if shift == 0 else pltpu.roll(v, shift, 1)


def x_pattern(lane, a):
    out = jnp.zeros((8, LANES), F32)
    for cx in (1, -1):
        for cy in (-1, 0, 1):
            for cz in (-1, 0, 1):
                b, base = x_place(cx, cy, cz)
                if b == a:
                    out = jnp.where(lane // 16 == base // 16, WEIGHT[pop(cx, cy, cz)], out)
    return out


def y_pattern(lane):
    out = jnp.zeros((8, LANES), F32)
    for cx in (-1, 0, 1):
        for cz in (-1, 0, 1):
            out = jnp.where(lane % 16 == y_slot(cx, cz), WEIGHT[pop(cx, 1, cz)], out)
    return out


def moments(f):
    def total(vals):
        vals = list(vals)
        while len(vals) > 1:
            vals = [a + b for a, b in zip(vals[::2], vals[1::2])] + ([vals[-1]] if len(vals) % 2 else [])
        return vals[0]

    s = {}
    d = {}
    e = {}
    for cx in (-1, 0, 1):
        for cy in (-1, 0, 1):
            lo, mid, hi = f[pop(cx, cy, -1)], f[pop(cx, cy, 0)], f[pop(cx, cy, 1)]
            e[cx, cy] = lo + hi
            d[cx, cy] = hi - lo
            s[cx, cy] = mid + e[cx, cy]
    rows = {cx: s[cx, -1] + s[cx, 1] for cx in (-1, 0, 1)}
    full = {cx: rows[cx] + s[cx, 0] for cx in (-1, 0, 1)}
    dsum = {cx: d[cx, -1] + d[cx, 0] + d[cx, 1] for cx in (-1, 0, 1)}
    sxx = full[-1] + full[1]
    rho = sxx + full[0]
    jx = full[1] - full[-1]
    ydif = {cx: s[cx, 1] - s[cx, -1] for cx in (-1, 0, 1)}
    jy = ydif[-1] + ydif[0] + ydif[1]
    jz = dsum[-1] + dsum[0] + dsum[1]
    syy = rows[-1] + rows[0] + rows[1]
    szz = total([e[k] for k in e])
    sxy = ydif[1] - ydif[-1]
    sxz = dsum[1] - dsum[-1]
    syz = (d[-1, 1] + d[0, 1] + d[1, 1]) - (d[-1, -1] + d[0, -1] + d[1, -1])
    return rho, jx, jy, jz, sxx, syy, szz, sxy, sxz, syz


def collide(f, mom):
    rho, jx, jy, jz, sxx, syy, szz, sxy, sxz, syz = mom
    inv = 1.0 / rho
    ux, uy, uz = jx * inv, jy * inv, jz * inv
    pxx, pyy, pzz = sxx - jx * ux, syy - jy * uy, szz - jz * uz
    pxy, pxz, pyz = sxy - jx * uy, sxz - jx * uz, syz - jy * uz
    third = (pxx + pyy + pzz) * (1.0 / 3.0)
    qx, qy, qz = 4.5 * (pxx - third), 4.5 * (pyy - third), 4.5 * (pzz - third)
    qxy, qxz, qyz = 9.0 * pxy, 9.0 * pxz, 9.0 * pyz
    base = 1.0 - 1.5 * (ux * ux + uy * uy + uz * uz)
    rest = rho * base
    rho3 = 3.0 * rho
    rho45 = 4.5 * rho
    cross = None
    squares = {}
    higher = [None] * 27
    shear = [None] * 27
    for i in range(14):
        c = VELS[i]
        w = WEIGHT[i]
        cls = sum(abs(a) for a in c)
        if i == 13:
            h = f[13] - w * rest
            higher[13] = h
            squares[0] = h * h
            continue
        cu = None
        for a, u in zip(c, (ux, uy, uz)):
            if a:
                cu = (u if a > 0 else -u) if cu is None else (cu + u if a > 0 else cu - u)
        q = None
        for a, v in zip(c, (qx, qy, qz)):
            if a:
                q = v if q is None else q + v
        for a, b, v in ((c[0], c[1], qxy), (c[0], c[2], qxz), (c[1], c[2], qyz)):
            if a * b > 0:
                q = q + v
            elif a * b < 0:
                q = q - v
        even = w * (rest + rho45 * (cu * cu) + q)
        odd = (w * rho3) * cu
        hp = f[i] - even - odd
        hm = f[26 - i] - even + odd
        higher[i], higher[26 - i] = hp, hm
        shear[i] = shear[26 - i] = q
        term = q * (hp + hm)
        cross = term if cross is None else cross + term
        sq = hp * hp + hm * hm
        squares[cls] = sq if cls not in squares else squares[cls] + sq
    norm = squares[0] * (27.0 / 8.0) + squares[1] * 13.5 + squares[2] * 54.0 + squares[3] * 216.0
    gamma = 1.0 / BETA - (2.0 - 1.0 / BETA) * cross / jnp.maximum(norm, FLOOR)
    bg = BETA * gamma
    star = []
    for i in range(27):
        v = f[i] - bg * higher[i]
        if i != 13:
            v = v - (2.0 * BETA * WEIGHT[i]) * shear[i]
        star.append(v)
    return star, (rho, ux, uy, uz)


def pack(star, flag, lane, patterns):
    group = lane // 16
    slot = lane % 16
    xs = [jnp.zeros((8, LANES), F32) for _ in range(3)]
    for cx in (1, -1):
        source = 112 if cx > 0 else 0
        for cy in (-1, 0, 1):
            for cz in (-1, 0, 1):
                a, base = x_place(cx, cy, cz)
                xs[a] = jnp.where(group == base // 16, turn(star[pop(cx, cy, cz)], base - source), xs[a])
        if flag is not None:
            a, base = x_flag_place(cx)
            xs[a] = jnp.where(group == base // 16, turn(flag, base - source), xs[a])
    ys = []
    for cy in (1, -1):
        edge = 15 if cy > 0 else 0
        acc = jnp.zeros((8, LANES), F32)
        for cx in (-1, 0, 1):
            for cz in (-1, 0, 1):
                j = y_slot(cx, cz)
                acc = jnp.where(slot == j, turn(star[pop(cx, cy, cz)], 16 * cx + j - edge), acc)
            if flag is not None:
                j = y_flag_slot(cx)
                acc = jnp.where(slot == j, turn(flag, 16 * cx + j - edge), acc)
        ys.append(acc)
    return [v - p for v, p in zip(xs + ys, patterns)]


def corner_lanes(lane, cx):
    col = 0 if cx > 0 else 112
    slots = [y_slot(cx, cz) for cz in (-1, 0, 1)] + [y_flag_slot(cx)]
    out = lane == col + slots[0]
    for j in slots[1:]:
        out = out | (lane == col + j)
    return out


def corners(yp, ym):
    lane = lax.broadcasted_iota(jnp.int32, yp.shape, 1)
    up = corner_lanes(lane, 1) | corner_lanes(lane, -1)
    return jnp.where(up, yp, turn(ym, 16))


def all_patterns(lane):
    yp = y_pattern(lane)
    return [x_pattern(lane, 0), x_pattern(lane, 1), x_pattern(lane, 2), yp, yp]


def initial_kernel(perturb_hbm, density_hbm, velocity_hbm, excitation_hbm, solid_hbm, f_out, lo_out, hi_out, s_out,
                   perturb, density, velocity, excitation, solid, chunk_sem, sem):
    small = [
        pltpu.make_async_copy(src, dst, sem.at[k])
        for k, (src, dst) in enumerate(((density_hbm, density), (velocity_hbm, velocity),
                                        (excitation_hbm, excitation), (solid_hbm, solid)))
    ]
    for copy in small:
        copy.start()
    chunks = [
        pltpu.make_async_copy(perturb_hbm.at[pl.ds(3 * k, 3)], perturb.at[pl.ds(3 * k, 3)], chunk_sem.at[k])
        for k in range(9)
    ]
    for copy in chunks:
        copy.start()
    for copy in small:
        copy.wait()
    rho = density[...]
    ux, uy, uz = velocity[0], velocity[1], velocity[2]
    amplitude = excitation[...]
    base = 1.0 - 1.5 * (ux * ux + uy * uy + uz * uz)

    def put(i, v, out):
        out[FIRST : FIRST + 128, :] = v
        lo_out[4 * i : 4 * i + 4, :] = v[0:4, :]
        hi_out[4 * i : 4 * i + 4, :] = v[124:128, :]

    put(27, solid[...].astype(F32).T, s_out)
    for i in range(27):
        c = VELS[i]
        shape = base
        cu = None
        for a, u in zip(c, (ux, uy, uz)):
            if a:
                cu = (u if a > 0 else -u) if cu is None else (cu + u if a > 0 else cu - u)
        if cu is not None:
            shape = shape + 3.0 * cu + 4.5 * (cu * cu)
        if i % 3 == 0:
            chunks[i // 3].wait()
        v = (WEIGHT[i] * rho) * shape * (1.0 + amplitude * perturb[i])
        put(i, v.T, f_out.at[i])


def pack_tile(t, star_ref, flag_ref, lane, patterns, x_tmp, y_tmp):
    at = pl.ds(pl.multiple_of(8 * t, 8), 8)
    flag = None if flag_ref is None else flag_ref[at, :]
    packed = pack([star_ref[i, at, :] for i in range(27)], flag, lane, patterns)
    row = pl.ds(pl.multiple_of(8 * t - 8, 8), 8)
    for a in range(3):
        x_tmp[a, row, :] = packed[a]
    y_tmp[0, row, :] = packed[3]
    y_tmp[1, row, :] = packed[4]


def first_kernel(f_in, s_in, lo, hi, unused, star_out, s_out, xp_out, yp_out, ym_out, xc_out, edge, x_tmp, y_tmp):
    lane = lane_iota()
    patterns = all_patterns(lane)
    for i in range(28):
        below = lo[4 * i : 4 * i + 4, :]
        above = hi[4 * i : 4 * i + 4, :]
        edge[i, 0:4, :] = below
        edge[i, 4:8, :] = below
        edge[i, 8:12, :] = above
        edge[i, 12:16, :] = above

    def emit(t, load):
        f = [load(i) for i in range(27)]
        star, _ = collide(f, moments(f))
        at = pl.ds(pl.multiple_of(8 * t, 8), 8)
        for i in range(27):
            star_out[i, at, :] = star[i]
        s_out[at, :] = load(27)

    def pack_at(t):
        pack_tile(t, star_out, s_out, lane, patterns, x_tmp, y_tmp)

    def outer(k, carry):
        at = pl.ds(pl.multiple_of(8 * k, 8), 8)
        emit(1 + 17 * k, lambda i: edge[i, at, :])
        return carry

    def inner(k, carry):
        t = k + 2
        pack_at(t - 1)
        at = pl.ds(pl.multiple_of(8 * t, 8), 8)
        emit(t, lambda i: s_in[at, :] if i == 27 else f_in[i, at, :])
        return carry

    lax.fori_loop(0, 2, outer, 0)
    lax.fori_loop(0, 16, inner, 0)
    pack_at(17)
    pack_at(18)
    xp_out[...] = x_tmp[...].astype(xp_out.dtype)
    yp_out[...] = y_tmp[0].astype(yp_out.dtype)
    ym_out[...] = y_tmp[1].astype(ym_out.dtype)
    xc_out[...] = corners(y_tmp[0], y_tmp[1]).astype(xc_out.dtype)


def patch_kernel(low, high, yp_in, ym_in, yp_out, ym_out):
    lane = lax.broadcasted_iota(jnp.int32, (HALO_ROWS, LANES), 1)
    for shift, source, out in ((0, yp_in, yp_out), (-16, ym_in, ym_out)):
        acc = source[...].astype(F32)
        for cx, got in ((1, low), (-1, high)):
            acc = jnp.where(corner_lanes(lane, cx), turn(got[...].astype(F32), shift), acc)
        out[...] = acc.astype(out.dtype)


def step_kernel(first, last, *refs):
    refs = list(refs)
    star_in, s_in, xh, yph, ymh, _ = refs[:6]
    refs = refs[6:]
    if last:
        mom_out = refs.pop(0)
        star_out = None
    else:
        mom_out, star_out, xp_out, yp_out, ym_out, xc_out = refs[:6]
        refs = refs[6:]
    if first:
        wall_ref = refs.pop(0)
    else:
        wall_ref = s_in
    xs, ys = refs[:2]
    lane = lane_iota()
    patterns = all_patterns(lane)
    slot = lane % 16
    halo = pl.ds(8, HALO_ROWS)

    def tall(v):
        return jnp.concatenate([v] * TILES, axis=0)

    for a in range(3):
        xs[a, halo, :] = xh[a].astype(F32) + tall(patterns[a])
    ys[0, halo, :] = yph[...].astype(F32) + tall(patterns[3])
    ys[1, halo, :] = ymh[...].astype(F32) + tall(patterns[4])
    edge_rows = (pl.ds(0, 8), pl.ds(ROWS - 8, 8))
    for at in edge_rows:
        for a in range(3):
            xs[a, at, :] = jnp.zeros((8, LANES), F32)
        for a in range(2):
            ys[a, at, :] = jnp.zeros((8, LANES), F32)
        if first:
            for k in range(9):
                wall_ref[k, at, :] = jnp.zeros((8, LANES), F32)

    def gather(v, cx, cy, x_at, x_load, y_slot_of, y_load):
        v = turn(v, 16 * cx + cy)
        if cx:
            a, base = x_at
            if cx > 0:
                v = jnp.where(lane < 16, turn(x_load(a), cy - base), v)
            else:
                v = jnp.where(lane >= 112, turn(x_load(a), 112 - base + cy), v)
        if cy > 0:
            v = jnp.where(slot == 0, turn(y_load(0), -y_slot_of), v)
        elif cy < 0:
            v = jnp.where(slot == 15, turn(y_load(1), 15 - y_slot_of), v)
        return v

    if first:
        def walls(k, carry):
            at = pl.ds(pl.multiple_of(8 * k + 8, 8), 8)
            flag = s_in[at, :]
            for cx in (-1, 0, 1):
                for cy in (-1, 0, 1):
                    wall_ref[(cx + 1) * 3 + cy + 1, at, :] = gather(
                        flag, cx, cy, x_flag_place(cx), lambda a: xs[a, at, :],
                        y_flag_slot(cx), lambda a: ys[a, at, :])
            return carry

        lax.fori_loop(0, TILES, walls, 0)

    def gather_tile(t, buf):
        here = pl.ds(pl.multiple_of(8 * t, 8), 8)
        for i in range(27):
            cx, cy, cz = VELS[i]
            at = here if cz == 0 else pl.ds(8 * t - cz, 8)
            v = star_in[i, at, :]
            if i != 13:
                v = gather(v, cx, cy, x_place(cx, cy, cz), lambda a: xs[a, at, :],
                           y_slot(cx, cz), lambda a: ys[a, at, :])
                wall = wall_ref[(cx + 1) * 3 + cy + 1, at, :]
                v = jnp.where(wall > 0.5, star_in[26 - i, here, :], v)
            buf[i] = v

    def collide_tile(t, buf):
        f = [buf[i] for i in range(27)]
        mom = moments(f)
        if last:
            inv = 1.0 / mom[0]
            macro = mom[0], mom[1] * inv, mom[2] * inv, mom[3] * inv
        else:
            star, macro = collide(f, mom)
            here = pl.ds(pl.multiple_of(8 * t, 8), 8)
            for i in range(27):
                star_out[i, here, :] = star[i]
        row = pl.ds(pl.multiple_of(8 * t - 8, 8), 8)
        for a, v in enumerate(macro):
            mom_out[a, row, :] = v

    if not last:
        xs_next, ys_next = refs[2:4]
        refs = refs[2:]
    even, odd = refs[2:4]

    def pack_at(t):
        if not last:
            pack_tile(t, star_out, None, lane, patterns, xs_next, ys_next)

    def body(m, carry):
        pack_at(jnp.maximum(2 * m, 1))
        collide_tile(2 * m + 1, even)
        gather_tile(2 * m + 2, odd)
        pack_at(2 * m + 1)
        collide_tile(2 * m + 2, odd)
        gather_tile(jnp.minimum(2 * m + 3, TILES), even)
        return carry

    gather_tile(1, even)
    lax.fori_loop(0, TILES // 2, body, 0)
    pack_at(TILES)
    if not last:
        xp_out[...] = xs_next[...].astype(xp_out.dtype)
        yp_out[...] = ys_next[0].astype(yp_out.dtype)
        ym_out[...] = ys_next[1].astype(ym_out.dtype)
        xc_out[...] = corners(ys_next[0], ys_next[1]).astype(xc_out.dtype)


def prepare_kernel(capacity, owner_row, owner_col, cell, placing_out, lane_out, row_out):
    slots = owner_row.shape[1]
    q = lax.broadcasted_iota(jnp.int32, (slots, slots), 0)
    p = lax.broadcasted_iota(jnp.int32, (slots, slots), 1)
    same = (owner_row[...] == owner_col[...]) & (q < p)
    rank = jnp.sum(same.astype(F32), axis=0, keepdims=True).astype(jnp.int32)
    column = owner_row[...] * capacity + rank
    rows = placing_out.shape[0]
    placing_out[...] = (lax.broadcasted_iota(jnp.int32, (rows, slots), 0) == column).astype(F32).astype(jnp.bfloat16)
    k = lax.broadcasted_iota(jnp.int32, (LANES, slots), 0)
    lane_out[...] = (k == cell[...] // 128).astype(F32).astype(jnp.bfloat16)
    row_out[...] = (k == cell[...] % 128).astype(F32)


def split3(v):
    hi = v.astype(jnp.bfloat16)
    left = v - hi.astype(F32)
    mid = left.astype(jnp.bfloat16)
    low = (left - mid.astype(F32)).astype(jnp.bfloat16)
    return hi, mid, low


def sample_kernel(upper, mom, lane_hot, row_hot, area, placing, out):
    fields = []
    hot = row_hot[...]
    lanes = lane_hot[...]
    for a in range(4):
        picked = None
        for part in split3(mom[a, 8 : 8 + 128, :]):
            term = jnp.dot(part, lanes, preferred_element_type=F32)
            picked = term if picked is None else picked + term
        fields.append(jnp.sum(picked * hot, axis=0, keepdims=True))
    rho, u = fields[0], fields[1:]
    pressure = (rho - 1.0) / 3.0
    normal = [area[j : j + 1, :] for j in range(3)]
    flow = u[0] * normal[0] + u[1] * normal[1] + u[2] * normal[2]
    rows = [rho * flow] + [pressure * normal[j] + rho * u[j] * flow for j in range(3)]
    blank = [jnp.zeros_like(rho)] * 4
    stacked = jnp.concatenate(blank + rows if upper else rows + blank, axis=0).astype(jnp.bfloat16)
    out[...] = lax.dot_general(stacked, placing[...], (((1,), (1,)), ((), ())), preferred_element_type=F32)


def scatter_kernel(groups, capacity, *refs):
    parts, out = refs[:-1], refs[-1]
    pairs = [parts[0][...] + parts[1][...], parts[2][...] + parts[3][...]]
    lane = lane_iota()
    for g in range(groups):
        start = g * capacity
        tile = slice(start // LANES * LANES, start // LANES * LANES + LANES)
        low = turn(pairs[0][:, tile], -start)
        high = turn(pairs[1][:, tile], 64 - start)
        out[g] = jnp.where(lane < 64, low, high)


def window_kernel(solid_hbm, mom, unused, density_out, velocity_out, solid, sem):
    copy = pltpu.make_async_copy(solid_hbm, solid, sem.at[0])
    copy.start()
    copy.wait()
    wall = solid[...] != 0
    density_out[...] = jnp.where(wall, 1.0, mom[0, 8:136, :].T)
    for a in range(3):
        velocity_out[a] = jnp.where(wall, 0.0, mom[a + 1, 8:136, :].T)


def observe_kernel(groups, capacity, ptile, rec, weights_hbm, offset, out, weights, sem):
    obs = weights.shape[2]
    part = obs // 2
    copies = {}
    for h in range(2):
        for k in range(4):
            at = (k, slice(None), pl.ds(h * part, part))
            copies[h, k] = pltpu.make_async_copy(weights_hbm.at[at], weights.at[at], sem.at[4 * h + k])
            copies[h, k].start()
    tiles = offset.shape[0]
    rows = groups * capacity
    halves = []
    lane = lane_iota()
    per = LANES // capacity
    for half in range(2):
        pieces = []
        for start in range(0, groups, per):
            acc = jnp.zeros((8, LANES), F32)
            for g in range(start, start + per):
                moved = turn(rec[g], (g - start) * capacity - 64 * half)
                acc = jnp.where(lane // capacity == g - start, moved, acc)
            pieces.append(acc)
        halves.append(jnp.concatenate(pieces, axis=1))
    keep = lax.broadcasted_iota(jnp.int32, (tiles, rows), 1) // ptile == lax.broadcasted_iota(jnp.int32, (tiles, rows), 0)
    lefts = []
    for k in range(4):
        left = [
            jnp.where(keep, jnp.broadcast_to(halves[s // 2][4 * (s % 2) + k : 4 * (s % 2) + k + 1, :], (tiles, rows)), 0.0)
            for s in range(STEPS)
        ]
        lefts.append(jnp.concatenate(left, axis=0).astype(jnp.bfloat16))
    devices = out.shape[0]
    count = obs // devices
    obs_tile = obs // offset.shape[1]
    for h in range(2):
        acc = None
        for k in range(4):
            copies[h, k].wait()
            term = jnp.dot(lefts[k], weights[k, :, h * part : (h + 1) * part], preferred_element_type=F32)
            acc = term if acc is None else acc + term
        for d in range(h * devices // 2, (h + 1) * devices // 2):
            start = d * count
            here = start - h * part
            piece = jnp.zeros((tiles, LANES), F32)
            for s in range(STEPS):
                block = acc[tiles * s : tiles * (s + 1), here // LANES * LANES : here // LANES * LANES + LANES]
                moved = turn(block, s * count - start % LANES)
                piece = jnp.where(lane // count == s, moved, piece)
            out[d, 0:tiles, :] = piece
            o = start // obs_tile
            out[d, tiles : 2 * tiles, :] = jnp.broadcast_to(offset[:, o : o + 1], (tiles, LANES))


def signal_kernel(got, out):
    devices, twice = got.shape[0], got.shape[1]
    tiles = twice // 2
    count = out.shape[0]
    values = got[:, 0:tiles, :].reshape(devices * tiles, LANES)
    start = got[:, tiles:twice, :].reshape(devices * tiles, LANES)
    bins = lax.broadcasted_iota(jnp.int32, (devices * tiles, NB), 1).astype(F32)
    parts = split3(values)
    total = None
    for s in range(STEPS):
        hot = (start + float(s) == bins).astype(F32).astype(jnp.bfloat16)
        acc = None
        for part in parts:
            term = lax.dot_general(part, hot, (((0,), (0,)), ((), ())), preferred_element_type=F32)
            acc = term if acc is None else acc + term
        acc = acc[s * count : (s + 1) * count, :]
        total = acc if total is None else total + acc
    out[...] = total


def call(kernel, outs, *args, scratch=(), flops=1000000, limit=24, far=()):
    args = [pltpu.with_memory_space_constraint(a, pltpu.HBM) if k in far else a for k, a in enumerate(args)]
    return pl.pallas_call(
        kernel,
        out_shape=outs,
        in_specs=[pl.BlockSpec(memory_space=pltpu.HBM if k in far else pltpu.VMEM) for k in range(len(args))],
        out_specs=jax.tree.map(lambda _: pl.BlockSpec(memory_space=pltpu.VMEM), outs),
        scratch_shapes=list(scratch),
        compiler_params=pltpu.CompilerParams(vmem_limit_bytes=limit << 20),
        cost_estimate=pl.CostEstimate(
            flops=flops, transcendentals=0,
            bytes_accessed=sum(a.size * a.dtype.itemsize for a in args)),
    )(*args)


def ring(axis, shift):
    count = lax.axis_size(axis)
    return [(i, (i + shift) % count) for i in range(count)]


def shift(value, axis, by):
    return lax.ppermute(value, axis, ring(axis, by))


def exchange(xp, yp, ym, xc):
    if lax.axis_size("gx") == 2:
        low = high = shift(xc, "gx", 1)
        xh = shift(xp, "gx", 1)
    else:
        low = shift(xc, "gx", 1)
        high = shift(xc, "gx", -1)
        up = shift(jnp.stack([xp[0], xp[2]]), "gx", 1)
        down = shift(jnp.stack([xp[1], xp[2]]), "gx", -1)
        xh = jnp.stack([up[0], down[0], jnp.where(jnp.arange(LANES) < 64, up[1], down[1])])
    face = jax.ShapeDtypeStruct((HALO_ROWS, LANES), HALO_TYPE)
    yp, ym = call(patch_kernel, (face, face), low, high, yp, ym)
    return xh, shift(yp, "gy", 1), shift(ym, "gy", -1)


def shards(perturb, density, velocity, excitation, solid_flag, panel_cell, panel_owner, panel_area, weights, bin_offset):
    bx, by, bz = density.shape
    assert bx * by == LANES and bz == LANES and by == 16
    flat = (LANES, LANES)
    solid = solid_flag.reshape(flat)
    block = jax.ShapeDtypeStruct((27, ROWS, LANES), F32)
    one = jax.ShapeDtypeStruct((ROWS, LANES), F32)
    rim = jax.ShapeDtypeStruct((28 * 4, LANES), F32)
    x_face = jax.ShapeDtypeStruct((3, HALO_ROWS, LANES), HALO_TYPE)
    y_face = jax.ShapeDtypeStruct((HALO_ROWS, LANES), HALO_TYPE)
    x_scratch = pltpu.VMEM((3, HALO_ROWS, LANES), F32)
    y_scratch = pltpu.VMEM((2, HALO_ROWS, LANES), F32)

    f0, low_rim, high_rim, flags = call(
        initial_kernel, (block, rim, rim, one),
        perturb.reshape((27,) + flat), density.reshape(flat), velocity.reshape((3,) + flat),
        excitation.reshape(flat), solid,
        far=range(5),
        scratch=(pltpu.VMEM((27,) + flat, F32), pltpu.VMEM(flat, F32), pltpu.VMEM((3,) + flat, F32), pltpu.VMEM(flat, F32),
                 pltpu.VMEM(flat, jnp.int32), pltpu.SemaphoreType.DMA((9,)), pltpu.SemaphoreType.DMA((4,))))
    below = lax.ppermute(high_rim, "gz", ring("gz", 1))
    above = lax.ppermute(low_rim, "gz", ring("gz", -1))

    group_count = lax.axis_size(("gx", "gy"))
    slots = panel_owner.shape[0]
    row_count = 2 * slots
    capacity = row_count // group_count
    placing, lane_hot, row_hot = call(
        functools.partial(prepare_kernel, capacity),
        (jax.ShapeDtypeStruct((row_count, slots), jnp.bfloat16),
         jax.ShapeDtypeStruct((LANES, slots), jnp.bfloat16),
         jax.ShapeDtypeStruct((LANES, slots), F32)),
        panel_owner.reshape(1, slots), panel_owner.reshape(slots, 1), panel_cell.reshape(1, slots))

    star, walls, xp, yp, ym, xc = call(
        first_kernel, (block, one, x_face, y_face, y_face, y_face), f0, flags, below, above, placing,
        scratch=(pltpu.VMEM((28, 16, LANES), F32), x_scratch, y_scratch))

    mom_shape = jax.ShapeDtypeStruct((4, HALO_ROWS, LANES), F32)
    routed = []
    for s in range(STEPS):
        first, last = s == 0, s == STEPS - 1
        xh, yph, ymh = exchange(xp, yp, ym, xc)
        outs = [mom_shape]
        if not last:
            outs += [block, x_face, y_face, y_face, y_face]
        if first:
            outs += [jax.ShapeDtypeStruct((9, ROWS, LANES), F32)]
        scratch = [pltpu.VMEM((3, ROWS, LANES), F32), pltpu.VMEM((2, ROWS, LANES), F32)]
        if not last:
            scratch += [x_scratch, y_scratch]
        scratch += [pltpu.VMEM((27, 8, LANES), F32)] * 2
        res = call(functools.partial(step_kernel, first, last), tuple(outs), star, walls, xh, yph, ymh,
                   routed[-1] if routed else placing, scratch=scratch)
        mom = res[0]
        if not last:
            star, xp, yp, ym, xc = res[1:6]
        if first:
            walls = res[6]
        routed.append(call(functools.partial(sample_kernel, s % 2), jax.ShapeDtypeStruct((8, row_count), F32),
                           mom, lane_hot, row_hot, panel_area, placing))

    sent = call(functools.partial(scatter_kernel, group_count, capacity),
                jax.ShapeDtypeStruct((group_count, 8, LANES), F32), *routed)
    received = lax.all_to_all(sent, ("gx", "gy"), split_axis=0, concat_axis=0, tiled=True)

    final_density, final_velocity = call(
        window_kernel,
        (jax.ShapeDtypeStruct(flat, F32), jax.ShapeDtypeStruct((3,) + flat, F32)),
        solid, mom, sent, far=(0,), scratch=(pltpu.VMEM(flat, jnp.int32), pltpu.SemaphoreType.DMA((1,))))

    tiles, obs_tiles = bin_offset.shape
    devices = lax.axis_size(("gx", "gy", "gz"))
    obs = weights.shape[2]
    count = obs // devices
    assert obs // obs_tiles % count == 0 and tiles % 8 == 0 and STEPS * count <= LANES and capacity <= 64
    observed = call(
        functools.partial(observe_kernel, group_count, capacity, row_count // tiles),
        jax.ShapeDtypeStruct((devices, 2 * tiles, LANES), F32),
        received, weights, bin_offset.astype(F32), far=(1,),
        scratch=(pltpu.VMEM(weights.shape, weights.dtype), pltpu.SemaphoreType.DMA((8,))))
    got = lax.all_to_all(observed, ("gx", "gy", "gz"), split_axis=0, concat_axis=0, tiled=True)
    signal = call(signal_kernel, jax.ShapeDtypeStruct((count, NB), F32), got)
    return final_density.reshape(density.shape), final_velocity.reshape(velocity.shape), signal


def solution(mesh):
    cells = P("gx", "gy", "gz")
    vectors = P(None, "gx", "gy", "gz")
    every = ("gx", "gy", "gz")
    placed = (vectors, cells, vectors, cells, cells, P(every), P(every), P(None, every), P(None, every, None), P(every, None))
    return jax.shard_map(
        shards, mesh=mesh, in_specs=placed, out_specs=(cells, vectors, P(every, None)), check_vma=False)
```

profile of v0, /device:TPU:0, one launch (start us, length us, event | category | flops | bytes accessed | tf_op | source)
XLA Modules:
  0.0 100.9 jit_solution(12442514813959180826)
XLA Ops:
  0.7 3.1 %shard_map.121 = (f32[27,160,128]{2,1,0:T(8,128)S(1)}, f32[112,128]{1,0:T(8,128)S(1)}, f32[112,128]{1,0:T(8,128)S(1)}, f32[160,128]{1,0:T(8,128)S(1)}) custom-call(f32[27,128,128]{2,1,0:T(8,128)} %bitcast.13, f32[128,128]{1,0:T(8,128)} %bitcast.17, f32[3,128,128]{2,1,0:T(8,128)} %bitcast.16, f32[128,128]{1,0:T(8,128)} %bitcast.18, s32[128,128]{1,0:T(8,128)} %bitcast.14), custom_call_target="tpu_custom_call" | custom-call | flops 1000000 | bytes 2162688 | tf_op jit(solution)/shard_map/pallas_call | solution.py:586
  3.7 0.5 collective-permute-start
  4.3 2.0 %collective-permute-start.1 = (f32[112,128]{1,0:T(8,128)S(1)}, f32[112,128]{1,0:T(8,128)S(1)}, u32[]{:S(2)}, u32[]{:S(2)}) collective-permute-start(f32[112,128]{1,0:T(8,128)S(1)} %get-tuple-element.48), channel_id=1, source_target_pairs={{0,3},{1,0},{2,1},{3,2},{4,7},{5,4},{6,5},{7,6},{8,11},{9,8},{10,9... | collective-permute-start | bytes 172040 | tf_op jit(solution)/shard_map/ppermute | solution.py:644
  6.3 0.8 copy.13.owner_col
  7.1 0.2 shard_map.122
  7.3 0.7 collective-permute-done.lo
  8.1 0.4 collective-permute-done.1.hi
  8.5 2.5 %shard_map.123 = (f32[27,160,128]{2,1,0:T(8,128)S(1)}, f32[160,128]{1,0:T(8,128)S(1)}, bf16[3,144,128]{2,1,0:T(8,128)(2,1)S(1)}, bf16[144,128]{1,0:T(8,128)(2,1)...) custom-call(f32[27,160,128]{2,1,0:T(8,128)S(1)} %get-tuple-element.45.f_in, ...), custom_call_target="tpu_custom_call" | custom-call | flops 1000000 | bytes 2670592 | tf_op jit(solution)/shard_map/pallas_call | solution.py:586
  11.0 1.9 %collective-permute-start.2 = (bf16[3,144,128]{2,1,0:T(8,128)(2,1)S(1)}, bf16[3,144,128]{2,1,0:T(8,128)(2,1)S(1)}, u32[]{:S(2)}, u32[]{:S(2)}) collective-permute-start(bf16[3,144,128]{2,1,0:T(8,128)(2,1)S(1)} %get-tuple-element.52), channel_id=1, source_target_pairs={{0,16},{16,0},{1,17},{17,1},{2,18},{18,2},{3,19},{19,3},{4,20},{20... | collective-permute-start | bytes 331784 | tf_op jit(solution)/shard_map/ppermute | solution.py:605
  13.1 4.2 %collective-permute-done.3.low.high = bf16[144,128]{1,0:T(8,128)(2,1)S(1)} collective-permute-done((bf16[144,128]{1,0:T(8,128)(2,1)S(1)}, bf16[144,128]{1,0:T(8,128)(2,1)S(1)}, u32[]{:S(2)}, u32[]{:S(2)}) %collective-permute-start.3) | collective-permute-done | bytes 36896 | tf_op jit(solution)/shard_map/ppermute | solution.py:605
  17.4 1.8 %collective-permute-start.4 = (bf16[144,128]{1,0:T(8,128)(2,1)S(1)}, bf16[144,128]{1,0:T(8,128)(2,1)S(1)}, u32[]{:S(2)}, u32[]{:S(2)}) collective-permute-start(bf16[144,128]{1,0:T(8,128)(2,1)S(1)} %get-tuple-element.56), channel_id=1, source_target_pairs={{0,4},{4,8},{8,12},{12,0},{1,5},{5,9},{9,13},{13,1},{2,6},{6,10},{... | collective-permute-start | bytes 110600 | tf_op jit(solution)/shard_map/ppermute | solution.py:605
  19.2 2.1 %collective-permute-start.5 = (bf16[144,128]{1,0:T(8,128)(2,1)S(1)}, bf16[144,128]{1,0:T(8,128)(2,1)S(1)}, u32[]{:S(2)}, u32[]{:S(2)}) collective-permute-start(bf16[144,128]{1,0:T(8,128)(2,1)S(1)} %get-tuple-element.57), channel_id=1, source_target_pairs={{0,12},{4,0},{8,4},{12,8},{1,13},{5,1},{9,5},{13,9},{2,14},{6,2},{... | collective-permute-start | bytes 110600 | tf_op jit(solution)/shard_map/ppermute | solution.py:605
  21.3 2.1 %collective-permute-done.4.refs_3_ = bf16[144,128]{1,0:T(8,128)(2,1)S(1)} collective-permute-done((bf16[144,128]{1,0:T(8,128)(2,1)S(1)}, bf16[144,128]{1,0:T(8,128)(2,1)S(1)}, u32[]{:S(2)}, u32[]{:S(2)}) %collective-permute-start.4) | collective-permute-done | bytes 36896 | tf_op jit(solution)/shard_map/ppermute | solution.py:605
  23.4 0.3 collective-permute-done.5.refs_4_
  23.8 4.6 %shard_map.125 = (f32[4,144,128]{2,1,0:T(8,128)S(1)}, f32[27,160,128]{2,1,0:T(8,128)S(1)}, bf16[3,144,128]{2,1,0:T(8,128)(2,1)S(1)}, bf16[144,128]{1,0:T(8,128)(...) custom-call(f32[27,160,128]{2,1,0:T(8,128)S(1)} %get-tuple-element.50.refs_0_, ...), custom_call_target="tpu_custom_call" | custom-call | flops 1000000 | bytes 2740224 | tf_op jit(solution)/shard_map/pallas_call | solution.py:586
  28.4 1.5 %collective-permute-start.6 = (bf16[3,144,128]{2,1,0:T(8,128)(2,1)S(1)}, bf16[3,144,128]{2,1,0:T(8,128)(2,1)S(1)}, u32[]{:S(2)}, u32[]{:S(2)}) collective-permute-start(bf16[3,144,128]{2,1,0:T(8,128)(2,1)S(1)} %get-tuple-element.60), channel_id=1, source_target_pairs={{0,16},{16,0},{1,17},{17,1},{2,18},{18,2},{3,19},{19,3},{4,20},{20... | collective-permute-start | bytes 331784 | tf_op jit(solution)/shard_map/ppermute | solution.py:605
  29.9 0.5 collective-permute-start.7
  30.4 3.4 %collective-permute-done.7.low.high = bf16[144,128]{1,0:T(8,128)(2,1)S(1)} collective-permute-done((bf16[144,128]{1,0:T(8,128)(2,1)S(1)}, bf16[144,128]{1,0:T(8,128)(2,1)S(1)}, u32[]{:S(2)}, u32[]{:S(2)}) %collective-permute-start.7) | collective-permute-done | bytes 36896 | tf_op jit(solution)/shard_map/ppermute | solution.py:605
  34.0 1.0 %collective-permute-start.8 = (bf16[144,128]{1,0:T(8,128)(2,1)S(1)}, bf16[144,128]{1,0:T(8,128)(2,1)S(1)}, u32[]{:S(2)}, u32[]{:S(2)}) collective-permute-start(bf16[144,128]{1,0:T(8,128)(2,1)S(1)} %get-tuple-element.64), channel_id=1, source_target_pairs={{0,4},{4,8},{8,12},{12,0},{1,5},{5,9},{9,13},{13,1},{2,6},{6,10},{... | collective-permute-start | bytes 110600 | tf_op jit(solution)/shard_map/ppermute | solution.py:605
  35.0 2.8 %collective-permute-start.9 = (bf16[144,128]{1,0:T(8,128)(2,1)S(1)}, bf16[144,128]{1,0:T(8,128)(2,1)S(1)}, u32[]{:S(2)}, u32[]{:S(2)}) collective-permute-start(bf16[144,128]{1,0:T(8,128)(2,1)S(1)} %get-tuple-element.65), channel_id=1, source_target_pairs={{0,12},{4,0},{8,4},{12,8},{1,13},{5,1},{9,5},{13,9},{2,14},{6,2},{... | collective-permute-start | bytes 110600 | tf_op jit(solution)/shard_map/ppermute | solution.py:605
  37.8 0.5 shard_map.127.refs_5_.refs_0_
  38.3 1.5 %collective-permute-done.8.refs_3_ = bf16[144,128]{1,0:T(8,128)(2,1)S(1)} collective-permute-done((bf16[144,128]{1,0:T(8,128)(2,1)S(1)}, bf16[144,128]{1,0:T(8,128)(2,1)S(1)}, u32[]{:S(2)}, u32[]{:S(2)}) %collective-permute-start.8) | collective-permute-done | bytes 36896 | tf_op jit(solution)/shard_map/ppermute | solution.py:605
  39.8 3.0 %shard_map.128 = (f32[4,144,128]{2,1,0:T(8,128)S(1)}, f32[27,160,128]{2,1,0:T(8,128)S(1)}, bf16[3,144,128]{2,1,0:T(8,128)(2,1)S(1)}, bf16[144,128]{1,0:T(8,128)(...) custom-call(f32[27,160,128]{2,1,0:T(8,128)S(1)} %get-tuple-element.58.refs_0_, ...), custom_call_target="tpu_custom_call" | custom-call | flops 1000000 | bytes 3149824 | tf_op jit(solution)/shard_map/pallas_call | solution.py:586
  42.8 1.2 %collective-permute-start.10 = (bf16[3,144,128]{2,1,0:T(8,128)(2,1)S(1)}, bf16[3,144,128]{2,1,0:T(8,128)(2,1)S(1)}, u32[]{:S(2)}, u32[]{:S(2)}) collective-permute-start(bf16[3,144,128]{2,1,0:T(8,128)(2,1)S(1)} %get-tuple-element.70), channel_id=1, source_target_pairs={{0,16},{16,0},{1,17},{17,1},{2,18},{18,2},{3,19},{19,3},{4,20},{20... | collective-permute-start | bytes 331784 | tf_op jit(solution)/shard_map/ppermute | solution.py:605
  44.1 0.8 collective-permute-start.11
  44.9 3.1 %collective-permute-done.11.low.high = bf16[144,128]{1,0:T(8,128)(2,1)S(1)} collective-permute-done((bf16[144,128]{1,0:T(8,128)(2,1)S(1)}, bf16[144,128]{1,0:T(8,128)(2,1)S(1)}, u32[]{:S(2)}, u32[]{:S(2)}) %collective-permute-start.11) | collective-permute-done | bytes 36896 | tf_op jit(solution)/shard_map/ppermute | solution.py:605
  48.1 1.0 collective-permute-start.12
  49.1 2.9 %collective-permute-start.13 = (bf16[144,128]{1,0:T(8,128)(2,1)S(1)}, bf16[144,128]{1,0:T(8,128)(2,1)S(1)}, u32[]{:S(2)}, u32[]{:S(2)}) collective-permute-start(bf16[144,128]{1,0:T(8,128)(2,1)S(1)} %get-tuple-element.75), channel_id=1, source_target_pairs={{0,12},{4,0},{8,4},{12,8},{1,13},{5,1},{9,5},{13,9},{2,14},{6,2},{... | collective-permute-start | bytes 110600 | tf_op jit(solution)/shard_map/ppermute | solution.py:605
  52.0 0.5 shard_map.130.refs_5_.refs_1_
  52.5 1.4 %collective-permute-done.12.refs_3_ = bf16[144,128]{1,0:T(8,128)(2,1)S(1)} collective-permute-done((bf16[144,128]{1,0:T(8,128)(2,1)S(1)}, bf16[144,128]{1,0:T(8,128)(2,1)S(1)}, u32[]{:S(2)}, u32[]{:S(2)}) %collective-permute-start.12) | collective-permute-done | bytes 36896 | tf_op jit(solution)/shard_map/ppermute | solution.py:605
  53.9 3.0 %shard_map.131 = (f32[4,144,128]{2,1,0:T(8,128)S(1)}, f32[27,160,128]{2,1,0:T(8,128)S(1)}, bf16[3,144,128]{2,1,0:T(8,128)(2,1)S(1)}, bf16[144,128]{1,0:T(8,128)(...) custom-call(f32[27,160,128]{2,1,0:T(8,128)S(1)} %get-tuple-element.69.refs_0_, ...), custom_call_target="tpu_custom_call" | custom-call | flops 1000000 | bytes 3149824 | tf_op jit(solution)/shard_map/pallas_call | solution.py:586
  57.0 1.2 %collective-permute-start.14 = (bf16[3,144,128]{2,1,0:T(8,128)(2,1)S(1)}, bf16[3,144,128]{2,1,0:T(8,128)(2,1)S(1)}, u32[]{:S(2)}, u32[]{:S(2)}) collective-permute-start(bf16[3,144,128]{2,1,0:T(8,128)(2,1)S(1)} %get-tuple-element.78), channel_id=1, source_target_pairs={{0,16},{16,0},{1,17},{17,1},{2,18},{18,2},{3,19},{19,3},{4,20},{20... | collective-permute-start | bytes 331784 | tf_op jit(solution)/shard_map/ppermute | solution.py:605
  58.2 0.8 collective-permute-start.15
  59.0 3.1 %collective-permute-done.15.low.high = bf16[144,128]{1,0:T(8,128)(2,1)S(1)} collective-permute-done((bf16[144,128]{1,0:T(8,128)(2,1)S(1)}, bf16[144,128]{1,0:T(8,128)(2,1)S(1)}, u32[]{:S(2)}, u32[]{:S(2)}) %collective-permute-start.15) | collective-permute-done | bytes 36896 | tf_op jit(solution)/shard_map/ppermute | solution.py:605
  62.2 1.2 %collective-permute-start.16 = (bf16[144,128]{1,0:T(8,128)(2,1)S(1)}, bf16[144,128]{1,0:T(8,128)(2,1)S(1)}, u32[]{:S(2)}, u32[]{:S(2)}) collective-permute-start(bf16[144,128]{1,0:T(8,128)(2,1)S(1)} %get-tuple-element.82), channel_id=1, source_target_pairs={{0,4},{4,8},{8,12},{12,0},{1,5},{5,9},{9,13},{13,1},{2,6},{6,10},{... | collective-permute-start | bytes 110600 | tf_op jit(solution)/shard_map/ppermute | solution.py:605
  63.4 2.8 %collective-permute-start.17 = (bf16[144,128]{1,0:T(8,128)(2,1)S(1)}, bf16[144,128]{1,0:T(8,128)(2,1)S(1)}, u32[]{:S(2)}, u32[]{:S(2)}) collective-permute-start(bf16[144,128]{1,0:T(8,128)(2,1)S(1)} %get-tuple-element.83), channel_id=1, source_target_pairs={{0,12},{4,0},{8,4},{12,8},{1,13},{5,1},{9,5},{13,9},{2,14},{6,2},{... | collective-permute-start | bytes 110600 | tf_op jit(solution)/shard_map/ppermute | solution.py:605
  66.2 0.5 shard_map.133.refs_5_.refs_2_
  66.7 1.4 %collective-permute-done.16.refs_3_ = bf16[144,128]{1,0:T(8,128)(2,1)S(1)} collective-permute-done((bf16[144,128]{1,0:T(8,128)(2,1)S(1)}, bf16[144,128]{1,0:T(8,128)(2,1)S(1)}, u32[]{:S(2)}, u32[]{:S(2)}) %collective-permute-start.16) | collective-permute-done | bytes 36896 | tf_op jit(solution)/shard_map/ppermute | solution.py:605
  68.1 2.0 %shard_map.134.mom = f32[4,144,128]{2,1,0:T(8,128)S(1)} custom-call(f32[27,160,128]{2,1,0:T(8,128)S(1)} %get-tuple-element.77.refs_0_, f32[9,160,128]{2,1,0:T(8,128)S(1)} %get-tuple-element.59.refs_1_, bf16[3,144,128]{2,1,0:T(8,128)(2,1)S(1)} %collective-permute-done.14.refs_2_, bf16[144,128]{1,0:T(8,128)(2,1)S(1)} %collective-permute-done.16.refs_3_, ...), custom_call_target="tpu_custom_call" | custom-call | flops 1000000 | bytes 3149824 | tf_op jit(solution)/shard_map/pallas_call | solution.py:586
  70.1 0.5 shard_map.135.refs_3_
  70.6 0.7 shard_map.136.unused
  71.3 5.8 %all-to-all-start = ((f32[8,8,128]{2,1,0:T(8,128)}), f32[8,8,128]{2,1,0:T(8,128)S(1)}, u32[]{:S(2)}, u32[]{:S(2)}) async-start(f32[8,8,128]{2,1,0:T(8,128)} %shard_map.136.unused), calls=%async_computation | async-start | bytes 65536 | tf_op jit(solution)/shard_map/all_to_all | solution.py:687
  77.1 6.7 %all-to-all-done.rec = f32[8,8,128]{2,1,0:T(8,128)S(1)} async-done(((f32[8,8,128]{2,1,0:T(8,128)}), f32[8,8,128]{2,1,0:T(8,128)S(1)}, u32[]{:S(2)}, u32[]{:S(2)}) %all-to-all-start) | async-done | bytes 32800 | tf_op jit(solution)/shard_map/all_to_all | solution.py:687
  83.8 3.2 %shard_map.138 = f32[32,16,128]{2,1,0:T(8,128)} custom-call(f32[8,8,128]{2,1,0:T(8,128)S(1)} %all-to-all-done.rec, bf16[4,512,1024]{2,1,0:T(8,128)(2,1)} %weights_hbm.1, f32[8,8]{1,0:T(8,128)S(1)} %convert_element_type.3.offset), custom_call_target="tpu_custom_call" | custom-call | flops 1000000 | bytes 4227328 | tf_op jit(solution)/shard_map/pallas_call | solution.py:586
  87.0 2.6 %all-to-all-start.1 = ((f32[32,16,128]{2,1,0:T(8,128)}), f32[32,16,128]{2,1,0:T(8,128)S(1)}, u32[]{:S(2)}, u32[]{:S(2)}) async-start(f32[32,16,128]{2,1,0:T(8,128)} %shard_map.138), calls=%async_computation.1 | async-start | bytes 524288 | tf_op jit(solution)/shard_map/all_to_all | solution.py:704
  89.7 2.4 %shard_map.137 = (f32[128,128]{1,0:T(8,128)}, f32[3,128,128]{2,1,0:T(8,128)}) custom-call(s32[128,128]{1,0:T(8,128)} %bitcast.15, f32[4,144,128]{2,1,0:T(8,128)S(1)} %shard_map.134.mom, f32[8,8,128]{2,1,0:T(8,128)} %shard_map.136.unused), custom_call_target="tpu_custom_call" | custom-call | flops 1000000 | bytes 393216 | tf_op jit(solution)/shard_map/pallas_call | solution.py:586
  92.1 7.8 %all-to-all-done.1.got = f32[32,16,128]{2,1,0:T(8,128)S(1)} async-done(((f32[32,16,128]{2,1,0:T(8,128)}), f32[32,16,128]{2,1,0:T(8,128)S(1)}, u32[]{:S(2)}, u32[]{:S(2)}) %all-to-all-start.1) | async-done | bytes 262176 | tf_op jit(solution)/shard_map/all_to_all | solution.py:704
  99.9 1.0 %shard_map.139 = f32[32,128]{1,0:T(8,128)} custom-call(f32[32,16,128]{2,1,0:T(8,128)S(1)} %all-to-all-done.1.got), custom_call_target="tpu_custom_call" | custom-call | flops 1000000 | bytes 262144 | tf_op jit(solution)/shard_map/pallas_call | solution.py:586
  (21 shorter events, 0.6 us)
Async XLA Ops:
  0.6 6.4 %copy-start.1 = (s32[256]{0:T(256)S(1)}, s32[256]{0:T(256)}, u32[]{:S(2)}) copy-start(s32[256]{0:T(256)} %param.16) | copy-start | bytes 3076
  0.6 6.4 %copy-start.2 = (s32[256]{0:T(256)S(1)}, s32[256]{0:T(256)}, u32[]{:S(2)}) copy-start(s32[256]{0:T(256)} %param.15) | copy-start | bytes 3076
  3.7 4.3 %collective-permute-start = (f32[112,128]{1,0:T(8,128)S(1)}, f32[112,128]{1,0:T(8,128)S(1)}, u32[]{:S(2)}, u32[]{:S(2)}) collective-permute-start(f32[112,128]{1,0:T(8,128)S(1)} %get-tuple-element.47), channel_id=1, source_target_pairs={{0,1},{1,2},{2,3},{3,0},{4,5},{5,6},{6,7},{7,4},{8,9},{9,10},{10,1... | collective-permute-start | bytes 172040 | tf_op jit(solution)/shard_map/ppermute | solution.py:643
  4.3 4.2 %collective-permute-start.1 = (f32[112,128]{1,0:T(8,128)S(1)}, f32[112,128]{1,0:T(8,128)S(1)}, u32[]{:S(2)}, u32[]{:S(2)}) collective-permute-start(f32[112,128]{1,0:T(8,128)S(1)} %get-tuple-element.48), channel_id=1, source_target_pairs={{0,3},{1,0},{2,1},{3,2},{4,7},{5,4},{6,5},{7,6},{8,11},{9,8},{10,9... | collective-permute-start | bytes 172040 | tf_op jit(solution)/shard_map/ppermute | solution.py:644
  8.5 29.3 %copy-start = (f32[3,256]{1,0:T(4,128)S(1)}, f32[3,256]{1,0:T(4,128)}, u32[]{:S(2)}) copy-start(f32[3,256]{1,0:T(4,128)} %area.7) | copy-start | bytes 9220
  11.0 12.7 %collective-permute-start.2 = (bf16[3,144,128]{2,1,0:T(8,128)(2,1)S(1)}, bf16[3,144,128]{2,1,0:T(8,128)(2,1)S(1)}, u32[]{:S(2)}, u32[]{:S(2)}) collective-permute-start(bf16[3,144,128]{2,1,0:T(8,128)(2,1)S(1)} %get-tuple-element.52), channel_id=1, source_target_pairs={{0,16},{16,0},{1,17},{17,1},{2,18},{18,2},{3,19},{19,3},{4,20},{20... | collective-permute-start | bytes 331784 | tf_op jit(solution)/shard_map/ppermute | solution.py:605
  12.9 4.4 %collective-permute-start.3 = (bf16[144,128]{1,0:T(8,128)(2,1)S(1)}, bf16[144,128]{1,0:T(8,128)(2,1)S(1)}, u32[]{:S(2)}, u32[]{:S(2)}) collective-permute-start(bf16[144,128]{1,0:T(8,128)(2,1)S(1)} %get-tuple-element.53), channel_id=1, source_target_pairs={{0,16},{16,0},{1,17},{17,1},{2,18},{18,2},{3,19},{19,3},{4,20},{20... | collective-permute-start | bytes 110600 | tf_op jit(solution)/shard_map/ppermute | solution.py:605
  17.4 6.1 %collective-permute-start.4 = (bf16[144,128]{1,0:T(8,128)(2,1)S(1)}, bf16[144,128]{1,0:T(8,128)(2,1)S(1)}, u32[]{:S(2)}, u32[]{:S(2)}) collective-permute-start(bf16[144,128]{1,0:T(8,128)(2,1)S(1)} %get-tuple-element.56), channel_id=1, source_target_pairs={{0,4},{4,8},{8,12},{12,0},{1,5},{5,9},{9,13},{13,1},{2,6},{6,10},{... | collective-permute-start | bytes 110600 | tf_op jit(solution)/shard_map/ppermute | solution.py:605
  19.2 4.5 %collective-permute-start.5 = (bf16[144,128]{1,0:T(8,128)(2,1)S(1)}, bf16[144,128]{1,0:T(8,128)(2,1)S(1)}, u32[]{:S(2)}, u32[]{:S(2)}) collective-permute-start(bf16[144,128]{1,0:T(8,128)(2,1)S(1)} %get-tuple-element.57), channel_id=1, source_target_pairs={{0,12},{4,0},{8,4},{12,8},{1,13},{5,1},{9,5},{13,9},{2,14},{6,2},{... | collective-permute-start | bytes 110600 | tf_op jit(solution)/shard_map/ppermute | solution.py:605
  28.4 11.4 %collective-permute-start.6 = (bf16[3,144,128]{2,1,0:T(8,128)(2,1)S(1)}, bf16[3,144,128]{2,1,0:T(8,128)(2,1)S(1)}, u32[]{:S(2)}, u32[]{:S(2)}) collective-permute-start(bf16[3,144,128]{2,1,0:T(8,128)(2,1)S(1)} %get-tuple-element.60), channel_id=1, source_target_pairs={{0,16},{16,0},{1,17},{17,1},{2,18},{18,2},{3,19},{19,3},{4,20},{20... | collective-permute-start | bytes 331784 | tf_op jit(solution)/shard_map/ppermute | solution.py:605
  29.9 4.0 %collective-permute-start.7 = (bf16[144,128]{1,0:T(8,128)(2,1)S(1)}, bf16[144,128]{1,0:T(8,128)(2,1)S(1)}, u32[]{:S(2)}, u32[]{:S(2)}) collective-permute-start(bf16[144,128]{1,0:T(8,128)(2,1)S(1)} %get-tuple-element.61), channel_id=1, source_target_pairs={{0,16},{16,0},{1,17},{17,1},{2,18},{18,2},{3,19},{19,3},{4,20},{20... | collective-permute-start | bytes 110600 | tf_op jit(solution)/shard_map/ppermute | solution.py:605
  34.0 5.8 %collective-permute-start.8 = (bf16[144,128]{1,0:T(8,128)(2,1)S(1)}, bf16[144,128]{1,0:T(8,128)(2,1)S(1)}, u32[]{:S(2)}, u32[]{:S(2)}) collective-permute-start(bf16[144,128]{1,0:T(8,128)(2,1)S(1)} %get-tuple-element.64), channel_id=1, source_target_pairs={{0,4},{4,8},{8,12},{12,0},{1,5},{5,9},{9,13},{13,1},{2,6},{6,10},{... | collective-permute-start | bytes 110600 | tf_op jit(solution)/shard_map/ppermute | solution.py:605
  35.0 4.8 %collective-permute-start.9 = (bf16[144,128]{1,0:T(8,128)(2,1)S(1)}, bf16[144,128]{1,0:T(8,128)(2,1)S(1)}, u32[]{:S(2)}, u32[]{:S(2)}) collective-permute-start(bf16[144,128]{1,0:T(8,128)(2,1)S(1)} %get-tuple-element.65), channel_id=1, source_target_pairs={{0,12},{4,0},{8,4},{12,8},{1,13},{5,1},{9,5},{13,9},{2,14},{6,2},{... | collective-permute-start | bytes 110600 | tf_op jit(solution)/shard_map/ppermute | solution.py:605
  42.8 11.1 %collective-permute-start.10 = (bf16[3,144,128]{2,1,0:T(8,128)(2,1)S(1)}, bf16[3,144,128]{2,1,0:T(8,128)(2,1)S(1)}, u32[]{:S(2)}, u32[]{:S(2)}) collective-permute-start(bf16[3,144,128]{2,1,0:T(8,128)(2,1)S(1)} %get-tuple-element.70), channel_id=1, source_target_pairs={{0,16},{16,0},{1,17},{17,1},{2,18},{18,2},{3,19},{19,3},{4,20},{20... | collective-permute-start | bytes 331784 | tf_op jit(solution)/shard_map/ppermute | solution.py:605
  44.1 4.0 %collective-permute-start.11 = (bf16[144,128]{1,0:T(8,128)(2,1)S(1)}, bf16[144,128]{1,0:T(8,128)(2,1)S(1)}, u32[]{:S(2)}, u32[]{:S(2)}) collective-permute-start(bf16[144,128]{1,0:T(8,128)(2,1)S(1)} %get-tuple-element.71), channel_id=1, source_target_pairs={{0,16},{16,0},{1,17},{17,1},{2,18},{18,2},{3,19},{19,3},{4,20},{20... | collective-permute-start | bytes 110600 | tf_op jit(solution)/shard_map/ppermute | solution.py:605
  48.1 5.8 %collective-permute-start.12 = (bf16[144,128]{1,0:T(8,128)(2,1)S(1)}, bf16[144,128]{1,0:T(8,128)(2,1)S(1)}, u32[]{:S(2)}, u32[]{:S(2)}) collective-permute-start(bf16[144,128]{1,0:T(8,128)(2,1)S(1)} %get-tuple-element.74), channel_id=1, source_target_pairs={{0,4},{4,8},{8,12},{12,0},{1,5},{5,9},{9,13},{13,1},{2,6},{6,10},{... | collective-permute-start | bytes 110600 | tf_op jit(solution)/shard_map/ppermute | solution.py:605
  49.1 4.8 %collective-permute-start.13 = (bf16[144,128]{1,0:T(8,128)(2,1)S(1)}, bf16[144,128]{1,0:T(8,128)(2,1)S(1)}, u32[]{:S(2)}, u32[]{:S(2)}) collective-permute-start(bf16[144,128]{1,0:T(8,128)(2,1)S(1)} %get-tuple-element.75), channel_id=1, source_target_pairs={{0,12},{4,0},{8,4},{12,8},{1,13},{5,1},{9,5},{13,9},{2,14},{6,2},{... | collective-permute-start | bytes 110600 | tf_op jit(solution)/shard_map/ppermute | solution.py:605
  57.0 11.1 %collective-permute-start.14 = (bf16[3,144,128]{2,1,0:T(8,128)(2,1)S(1)}, bf16[3,144,128]{2,1,0:T(8,128)(2,1)S(1)}, u32[]{:S(2)}, u32[]{:S(2)}) collective-permute-start(bf16[3,144,128]{2,1,0:T(8,128)(2,1)S(1)} %get-tuple-element.78), channel_id=1, source_target_pairs={{0,16},{16,0},{1,17},{17,1},{2,18},{18,2},{3,19},{19,3},{4,20},{20... | collective-permute-start | bytes 331784 | tf_op jit(solution)/shard_map/ppermute | solution.py:605
  58.2 4.0 %collective-permute-start.15 = (bf16[144,128]{1,0:T(8,128)(2,1)S(1)}, bf16[144,128]{1,0:T(8,128)(2,1)S(1)}, u32[]{:S(2)}, u32[]{:S(2)}) collective-permute-start(bf16[144,128]{1,0:T(8,128)(2,1)S(1)} %get-tuple-element.79), channel_id=1, source_target_pairs={{0,16},{16,0},{1,17},{17,1},{2,18},{18,2},{3,19},{19,3},{4,20},{20... | collective-permute-start | bytes 110600 | tf_op jit(solution)/shard_map/ppermute | solution.py:605
  62.2 5.9 %collective-permute-start.16 = (bf16[144,128]{1,0:T(8,128)(2,1)S(1)}, bf16[144,128]{1,0:T(8,128)(2,1)S(1)}, u32[]{:S(2)}, u32[]{:S(2)}) collective-permute-start(bf16[144,128]{1,0:T(8,128)(2,1)S(1)} %get-tuple-element.82), channel_id=1, source_target_pairs={{0,4},{4,8},{8,12},{12,0},{1,5},{5,9},{9,13},{13,1},{2,6},{6,10},{... | collective-permute-start | bytes 110600 | tf_op jit(solution)/shard_map/ppermute | solution.py:605
  63.4 4.7 %collective-permute-start.17 = (bf16[144,128]{1,0:T(8,128)(2,1)S(1)}, bf16[144,128]{1,0:T(8,128)(2,1)S(1)}, u32[]{:S(2)}, u32[]{:S(2)}) collective-permute-start(bf16[144,128]{1,0:T(8,128)(2,1)S(1)} %get-tuple-element.83), channel_id=1, source_target_pairs={{0,12},{4,0},{8,4},{12,8},{1,13},{5,1},{9,5},{13,9},{2,14},{6,2},{... | collective-permute-start | bytes 110600 | tf_op jit(solution)/shard_map/ppermute | solution.py:605
  66.7 10.4 %copy-start.3 = (s32[8,8]{1,0:T(8,128)S(1)}, s32[8,8]{1,0:T(8,128)}, u32[]{:S(2)}) copy-start(s32[8,8]{1,0:T(8,128)} %param.19) | copy-start | bytes 772
  71.3 12.5 %all-to-all-start = ((f32[8,8,128]{2,1,0:T(8,128)}), f32[8,8,128]{2,1,0:T(8,128)S(1)}, u32[]{:S(2)}, u32[]{:S(2)}) async-start(f32[8,8,128]{2,1,0:T(8,128)} %shard_map.136.unused), calls=%async_computation | async-start | bytes 65536 | tf_op jit(solution)/shard_map/all_to_all | solution.py:687
  87.0 12.9 %all-to-all-start.1 = ((f32[32,16,128]{2,1,0:T(8,128)}), f32[32,16,128]{2,1,0:T(8,128)S(1)}, u32[]{:S(2)}, u32[]{:S(2)}) async-start(f32[32,16,128]{2,1,0:T(8,128)} %shard_map.138), calls=%async_computation.1 | async-start | bytes 524288 | tf_op jit(solution)/shard_map/all_to_all | solution.py:704
where the time goes:
time: 101 us
  waiting for transfers between devices  36.3 us (36%)
  starting transfers between devices  34.9 us (35%)
  Pallas kernels  28.1 us (28%)
    pallas_call x19, Pallas kernels, call(): pl.pallas_call(kernel, out_shape=outs, in_specs=[pl.BlockSpec(memory_spac...  28.1 us
    ppermute x16, starting transfers between devices, shift(): return lax.ppermute(value, axis, ring(axis, by))  24 us
    ppermute x16, waiting for transfers between devices, shift(): return lax.ppermute(value, axis, ring(axis, by))  20.6 us
    all_to_all x1, waiting for transfers between devices, shards(): lax.all_to_all(observed, ('gx', 'gy', 'gz'), split_axis=0, concat_axis=0,...  7.83 us
    all_to_all x1, waiting for transfers between devices, shards(): lax.all_to_all(sent, ('gx', 'gy'), split_axis=0, concat_axis=0, tiled=True)  6.71 us
    all_to_all x1, starting transfers between devices, shards(): lax.all_to_all(sent, ('gx', 'gy'), split_axis=0, concat_axis=0, tiled=True)  5.78 us
    all_to_all x1, starting transfers between devices, shards(): lax.all_to_all(observed, ('gx', 'gy', 'gz'), split_axis=0, concat_axis=0,...  2.6 us
  transfers between devices with their start and end apart: 20, of which 13 were waited for; matrix products, arithmetic and copies ran while one was open for 1% of the time, Pallas kernels for 4%

commit v1 on v0

--- a/solution.py
+++ b/solution.py
@@ -18,6 +18,7 @@
 HALO_ROWS = 8 * TILES
 HALO_TYPE = jnp.bfloat16
 F32 = jnp.float32
+TOP = 14.0
 
 
 VELS = [(i // 9 - 1, (i // 3) % 3 - 1, i % 3 - 1) for i in range(27)]
@@ -197,6 +198,9 @@
     return [v - p for v, p in zip(xs + ys, patterns)]
 
 
+FOLD = 48
+
+
 def corner_lanes(lane, cx):
     col = 0 if cx > 0 else 112
     slots = [y_slot(cx, cz) for cz in (-1, 0, 1)] + [y_flag_slot(cx)]
@@ -208,8 +212,13 @@
 
 def corners(yp, ym):
     lane = lax.broadcasted_iota(jnp.int32, yp.shape, 1)
-    up = corner_lanes(lane, 1) | corner_lanes(lane, -1)
-    return jnp.where(up, yp, turn(ym, 16))
+    upper = corner_lanes(lane + 96, -1)
+    lines = jnp.where(corner_lanes(lane, 1), yp, jnp.where(upper, turn(yp, -96), turn(ym, 16)))
+    lane = lane[:FOLD]
+    out = lines[:FOLD]
+    for k in range(1, HALO_ROWS // FOLD):
+        out = jnp.where(lane // 32 == k, turn(lines[k * FOLD : (k + 1) * FOLD], 32 * k), out)
+    return out
 
 
 def all_patterns(lane):
@@ -316,12 +325,14 @@
 
 
 def patch_kernel(low, high, yp_in, ym_in, yp_out, ym_out):
-    lane = lax.broadcasted_iota(jnp.int32, (HALO_ROWS, LANES), 1)
-    for shift, source, out in ((0, yp_in, yp_out), (-16, ym_in, ym_out)):
-        acc = source[...].astype(F32)
-        for cx, got in ((1, low), (-1, high)):
-            acc = jnp.where(corner_lanes(lane, cx), turn(got[...].astype(F32), shift), acc)
-        out[...] = acc.astype(out.dtype)
+    lane = lax.broadcasted_iota(jnp.int32, (FOLD, LANES), 1)
+    got = {1: low[...].astype(F32), -1: high[...].astype(F32)}
+    for shift, source, out in (({1: 0, -1: 96}, yp_in, yp_out), ({1: -16, -1: 112}, ym_in, ym_out)):
+        for k in range(HALO_ROWS // FOLD):
+            acc = source[k * FOLD : (k + 1) * FOLD, :].astype(F32)
+            for cx in (1, -1):
+                acc = jnp.where(corner_lanes(lane, cx), turn(got[cx], shift[cx] - 32 * k), acc)
+            out[k * FOLD : (k + 1) * FOLD, :] = acc.astype(out.dtype)
 
 
 def step_kernel(first, last, *refs):
@@ -386,7 +397,7 @@
                         y_flag_slot(cx), lambda a: ys[a, at, :])
             return carry
 
-        lax.fori_loop(0, TILES, walls, 0)
+        lax.fori_loop(0, TILES, walls, 0, unroll=6)
 
     def gather_tile(t, buf):
         here = pl.ds(pl.multiple_of(8 * t, 8), 8)
@@ -466,7 +477,7 @@
     return hi, mid, low
 
 
-def sample_kernel(upper, mom, lane_hot, row_hot, area, placing, out):
+def sample_rows(upper, mom, lane_hot, row_hot, area, placing):
     fields = []
     hot = row_hot[...]
     lanes = lane_hot[...]
@@ -483,19 +494,30 @@
     rows = [rho * flow] + [pressure * normal[j] + rho * u[j] * flow for j in range(3)]
     blank = [jnp.zeros_like(rho)] * 4
     stacked = jnp.concatenate(blank + rows if upper else rows + blank, axis=0).astype(jnp.bfloat16)
-    out[...] = lax.dot_general(stacked, placing[...], (((1,), (1,)), ((), ())), preferred_element_type=F32)
-
-
-def scatter_kernel(groups, capacity, *refs):
-    parts, out = refs[:-1], refs[-1]
-    pairs = [parts[0][...] + parts[1][...], parts[2][...] + parts[3][...]]
+    return lax.dot_general(stacked, placing[...], (((1,), (1,)), ((), ())), preferred_element_type=F32)
+
+
+def sample_kernel(upper, *refs):
+    refs[-1][...] = sample_rows(upper, *refs[:-1])
+
+
+def scatter_kernel(groups, capacity, mom, lane_hot, row_hot, area, placing, part0, part1, part2, out):
+    last = sample_rows(1, mom, lane_hot, row_hot, area, placing)
+    pairs = [part0[...] + part1[...], part2[...] + last]
     lane = lane_iota()
     for g in range(groups):
         start = g * capacity
         tile = slice(start // LANES * LANES, start // LANES * LANES + LANES)
         low = turn(pairs[0][:, tile], -start)
         high = turn(pairs[1][:, tile], 64 - start)
-        out[g] = jnp.where(lane < 64, low, high)
+        value = jnp.where(lane < 64, low, high)
+        out[g] = value
+
+
+def fetch_kernel(weights_hbm, unused, out, sem):
+    copy = pltpu.make_async_copy(weights_hbm.at[pl.ds(0, out.shape[0])], out, sem.at[0])
+    copy.start()
+    copy.wait()
 
 
 def window_kernel(solid_hbm, mom, unused, density_out, velocity_out, solid, sem):
@@ -508,15 +530,12 @@
         velocity_out[a] = jnp.where(wall, 0.0, mom[a + 1, 8:136, :].T)
 
 
-def observe_kernel(groups, capacity, ptile, rec, weights_hbm, offset, out, weights, sem):
-    obs = weights.shape[2]
+def observe_kernel(groups, capacity, ptile, weights_hbm, near, offset, rec, out_hbm, rest, out, sem):
+    ahead = near.shape[0]
+    copy = pltpu.make_async_copy(weights_hbm.at[pl.ds(ahead, 4 - ahead)], rest, sem.at[0])
+    copy.start()
+    obs = rest.shape[2]
     part = obs // 2
-    copies = {}
-    for h in range(2):
-        for k in range(4):
-            at = (k, slice(None), pl.ds(h * part, part))
-            copies[h, k] = pltpu.make_async_copy(weights_hbm.at[at], weights.at[at], sem.at[4 * h + k])
-            copies[h, k].start()
     tiles = offset.shape[0]
     rows = groups * capacity
     halves = []
@@ -542,12 +561,19 @@
     devices = out.shape[0]
     count = obs // devices
     obs_tile = obs // offset.shape[1]
+    stores = []
     for h in range(2):
         acc = None
         for k in range(4):
-            copies[h, k].wait()
-            term = jnp.dot(lefts[k], weights[k, :, h * part : (h + 1) * part], preferred_element_type=F32)
+            if k == ahead and h == 0:
+                copy.wait()
+            cols = slice(h * part, (h + 1) * part)
+            right = near[k, :, cols] if k < ahead else rest[k - ahead, :, cols]
+            term = jnp.dot(lefts[k], right, preferred_element_type=F32)
             acc = term if acc is None else acc + term
+        peak = jnp.max(jnp.max(jnp.abs(acc), axis=1, keepdims=True), axis=0, keepdims=True)
+        power = jnp.broadcast_to(jnp.ceil(jnp.log2(jnp.maximum(peak, 1e-30))), (tiles, LANES))
+        down = jnp.exp2(TOP - power)
         for d in range(h * devices // 2, (h + 1) * devices // 2):
             start = d * count
             here = start - h * part
@@ -556,28 +582,34 @@
                 block = acc[tiles * s : tiles * (s + 1), here // LANES * LANES : here // LANES * LANES + LANES]
                 moved = turn(block, s * count - start % LANES)
                 piece = jnp.where(lane // count == s, moved, piece)
-            out[d, 0:tiles, :] = piece
+            out[d, 0:tiles, :] = piece * down
             o = start // obs_tile
-            out[d, tiles : 2 * tiles, :] = jnp.broadcast_to(offset[:, o : o + 1], (tiles, LANES))
+            out[d, tiles : 2 * tiles, :] = jnp.where(lane < 64, jnp.broadcast_to(offset[:, o : o + 1], (tiles, LANES)), power)
+        half = pl.ds(h * (devices // 2), devices // 2)
+        stores.append(pltpu.make_async_copy(out.at[half], out_hbm.at[half], sem.at[1 + h]))
+        stores[h].start()
+    for store in stores:
+        store.wait()
 
 
 def signal_kernel(got, out):
     devices, twice = got.shape[0], got.shape[1]
     tiles = twice // 2
     count = out.shape[0]
-    values = got[:, 0:tiles, :].reshape(devices * tiles, LANES)
-    start = got[:, tiles:twice, :].reshape(devices * tiles, LANES)
+    shape = (devices * tiles, LANES)
+    notes = got[:, tiles:twice, :].reshape(shape)
+    start = jnp.broadcast_to(notes[:, 0:1], shape)
+    values = got[:, 0:tiles, :].reshape(shape) * jnp.exp2(jnp.broadcast_to(notes[:, 64:65], shape) - TOP)
     bins = lax.broadcasted_iota(jnp.int32, (devices * tiles, NB), 1).astype(F32)
-    parts = split3(values)
+    hot = (start == bins).astype(F32).astype(jnp.bfloat16)
+    acc = None
+    for part in split3(values):
+        term = lax.dot_general(part, hot, (((0,), (0,)), ((), ())), preferred_element_type=F32)
+        acc = term if acc is None else acc + term
     total = None
     for s in range(STEPS):
-        hot = (start + float(s) == bins).astype(F32).astype(jnp.bfloat16)
-        acc = None
-        for part in parts:
-            term = lax.dot_general(part, hot, (((0,), (0,)), ((), ())), preferred_element_type=F32)
-            acc = term if acc is None else acc + term
-        acc = acc[s * count : (s + 1) * count, :]
-        total = acc if total is None else total + acc
+        moved = turn(acc[s * count : (s + 1) * count, :], s)
+        total = moved if total is None else total + moved
     out[...] = total
 
 
@@ -630,6 +662,7 @@
     rim = jax.ShapeDtypeStruct((28 * 4, LANES), F32)
     x_face = jax.ShapeDtypeStruct((3, HALO_ROWS, LANES), HALO_TYPE)
     y_face = jax.ShapeDtypeStruct((HALO_ROWS, LANES), HALO_TYPE)
+    x_edge = jax.ShapeDtypeStruct((FOLD, LANES), HALO_TYPE)
     x_scratch = pltpu.VMEM((3, HALO_ROWS, LANES), F32)
     y_scratch = pltpu.VMEM((2, HALO_ROWS, LANES), F32)
 
@@ -655,7 +688,7 @@
         panel_owner.reshape(1, slots), panel_owner.reshape(slots, 1), panel_cell.reshape(1, slots))
 
     star, walls, xp, yp, ym, xc = call(
-        first_kernel, (block, one, x_face, y_face, y_face, y_face), f0, flags, below, above, placing,
+        first_kernel, (block, one, x_face, y_face, y_face, x_edge), f0, flags, below, above, placing,
         scratch=(pltpu.VMEM((28, 16, LANES), F32), x_scratch, y_scratch))
 
     mom_shape = jax.ShapeDtypeStruct((4, HALO_ROWS, LANES), F32)
@@ -665,7 +698,7 @@
         xh, yph, ymh = exchange(xp, yp, ym, xc)
         outs = [mom_shape]
         if not last:
-            outs += [block, x_face, y_face, y_face, y_face]
+            outs += [block, x_face, y_face, y_face, x_edge]
         if first:
             outs += [jax.ShapeDtypeStruct((9, ROWS, LANES), F32)]
         scratch = [pltpu.VMEM((3, ROWS, LANES), F32), pltpu.VMEM((2, ROWS, LANES), F32)]
@@ -679,30 +712,43 @@
             star, xp, yp, ym, xc = res[1:6]
         if first:
             walls = res[6]
-        routed.append(call(functools.partial(sample_kernel, s % 2), jax.ShapeDtypeStruct((8, row_count), F32),
-                           mom, lane_hot, row_hot, panel_area, placing))
-
-    sent = call(functools.partial(scatter_kernel, group_count, capacity),
-                jax.ShapeDtypeStruct((group_count, 8, LANES), F32), *routed)
+        if not last:
+            routed.append(call(functools.partial(sample_kernel, s % 2), jax.ShapeDtypeStruct((8, row_count), F32),
+                               mom, lane_hot, row_hot, panel_area, placing))
+
+    send = functools.partial(scatter_kernel, group_count, capacity)
+    samples = (mom, lane_hot, row_hot, panel_area, placing, *routed)
+
+    def fetch(count, after):
+        return call(fetch_kernel,
+                    jax.ShapeDtypeStruct((count,) + weights.shape[1:], weights.dtype), weights, after, far=(0,),
+                    scratch=(pltpu.SemaphoreType.DMA((1,)),))
+
+    sent = call(send, jax.ShapeDtypeStruct((group_count, 8, LANES), F32), *samples)
     received = lax.all_to_all(sent, ("gx", "gy"), split_axis=0, concat_axis=0, tiled=True)
-
-    final_density, final_velocity = call(
-        window_kernel,
-        (jax.ShapeDtypeStruct(flat, F32), jax.ShapeDtypeStruct((3,) + flat, F32)),
-        solid, mom, sent, far=(0,), scratch=(pltpu.VMEM(flat, jnp.int32), pltpu.SemaphoreType.DMA((1,))))
+    near = fetch(3, sent)
 
     tiles, obs_tiles = bin_offset.shape
     devices = lax.axis_size(("gx", "gy", "gz"))
     obs = weights.shape[2]
     count = obs // devices
     assert obs // obs_tiles % count == 0 and tiles % 8 == 0 and STEPS * count <= LANES and capacity <= 64
-    observed = call(
+    out_shape = (devices, 2 * tiles, LANES)
+    observed = pl.pallas_call(
         functools.partial(observe_kernel, group_count, capacity, row_count // tiles),
-        jax.ShapeDtypeStruct((devices, 2 * tiles, LANES), F32),
-        received, weights, bin_offset.astype(F32), far=(1,),
-        scratch=(pltpu.VMEM(weights.shape, weights.dtype), pltpu.SemaphoreType.DMA((8,))))
-    got = lax.all_to_all(observed, ("gx", "gy", "gz"), split_axis=0, concat_axis=0, tiled=True)
-    signal = call(signal_kernel, jax.ShapeDtypeStruct((count, NB), F32), got)
+        out_shape=jax.ShapeDtypeStruct(out_shape, F32),
+        in_specs=[pl.BlockSpec(memory_space=pltpu.HBM)] + [pl.BlockSpec(memory_space=pltpu.VMEM)] * 3,
+        out_specs=pl.BlockSpec(memory_space=pltpu.HBM),
+        scratch_shapes=[pltpu.VMEM((4 - near.shape[0],) + weights.shape[1:], weights.dtype), pltpu.VMEM(out_shape, F32),
+                        pltpu.SemaphoreType.DMA((3,))],
+        compiler_params=pltpu.CompilerParams(vmem_limit_bytes=24 << 20),
+    )(pltpu.with_memory_space_constraint(weights, pltpu.HBM), near, bin_offset.astype(F32), received)
+    final_density, final_velocity = call(
+        window_kernel,
+        (jax.ShapeDtypeStruct(flat, F32), jax.ShapeDtypeStruct((3,) + flat, F32)),
+        solid, mom, sent, far=(0,), scratch=(pltpu.VMEM(flat, jnp.int32), pltpu.SemaphoreType.DMA((1,))))
+    got = lax.all_to_all(observed.astype(jnp.float16), ("gx", "gy", "gz"), split_axis=0, concat_axis=0, tiled=True)
+    signal = call(signal_kernel, jax.ShapeDtypeStruct((count, NB), F32), got.astype(F32))
     return final_density.reshape(density.shape), final_velocity.reshape(velocity.shape), signal
 
 

time: 101 us -> 97.6 us (0.966)
  waiting for transfers between devices: 36.3 us -> 30.2 us
  Pallas kernels: 28.1 us -> 29.7 us
    all_to_all x1, waiting for transfers between devices: 6.71 us -> 4.03 us  [shards(): lax.all_to_all(sent, ('gx', 'gy'), split_axis=0, concat_axis=0, tiled=True)]
    pallas_call x0 -> x1, Pallas kernels: none -> 2.57 us  [shards(): pl.pallas_call(functools.partial(observe_kernel, group_count, capacity, r...]
    all_to_all x1, waiting for transfers between devices: 7.83 us -> 5.78 us  [shards(): lax.all_to_all(observed.astype(jnp.float16), ('gx', 'gy', 'gz'), split_ax...]
    ppermute x16, waiting for transfers between devices: 20.6 us -> 19.2 us  [shift(): return lax.ppermute(value, axis, ring(axis, by))]
    pallas_call x19 -> x18, Pallas kernels: 28.1 us -> 27.1 us  [call(): pl.pallas_call(kernel, out_shape=outs, in_specs=[pl.BlockSpec(memory_spac...]
  transfers between devices with their start and end apart: 20 -> 20, of which waited for: 13 -> 13; matrix products, arithmetic and copies ran while one was open for 1% -> 1% of each run, Pallas kernels for 4% -> 7%
where the time goes in v1:
time: 97.6 us; the launch traced here: 97 us
  starting transfers between devices  34.9 us (36%)
  waiting for transfers between devices  30.2 us (31%)
  Pallas kernels  29.7 us (30%)
    pallas_call x18, Pallas kernels, call(): pl.pallas_call(kernel, out_shape=outs, in_specs=[pl.BlockSpec(memory_spac...  27.1 us
    ppermute x16, starting transfers between devices, shift(): return lax.ppermute(value, axis, ring(axis, by))  23.9 us
    ppermute x16, waiting for transfers between devices, shift(): return lax.ppermute(value, axis, ring(axis, by))  19.2 us
    all_to_all x1, starting transfers between devices, shards(): lax.all_to_all(sent, ('gx', 'gy'), split_axis=0, concat_axis=0, tiled=True)  5.79 us
    all_to_all x1, waiting for transfers between devices, shards(): lax.all_to_all(observed.astype(jnp.float16), ('gx', 'gy', 'gz'), split_ax...  5.78 us
    all_to_all x1, waiting for transfers between devices, shards(): lax.all_to_all(sent, ('gx', 'gy'), split_axis=0, concat_axis=0, tiled=True)  4.03 us
    pallas_call x1, Pallas kernels, shards(): pl.pallas_call(functools.partial(observe_kernel, group_count, capacity, r...  2.57 us
    all_to_all x1, starting transfers between devices, shards(): lax.all_to_all(observed.astype(jnp.float16), ('gx', 'gy', 'gz'), split_ax...  2.56 us
  transfers between devices with their start and end apart: 20, of which 13 were waited for; matrix products, arithmetic and copies ran while one was open for 1% of the time, Pallas kernels for 7%

profile of v1, /device:TPU:0, one launch (start us, length us, event | category | flops | bytes accessed | tf_op | source)
XLA Modules:
  0.0 97.0 jit_solution(6724922948433495211)
XLA Ops:
  0.7 3.1 %shard_map.121 = (f32[27,160,128]{2,1,0:T(8,128)S(1)}, f32[112,128]{1,0:T(8,128)S(1)}, f32[112,128]{1,0:T(8,128)S(1)}, f32[160,128]{1,0:T(8,128)S(1)}) custom-call(f32[27,128,128]{2,1,0:T(8,128)} %bitcast.13, f32[128,128]{1,0:T(8,128)} %bitcast.17, f32[3,128,128]{2,1,0:T(8,128)} %bitcast.16, f32[128,128]{1,0:T(8,128)} %bitcast.18, s32[128,128]{1,0:T(8,128)} %bitcast.14), custom_call_target="tpu_custom_call" | custom-call | flops 1000000 | bytes 2162688 | tf_op jit(solution)/shard_map/pallas_call | solution.py:618
  3.7 0.5 collective-permute-start
  4.3 2.0 %collective-permute-start.1 = (f32[112,128]{1,0:T(8,128)S(1)}, f32[112,128]{1,0:T(8,128)S(1)}, u32[]{:S(2)}, u32[]{:S(2)}) collective-permute-start(f32[112,128]{1,0:T(8,128)S(1)} %get-tuple-element.48), channel_id=1, source_target_pairs={{0,3},{1,0},{2,1},{3,2},{4,7},{5,4},{6,5},{7,6},{8,11},{9,8},{10,9... | collective-permute-start | bytes 172040 | tf_op jit(solution)/shard_map/ppermute | solution.py:677
  6.3 0.8 copy.13.owner_col
  7.3 0.7 collective-permute-done.lo
  8.1 0.4 collective-permute-done.1.hi
  8.5 2.7 %shard_map.123 = (f32[27,160,128]{2,1,0:T(8,128)S(1)}, f32[160,128]{1,0:T(8,128)S(1)}, bf16[3,144,128]{2,1,0:T(8,128)(2,1)S(1)}, bf16[144,128]{1,0:T(8,128)(2,1)...) custom-call(f32[27,160,128]{2,1,0:T(8,128)S(1)} %get-tuple-element.45.f_in, ...), custom_call_target="tpu_custom_call" | custom-call | flops 1000000 | bytes 2670592 | tf_op jit(solution)/shard_map/pallas_call | solution.py:618
  11.2 1.9 %collective-permute-start.2 = (bf16[3,144,128]{2,1,0:T(8,128)(2,1)S(1)}, bf16[3,144,128]{2,1,0:T(8,128)(2,1)S(1)}, u32[]{:S(2)}, u32[]{:S(2)}) collective-permute-start(bf16[3,144,128]{2,1,0:T(8,128)(2,1)S(1)} %get-tuple-element.52), channel_id=1, source_target_pairs={{0,16},{16,0},{1,17},{17,1},{2,18},{18,2},{3,19},{19,3},{4,20},{20... | collective-permute-start | bytes 331784 | tf_op jit(solution)/shard_map/ppermute | solution.py:637
  13.3 3.6 %collective-permute-done.3.low.high = bf16[48,128]{1,0:T(8,128)(2,1)S(1)} collective-permute-done((bf16[48,128]{1,0:T(8,128)(2,1)S(1)}, bf16[48,128]{1,0:T(8,128)(2,1)S(1)}, u32[]{:S(2)}, u32[]{:S(2)}) %collective-permute-start.3) | collective-permute-done | bytes 12320 | tf_op jit(solution)/shard_map/ppermute | solution.py:637
  17.0 1.8 %collective-permute-start.4 = (bf16[144,128]{1,0:T(8,128)(2,1)S(1)}, bf16[144,128]{1,0:T(8,128)(2,1)S(1)}, u32[]{:S(2)}, u32[]{:S(2)}) collective-permute-start(bf16[144,128]{1,0:T(8,128)(2,1)S(1)} %get-tuple-element.56), channel_id=1, source_target_pairs={{0,4},{4,8},{8,12},{12,0},{1,5},{5,9},{9,13},{13,1},{2,6},{6,10},{... | collective-permute-start | bytes 110600 | tf_op jit(solution)/shard_map/ppermute | solution.py:637
  18.9 2.1 %collective-permute-start.5 = (bf16[144,128]{1,0:T(8,128)(2,1)S(1)}, bf16[144,128]{1,0:T(8,128)(2,1)S(1)}, u32[]{:S(2)}, u32[]{:S(2)}) collective-permute-start(bf16[144,128]{1,0:T(8,128)(2,1)S(1)} %get-tuple-element.57), channel_id=1, source_target_pairs={{0,12},{4,0},{8,4},{12,8},{1,13},{5,1},{9,5},{13,9},{2,14},{6,2},{... | collective-permute-start | bytes 110600 | tf_op jit(solution)/shard_map/ppermute | solution.py:637
  21.0 2.1 %collective-permute-done.4.refs_3_ = bf16[144,128]{1,0:T(8,128)(2,1)S(1)} collective-permute-done((bf16[144,128]{1,0:T(8,128)(2,1)S(1)}, bf16[144,128]{1,0:T(8,128)(2,1)S(1)}, u32[]{:S(2)}, u32[]{:S(2)}) %collective-permute-start.4) | collective-permute-done | bytes 36896 | tf_op jit(solution)/shard_map/ppermute | solution.py:637
  23.1 0.3 collective-permute-done.5.refs_4_
  23.4 3.7 %shard_map.125 = (f32[4,144,128]{2,1,0:T(8,128)S(1)}, f32[27,160,128]{2,1,0:T(8,128)S(1)}, bf16[3,144,128]{2,1,0:T(8,128)(2,1)S(1)}, bf16[144,128]{1,0:T(8,128)(...) custom-call(f32[27,160,128]{2,1,0:T(8,128)S(1)} %get-tuple-element.50.refs_0_, ...), custom_call_target="tpu_custom_call" | custom-call | flops 1000000 | bytes 2740224 | tf_op jit(solution)/shard_map/pallas_call | solution.py:618
  27.1 1.5 %collective-permute-start.6 = (bf16[3,144,128]{2,1,0:T(8,128)(2,1)S(1)}, bf16[3,144,128]{2,1,0:T(8,128)(2,1)S(1)}, u32[]{:S(2)}, u32[]{:S(2)}) collective-permute-start(bf16[3,144,128]{2,1,0:T(8,128)(2,1)S(1)} %get-tuple-element.60), channel_id=1, source_target_pairs={{0,16},{16,0},{1,17},{17,1},{2,18},{18,2},{3,19},{19,3},{4,20},{20... | collective-permute-start | bytes 331784 | tf_op jit(solution)/shard_map/ppermute | solution.py:637
  28.6 0.5 collective-permute-start.7
  29.2 3.2 %collective-permute-done.7.low.high = bf16[48,128]{1,0:T(8,128)(2,1)S(1)} collective-permute-done((bf16[48,128]{1,0:T(8,128)(2,1)S(1)}, bf16[48,128]{1,0:T(8,128)(2,1)S(1)}, u32[]{:S(2)}, u32[]{:S(2)}) %collective-permute-start.7) | collective-permute-done | bytes 12320 | tf_op jit(solution)/shard_map/ppermute | solution.py:637
  32.4 1.0 %collective-permute-start.8 = (bf16[144,128]{1,0:T(8,128)(2,1)S(1)}, bf16[144,128]{1,0:T(8,128)(2,1)S(1)}, u32[]{:S(2)}, u32[]{:S(2)}) collective-permute-start(bf16[144,128]{1,0:T(8,128)(2,1)S(1)} %get-tuple-element.64), channel_id=1, source_target_pairs={{0,4},{4,8},{8,12},{12,0},{1,5},{5,9},{9,13},{13,1},{2,6},{6,10},{... | collective-permute-start | bytes 110600 | tf_op jit(solution)/shard_map/ppermute | solution.py:637
  33.5 2.8 %collective-permute-start.9 = (bf16[144,128]{1,0:T(8,128)(2,1)S(1)}, bf16[144,128]{1,0:T(8,128)(2,1)S(1)}, u32[]{:S(2)}, u32[]{:S(2)}) collective-permute-start(bf16[144,128]{1,0:T(8,128)(2,1)S(1)} %get-tuple-element.65), channel_id=1, source_target_pairs={{0,12},{4,0},{8,4},{12,8},{1,13},{5,1},{9,5},{13,9},{2,14},{6,2},{... | collective-permute-start | bytes 110600 | tf_op jit(solution)/shard_map/ppermute | solution.py:637
  36.3 0.5 shard_map.127.refs_5_.part0
  36.8 1.5 %collective-permute-done.8.refs_3_ = bf16[144,128]{1,0:T(8,128)(2,1)S(1)} collective-permute-done((bf16[144,128]{1,0:T(8,128)(2,1)S(1)}, bf16[144,128]{1,0:T(8,128)(2,1)S(1)}, u32[]{:S(2)}, u32[]{:S(2)}) %collective-permute-start.8) | collective-permute-done | bytes 36896 | tf_op jit(solution)/shard_map/ppermute | solution.py:637
  38.3 3.1 %shard_map.128 = (f32[4,144,128]{2,1,0:T(8,128)S(1)}, f32[27,160,128]{2,1,0:T(8,128)S(1)}, bf16[3,144,128]{2,1,0:T(8,128)(2,1)S(1)}, bf16[144,128]{1,0:T(8,128)(...) custom-call(f32[27,160,128]{2,1,0:T(8,128)S(1)} %get-tuple-element.58.refs_0_, ...), custom_call_target="tpu_custom_call" | custom-call | flops 1000000 | bytes 3149824 | tf_op jit(solution)/shard_map/pallas_call | solution.py:618
  41.4 1.2 %collective-permute-start.10 = (bf16[3,144,128]{2,1,0:T(8,128)(2,1)S(1)}, bf16[3,144,128]{2,1,0:T(8,128)(2,1)S(1)}, u32[]{:S(2)}, u32[]{:S(2)}) collective-permute-start(bf16[3,144,128]{2,1,0:T(8,128)(2,1)S(1)} %get-tuple-element.70), channel_id=1, source_target_pairs={{0,16},{16,0},{1,17},{17,1},{2,18},{18,2},{3,19},{19,3},{4,20},{20... | collective-permute-start | bytes 331784 | tf_op jit(solution)/shard_map/ppermute | solution.py:637
  42.6 0.8 collective-permute-start.11
  43.5 2.9 %collective-permute-done.11.low.high = bf16[48,128]{1,0:T(8,128)(2,1)S(1)} collective-permute-done((bf16[48,128]{1,0:T(8,128)(2,1)S(1)}, bf16[48,128]{1,0:T(8,128)(2,1)S(1)}, u32[]{:S(2)}, u32[]{:S(2)}) %collective-permute-start.11) | collective-permute-done | bytes 12320 | tf_op jit(solution)/shard_map/ppermute | solution.py:637
  46.4 1.0 %collective-permute-start.12 = (bf16[144,128]{1,0:T(8,128)(2,1)S(1)}, bf16[144,128]{1,0:T(8,128)(2,1)S(1)}, u32[]{:S(2)}, u32[]{:S(2)}) collective-permute-start(bf16[144,128]{1,0:T(8,128)(2,1)S(1)} %get-tuple-element.74), channel_id=1, source_target_pairs={{0,4},{4,8},{8,12},{12,0},{1,5},{5,9},{9,13},{13,1},{2,6},{6,10},{... | collective-permute-start | bytes 110600 | tf_op jit(solution)/shard_map/ppermute | solution.py:637
  47.4 2.9 %collective-permute-start.13 = (bf16[144,128]{1,0:T(8,128)(2,1)S(1)}, bf16[144,128]{1,0:T(8,128)(2,1)S(1)}, u32[]{:S(2)}, u32[]{:S(2)}) collective-permute-start(bf16[144,128]{1,0:T(8,128)(2,1)S(1)} %get-tuple-element.75), channel_id=1, source_target_pairs={{0,12},{4,0},{8,4},{12,8},{1,13},{5,1},{9,5},{13,9},{2,14},{6,2},{... | collective-permute-start | bytes 110600 | tf_op jit(solution)/shard_map/ppermute | solution.py:637
  50.4 0.5 shard_map.130.refs_5_.part1
  50.8 1.4 %collective-permute-done.12.refs_3_ = bf16[144,128]{1,0:T(8,128)(2,1)S(1)} collective-permute-done((bf16[144,128]{1,0:T(8,128)(2,1)S(1)}, bf16[144,128]{1,0:T(8,128)(2,1)S(1)}, u32[]{:S(2)}, u32[]{:S(2)}) %collective-permute-start.12) | collective-permute-done | bytes 36896 | tf_op jit(solution)/shard_map/ppermute | solution.py:637
  52.2 3.1 %shard_map.131 = (f32[4,144,128]{2,1,0:T(8,128)S(1)}, f32[27,160,128]{2,1,0:T(8,128)S(1)}, bf16[3,144,128]{2,1,0:T(8,128)(2,1)S(1)}, bf16[144,128]{1,0:T(8,128)(...) custom-call(f32[27,160,128]{2,1,0:T(8,128)S(1)} %get-tuple-element.69.refs_0_, ...), custom_call_target="tpu_custom_call" | custom-call | flops 1000000 | bytes 3149824 | tf_op jit(solution)/shard_map/pallas_call | solution.py:618
  55.4 1.2 %collective-permute-start.14 = (bf16[3,144,128]{2,1,0:T(8,128)(2,1)S(1)}, bf16[3,144,128]{2,1,0:T(8,128)(2,1)S(1)}, u32[]{:S(2)}, u32[]{:S(2)}) collective-permute-start(bf16[3,144,128]{2,1,0:T(8,128)(2,1)S(1)} %get-tuple-element.78), channel_id=1, source_target_pairs={{0,16},{16,0},{1,17},{17,1},{2,18},{18,2},{3,19},{19,3},{4,20},{20... | collective-permute-start | bytes 331784 | tf_op jit(solution)/shard_map/ppermute | solution.py:637
  56.6 0.8 collective-permute-start.15
  57.4 2.9 %collective-permute-done.15.low.high = bf16[48,128]{1,0:T(8,128)(2,1)S(1)} collective-permute-done((bf16[48,128]{1,0:T(8,128)(2,1)S(1)}, bf16[48,128]{1,0:T(8,128)(2,1)S(1)}, u32[]{:S(2)}, u32[]{:S(2)}) %collective-permute-start.15) | collective-permute-done | bytes 12320 | tf_op jit(solution)/shard_map/ppermute | solution.py:637
  60.4 1.2 %collective-permute-start.16 = (bf16[144,128]{1,0:T(8,128)(2,1)S(1)}, bf16[144,128]{1,0:T(8,128)(2,1)S(1)}, u32[]{:S(2)}, u32[]{:S(2)}) collective-permute-start(bf16[144,128]{1,0:T(8,128)(2,1)S(1)} %get-tuple-element.82), channel_id=1, source_target_pairs={{0,4},{4,8},{8,12},{12,0},{1,5},{5,9},{9,13},{13,1},{2,6},{6,10},{... | collective-permute-start | bytes 110600 | tf_op jit(solution)/shard_map/ppermute | solution.py:637
  61.6 2.8 %collective-permute-start.17 = (bf16[144,128]{1,0:T(8,128)(2,1)S(1)}, bf16[144,128]{1,0:T(8,128)(2,1)S(1)}, u32[]{:S(2)}, u32[]{:S(2)}) collective-permute-start(bf16[144,128]{1,0:T(8,128)(2,1)S(1)} %get-tuple-element.83), channel_id=1, source_target_pairs={{0,12},{4,0},{8,4},{12,8},{1,13},{5,1},{9,5},{13,9},{2,14},{6,2},{... | collective-permute-start | bytes 110600 | tf_op jit(solution)/shard_map/ppermute | solution.py:637
  64.4 0.5 shard_map.133.refs_5_.part2
  64.9 1.4 %collective-permute-done.16.refs_3_ = bf16[144,128]{1,0:T(8,128)(2,1)S(1)} collective-permute-done((bf16[144,128]{1,0:T(8,128)(2,1)S(1)}, bf16[144,128]{1,0:T(8,128)(2,1)S(1)}, u32[]{:S(2)}, u32[]{:S(2)}) %collective-permute-start.16) | collective-permute-done | bytes 36896 | tf_op jit(solution)/shard_map/ppermute | solution.py:637
  66.3 2.0 %shard_map.134.mom = f32[4,144,128]{2,1,0:T(8,128)S(1)} custom-call(f32[27,160,128]{2,1,0:T(8,128)S(1)} %get-tuple-element.77.refs_0_, f32[9,160,128]{2,1,0:T(8,128)S(1)} %get-tuple-element.59.refs_1_, bf16[3,144,128]{2,1,0:T(8,128)(2,1)S(1)} %collective-permute-done.14.refs_2_, bf16[144,128]{1,0:T(8,128)(2,1)S(1)} %collective-permute-done.16.refs_3_, ...), custom_call_target="tpu_custom_call" | custom-call | flops 1000000 | bytes 3149824 | tf_op jit(solution)/shard_map/pallas_call | solution.py:618
  68.3 1.2 %shard_map.135.unused = f32[8,8,128]{2,1,0:T(8,128)} custom-call(f32[4,144,128]{2,1,0:T(8,128)S(1)} %shard_map.134.mom, bf16[128,256]{1,0:T(8,128)(2,1)S(1)} %get-tuple-element.67.refs_1_.lane_hot, f32[128,256]{1,0:T(8,128)S(1)} %get-tuple-element.68.refs_2_.row_hot, f32[3,256]{1,0:T(4,128)S(1)} %copy-done, ...), custom_call_target="tpu_custom_call" | custom-call | flops 1000000 | bytes 805888 | tf_op jit(solution)/shard_map/pallas_call | solution.py:618
  69.5 5.8 %all-to-all-start = ((f32[8,8,128]{2,1,0:T(8,128)}), f32[8,8,128]{2,1,0:T(8,128)S(1)}, u32[]{:S(2)}, u32[]{:S(2)}) async-start(f32[8,8,128]{2,1,0:T(8,128)} %shard_map.135.unused), calls=%async_computation | async-start | bytes 65536 | tf_op jit(solution)/shard_map/all_to_all | solution.py:728
  75.3 2.7 %shard_map.137.near = bf16[3,512,1024]{2,1,0:T(8,128)(2,1)S(1)} custom-call(bf16[4,512,1024]{2,1,0:T(8,128)(2,1)} %weights_hbm.3, f32[8,8,128]{2,1,0:T(8,128)} %shard_map.135.unused), custom_call_target="tpu_custom_call" | custom-call | flops 1000000 | bytes 4227072 | tf_op jit(solution)/shard_map/pallas_call | solution.py:618
  77.9 4.0 %all-to-all-done.rec = f32[8,8,128]{2,1,0:T(8,128)S(1)} async-done(((f32[8,8,128]{2,1,0:T(8,128)}), f32[8,8,128]{2,1,0:T(8,128)S(1)}, u32[]{:S(2)}, u32[]{:S(2)}) %all-to-all-start) | async-done | bytes 32800 | tf_op jit(solution)/shard_map/all_to_all | solution.py:728
  82.0 2.6 %shard_map.138 = f32[32,16,128]{2,1,0:T(8,128)S(1)} custom-call(bf16[4,512,1024]{2,1,0:T(8,128)(2,1)} %weights_hbm.3, bf16[3,512,1024]{2,1,0:T(8,128)(2,1)S(1)} %shard_map.137.near, f32[8,8]{1,0:T(8,128)S(1)} %convert_element_type.9.offset, f32[8,8,128]{2,1,0:T(8,128)S(1)} %all-to-all-done.rec), custom_call_target="tpu_custom_call" | custom-call | tf_op jit(solution)/shard_map/pallas_call | solution.py:737
  84.6 0.7 convert_element_type.10
  85.2 2.6 %all-to-all-start.1 = ((f16[32,16,128]{2,1,0:T(8,128)(2,1)}), f16[32,16,128]{2,1,0:T(8,128)(2,1)S(1)}, u32[]{:S(2)}, u32[]{:S(2)}) async-start(f16[32,16,128]{2,1,0:T(8,128)(2,1)} %convert_element_type.10), calls=%async_computation.1 | async-start | bytes 262144 | tf_op jit(solution)/shard_map/all_to_all | solution.py:750
  87.8 2.4 %shard_map.136 = (f32[128,128]{1,0:T(8,128)}, f32[3,128,128]{2,1,0:T(8,128)}) custom-call(s32[128,128]{1,0:T(8,128)} %bitcast.15, f32[4,144,128]{2,1,0:T(8,128)S(1)} %shard_map.134.mom, f32[8,8,128]{2,1,0:T(8,128)} %shard_map.135.unused), custom_call_target="tpu_custom_call" | custom-call | flops 1000000 | bytes 393216 | tf_op jit(solution)/shard_map/pallas_call | solution.py:618
  90.2 5.8 %all-to-all-done.1 = f16[32,16,128]{2,1,0:T(8,128)(2,1)S(1)} async-done(((f16[32,16,128]{2,1,0:T(8,128)(2,1)}), f16[32,16,128]{2,1,0:T(8,128)(2,1)S(1)}, u32[]{:S(2)}, u32[]{:S(2)}) %all-to-all-start.1) | async-done | bytes 131104 | tf_op jit(solution)/shard_map/all_to_all | solution.py:750
  96.0 1.0 %shard_map.139 = f32[32,128]{1,0:T(8,128)} custom-call(f32[32,16,128]{2,1,0:T(8,128)S(1)} %convert_element_type.11.got), custom_call_target="tpu_custom_call" | custom-call | flops 1000000 | bytes 262144 | tf_op jit(solution)/shard_map/pallas_call | solution.py:618
  (23 shorter events, 0.9 us)
Async XLA Ops:
  0.6 6.4 %copy-start.1 = (s32[256]{0:T(256)S(1)}, s32[256]{0:T(256)}, u32[]{:S(2)}) copy-start(s32[256]{0:T(256)} %param.16) | copy-start | bytes 3076
  0.6 6.4 %copy-start.2 = (s32[256]{0:T(256)S(1)}, s32[256]{0:T(256)}, u32[]{:S(2)}) copy-start(s32[256]{0:T(256)} %param.15) | copy-start | bytes 3076
  3.7 4.3 %collective-permute-start = (f32[112,128]{1,0:T(8,128)S(1)}, f32[112,128]{1,0:T(8,128)S(1)}, u32[]{:S(2)}, u32[]{:S(2)}) collective-permute-start(f32[112,128]{1,0:T(8,128)S(1)} %get-tuple-element.47), channel_id=1, source_target_pairs={{0,1},{1,2},{2,3},{3,0},{4,5},{5,6},{6,7},{7,4},{8,9},{9,10},{10,1... | collective-permute-start | bytes 172040 | tf_op jit(solution)/shard_map/ppermute | solution.py:676
  4.3 4.2 %collective-permute-start.1 = (f32[112,128]{1,0:T(8,128)S(1)}, f32[112,128]{1,0:T(8,128)S(1)}, u32[]{:S(2)}, u32[]{:S(2)}) collective-permute-start(f32[112,128]{1,0:T(8,128)S(1)} %get-tuple-element.48), channel_id=1, source_target_pairs={{0,3},{1,0},{2,1},{3,2},{4,7},{5,4},{6,5},{7,6},{8,11},{9,8},{10,9... | collective-permute-start | bytes 172040 | tf_op jit(solution)/shard_map/ppermute | solution.py:677
  8.5 27.8 %copy-start = (f32[3,256]{1,0:T(4,128)S(1)}, f32[3,256]{1,0:T(4,128)}, u32[]{:S(2)}) copy-start(f32[3,256]{1,0:T(4,128)} %area.1) | copy-start | bytes 9220
  11.2 12.2 %collective-permute-start.2 = (bf16[3,144,128]{2,1,0:T(8,128)(2,1)S(1)}, bf16[3,144,128]{2,1,0:T(8,128)(2,1)S(1)}, u32[]{:S(2)}, u32[]{:S(2)}) collective-permute-start(bf16[3,144,128]{2,1,0:T(8,128)(2,1)S(1)} %get-tuple-element.52), channel_id=1, source_target_pairs={{0,16},{16,0},{1,17},{17,1},{2,18},{18,2},{3,19},{19,3},{4,20},{20... | collective-permute-start | bytes 331784 | tf_op jit(solution)/shard_map/ppermute | solution.py:637
  13.1 3.8 %collective-permute-start.3 = (bf16[48,128]{1,0:T(8,128)(2,1)S(1)}, bf16[48,128]{1,0:T(8,128)(2,1)S(1)}, u32[]{:S(2)}, u32[]{:S(2)}) collective-permute-start(bf16[48,128]{1,0:T(8,128)(2,1)S(1)} %get-tuple-element.53), channel_id=1, source_target_pairs={{0,16},{16,0},{1,17},{17,1},{2,18},{18,2},{3,19},{19,3},{4,20},{20... | collective-permute-start | bytes 36872 | tf_op jit(solution)/shard_map/ppermute | solution.py:637
  17.0 6.1 %collective-permute-start.4 = (bf16[144,128]{1,0:T(8,128)(2,1)S(1)}, bf16[144,128]{1,0:T(8,128)(2,1)S(1)}, u32[]{:S(2)}, u32[]{:S(2)}) collective-permute-start(bf16[144,128]{1,0:T(8,128)(2,1)S(1)} %get-tuple-element.56), channel_id=1, source_target_pairs={{0,4},{4,8},{8,12},{12,0},{1,5},{5,9},{9,13},{13,1},{2,6},{6,10},{... | collective-permute-start | bytes 110600 | tf_op jit(solution)/shard_map/ppermute | solution.py:637
  18.9 4.5 %collective-permute-start.5 = (bf16[144,128]{1,0:T(8,128)(2,1)S(1)}, bf16[144,128]{1,0:T(8,128)(2,1)S(1)}, u32[]{:S(2)}, u32[]{:S(2)}) collective-permute-start(bf16[144,128]{1,0:T(8,128)(2,1)S(1)} %get-tuple-element.57), channel_id=1, source_target_pairs={{0,12},{4,0},{8,4},{12,8},{1,13},{5,1},{9,5},{13,9},{2,14},{6,2},{... | collective-permute-start | bytes 110600 | tf_op jit(solution)/shard_map/ppermute | solution.py:637
  27.1 11.2 %collective-permute-start.6 = (bf16[3,144,128]{2,1,0:T(8,128)(2,1)S(1)}, bf16[3,144,128]{2,1,0:T(8,128)(2,1)S(1)}, u32[]{:S(2)}, u32[]{:S(2)}) collective-permute-start(bf16[3,144,128]{2,1,0:T(8,128)(2,1)S(1)} %get-tuple-element.60), channel_id=1, source_target_pairs={{0,16},{16,0},{1,17},{17,1},{2,18},{18,2},{3,19},{19,3},{4,20},{20... | collective-permute-start | bytes 331784 | tf_op jit(solution)/shard_map/ppermute | solution.py:637
  28.6 3.7 %collective-permute-start.7 = (bf16[48,128]{1,0:T(8,128)(2,1)S(1)}, bf16[48,128]{1,0:T(8,128)(2,1)S(1)}, u32[]{:S(2)}, u32[]{:S(2)}) collective-permute-start(bf16[48,128]{1,0:T(8,128)(2,1)S(1)} %get-tuple-element.61), channel_id=1, source_target_pairs={{0,16},{16,0},{1,17},{17,1},{2,18},{18,2},{3,19},{19,3},{4,20},{20... | collective-permute-start | bytes 36872 | tf_op jit(solution)/shard_map/ppermute | solution.py:637
  32.4 5.8 %collective-permute-start.8 = (bf16[144,128]{1,0:T(8,128)(2,1)S(1)}, bf16[144,128]{1,0:T(8,128)(2,1)S(1)}, u32[]{:S(2)}, u32[]{:S(2)}) collective-permute-start(bf16[144,128]{1,0:T(8,128)(2,1)S(1)} %get-tuple-element.64), channel_id=1, source_target_pairs={{0,4},{4,8},{8,12},{12,0},{1,5},{5,9},{9,13},{13,1},{2,6},{6,10},{... | collective-permute-start | bytes 110600 | tf_op jit(solution)/shard_map/ppermute | solution.py:637
  33.5 4.8 %collective-permute-start.9 = (bf16[144,128]{1,0:T(8,128)(2,1)S(1)}, bf16[144,128]{1,0:T(8,128)(2,1)S(1)}, u32[]{:S(2)}, u32[]{:S(2)}) collective-permute-start(bf16[144,128]{1,0:T(8,128)(2,1)S(1)} %get-tuple-element.65), channel_id=1, source_target_pairs={{0,12},{4,0},{8,4},{12,8},{1,13},{5,1},{9,5},{13,9},{2,14},{6,2},{... | collective-permute-start | bytes 110600 | tf_op jit(solution)/shard_map/ppermute | solution.py:637
  41.4 10.8 %collective-permute-start.10 = (bf16[3,144,128]{2,1,0:T(8,128)(2,1)S(1)}, bf16[3,144,128]{2,1,0:T(8,128)(2,1)S(1)}, u32[]{:S(2)}, u32[]{:S(2)}) collective-permute-start(bf16[3,144,128]{2,1,0:T(8,128)(2,1)S(1)} %get-tuple-element.70), channel_id=1, source_target_pairs={{0,16},{16,0},{1,17},{17,1},{2,18},{18,2},{3,19},{19,3},{4,20},{20... | collective-permute-start | bytes 331784 | tf_op jit(solution)/shard_map/ppermute | solution.py:637
  42.6 3.7 %collective-permute-start.11 = (bf16[48,128]{1,0:T(8,128)(2,1)S(1)}, bf16[48,128]{1,0:T(8,128)(2,1)S(1)}, u32[]{:S(2)}, u32[]{:S(2)}) collective-permute-start(bf16[48,128]{1,0:T(8,128)(2,1)S(1)} %get-tuple-element.71), channel_id=1, source_target_pairs={{0,16},{16,0},{1,17},{17,1},{2,18},{18,2},{3,19},{19,3},{4,20},{20... | collective-permute-start | bytes 36872 | tf_op jit(solution)/shard_map/ppermute | solution.py:637
  46.4 5.8 %collective-permute-start.12 = (bf16[144,128]{1,0:T(8,128)(2,1)S(1)}, bf16[144,128]{1,0:T(8,128)(2,1)S(1)}, u32[]{:S(2)}, u32[]{:S(2)}) collective-permute-start(bf16[144,128]{1,0:T(8,128)(2,1)S(1)} %get-tuple-element.74), channel_id=1, source_target_pairs={{0,4},{4,8},{8,12},{12,0},{1,5},{5,9},{9,13},{13,1},{2,6},{6,10},{... | collective-permute-start | bytes 110600 | tf_op jit(solution)/shard_map/ppermute | solution.py:637
  47.4 4.8 %collective-permute-start.13 = (bf16[144,128]{1,0:T(8,128)(2,1)S(1)}, bf16[144,128]{1,0:T(8,128)(2,1)S(1)}, u32[]{:S(2)}, u32[]{:S(2)}) collective-permute-start(bf16[144,128]{1,0:T(8,128)(2,1)S(1)} %get-tuple-element.75), channel_id=1, source_target_pairs={{0,12},{4,0},{8,4},{12,8},{1,13},{5,1},{9,5},{13,9},{2,14},{6,2},{... | collective-permute-start | bytes 110600 | tf_op jit(solution)/shard_map/ppermute | solution.py:637
  55.4 10.9 %collective-permute-start.14 = (bf16[3,144,128]{2,1,0:T(8,128)(2,1)S(1)}, bf16[3,144,128]{2,1,0:T(8,128)(2,1)S(1)}, u32[]{:S(2)}, u32[]{:S(2)}) collective-permute-start(bf16[3,144,128]{2,1,0:T(8,128)(2,1)S(1)} %get-tuple-element.78), channel_id=1, source_target_pairs={{0,16},{16,0},{1,17},{17,1},{2,18},{18,2},{3,19},{19,3},{4,20},{20... | collective-permute-start | bytes 331784 | tf_op jit(solution)/shard_map/ppermute | solution.py:637
  56.6 3.7 %collective-permute-start.15 = (bf16[48,128]{1,0:T(8,128)(2,1)S(1)}, bf16[48,128]{1,0:T(8,128)(2,1)S(1)}, u32[]{:S(2)}, u32[]{:S(2)}) collective-permute-start(bf16[48,128]{1,0:T(8,128)(2,1)S(1)} %get-tuple-element.79), channel_id=1, source_target_pairs={{0,16},{16,0},{1,17},{17,1},{2,18},{18,2},{3,19},{19,3},{4,20},{20... | collective-permute-start | bytes 36872 | tf_op jit(solution)/shard_map/ppermute | solution.py:637
  60.4 5.9 %collective-permute-start.16 = (bf16[144,128]{1,0:T(8,128)(2,1)S(1)}, bf16[144,128]{1,0:T(8,128)(2,1)S(1)}, u32[]{:S(2)}, u32[]{:S(2)}) collective-permute-start(bf16[144,128]{1,0:T(8,128)(2,1)S(1)} %get-tuple-element.82), channel_id=1, source_target_pairs={{0,4},{4,8},{8,12},{12,0},{1,5},{5,9},{9,13},{13,1},{2,6},{6,10},{... | collective-permute-start | bytes 110600 | tf_op jit(solution)/shard_map/ppermute | solution.py:637
  61.6 4.7 %collective-permute-start.17 = (bf16[144,128]{1,0:T(8,128)(2,1)S(1)}, bf16[144,128]{1,0:T(8,128)(2,1)S(1)}, u32[]{:S(2)}, u32[]{:S(2)}) collective-permute-start(bf16[144,128]{1,0:T(8,128)(2,1)S(1)} %get-tuple-element.83), channel_id=1, source_target_pairs={{0,12},{4,0},{8,4},{12,8},{1,13},{5,1},{9,5},{13,9},{2,14},{6,2},{... | collective-permute-start | bytes 110600 | tf_op jit(solution)/shard_map/ppermute | solution.py:637
  64.9 10.4 %copy-start.3 = (s32[8,8]{1,0:T(8,128)S(1)}, s32[8,8]{1,0:T(8,128)}, u32[]{:S(2)}) copy-start(s32[8,8]{1,0:T(8,128)} %param.19) | copy-start | bytes 772
  69.5 12.5 %all-to-all-start = ((f32[8,8,128]{2,1,0:T(8,128)}), f32[8,8,128]{2,1,0:T(8,128)S(1)}, u32[]{:S(2)}, u32[]{:S(2)}) async-start(f32[8,8,128]{2,1,0:T(8,128)} %shard_map.135.unused), calls=%async_computation | async-start | bytes 65536 | tf_op jit(solution)/shard_map/all_to_all | solution.py:728
  85.2 10.8 %all-to-all-start.1 = ((f16[32,16,128]{2,1,0:T(8,128)(2,1)}), f16[32,16,128]{2,1,0:T(8,128)(2,1)S(1)}, u32[]{:S(2)}, u32[]{:S(2)}) async-start(f16[32,16,128]{2,1,0:T(8,128)(2,1)} %convert_element_type.10), calls=%async_computation.1 | async-start | bytes 262144 | tf_op jit(solution)/shard_map/all_to_all | solution.py:750

commit v2 on v1

--- a/solution.py
+++ b/solution.py
@@ -55,25 +55,6 @@
 def turn(v, shift):
     shift %= LANES
     return v if shift == 0 else pltpu.roll(v, shift, 1)
-
-
-def x_pattern(lane, a):
-    out = jnp.zeros((8, LANES), F32)
-    for cx in (1, -1):
-        for cy in (-1, 0, 1):
-            for cz in (-1, 0, 1):
-                b, base = x_place(cx, cy, cz)
-                if b == a:
-                    out = jnp.where(lane // 16 == base // 16, WEIGHT[pop(cx, cy, cz)], out)
-    return out
-
-
-def y_pattern(lane):
-    out = jnp.zeros((8, LANES), F32)
-    for cx in (-1, 0, 1):
-        for cz in (-1, 0, 1):
-            out = jnp.where(lane % 16 == y_slot(cx, cz), WEIGHT[pop(cx, 1, cz)], out)
-    return out
 
 
 def moments(f):
@@ -96,7 +77,7 @@
     full = {cx: rows[cx] + s[cx, 0] for cx in (-1, 0, 1)}
     dsum = {cx: d[cx, -1] + d[cx, 0] + d[cx, 1] for cx in (-1, 0, 1)}
     sxx = full[-1] + full[1]
-    rho = sxx + full[0]
+    rho = 1.0 + (sxx + full[0])
     jx = full[1] - full[-1]
     ydif = {cx: s[cx, 1] - s[cx, -1] for cx in (-1, 0, 1)}
     jy = ydif[-1] + ydif[0] + ydif[1]
@@ -119,7 +100,7 @@
     qx, qy, qz = 4.5 * (pxx - third), 4.5 * (pyy - third), 4.5 * (pzz - third)
     qxy, qxz, qyz = 9.0 * pxy, 9.0 * pxz, 9.0 * pyz
     base = 1.0 - 1.5 * (ux * ux + uy * uy + uz * uz)
-    rest = rho * base
+    rest = rho * base - 1.0
     rho3 = 3.0 * rho
     rho45 = 4.5 * rho
     cross = None
@@ -170,23 +151,29 @@
     return star, (rho, ux, uy, uz)
 
 
-def pack(star, flag, lane, patterns):
-    group = lane // 16
-    slot = lane % 16
-    xs = [jnp.zeros((8, LANES), F32) for _ in range(3)]
+def pack_pair(m, star_ref, flag_ref, xp_out, yp_out, ym_out):
+    source = pl.ds(pl.multiple_of(16 * m + 8, 8), 16)
+    target = pl.ds(pl.multiple_of(16 * m, 16), 16)
+    lane = lax.broadcasted_iota(jnp.int32, (16, LANES), 1)
+    group = (lane // 16).astype(F32).astype(HALO_TYPE)
+    slot = (lane % 16).astype(F32).astype(HALO_TYPE)
+    star = [star_ref[i, source, :].astype(HALO_TYPE) for i in range(27)]
+    flag = None if flag_ref is None else flag_ref[source, :].astype(HALO_TYPE)
+    xs = [jnp.zeros((16, LANES), HALO_TYPE) for _ in range(3)]
     for cx in (1, -1):
-        source = 112 if cx > 0 else 0
+        edge = 112 if cx > 0 else 0
         for cy in (-1, 0, 1):
             for cz in (-1, 0, 1):
                 a, base = x_place(cx, cy, cz)
-                xs[a] = jnp.where(group == base // 16, turn(star[pop(cx, cy, cz)], base - source), xs[a])
+                xs[a] = jnp.where(group == base // 16, turn(star[pop(cx, cy, cz)], base - edge), xs[a])
         if flag is not None:
             a, base = x_flag_place(cx)
-            xs[a] = jnp.where(group == base // 16, turn(flag, base - source), xs[a])
-    ys = []
-    for cy in (1, -1):
+            xs[a] = jnp.where(group == base // 16, turn(flag, base - edge), xs[a])
+    for a in range(3):
+        xp_out[a, target, :] = xs[a]
+    for cy, out in ((1, yp_out), (-1, ym_out)):
         edge = 15 if cy > 0 else 0
-        acc = jnp.zeros((8, LANES), F32)
+        acc = jnp.zeros((16, LANES), HALO_TYPE)
         for cx in (-1, 0, 1):
             for cz in (-1, 0, 1):
                 j = y_slot(cx, cz)
@@ -194,8 +181,7 @@
             if flag is not None:
                 j = y_flag_slot(cx)
                 acc = jnp.where(slot == j, turn(flag, 16 * cx + j - edge), acc)
-        ys.append(acc)
-    return [v - p for v, p in zip(xs + ys, patterns)]
+        out[target, :] = acc
 
 
 FOLD = 48
@@ -219,11 +205,6 @@
     for k in range(1, HALO_ROWS // FOLD):
         out = jnp.where(lane // 32 == k, turn(lines[k * FOLD : (k + 1) * FOLD], 32 * k), out)
     return out
-
-
-def all_patterns(lane):
-    yp = y_pattern(lane)
-    return [x_pattern(lane, 0), x_pattern(lane, 1), x_pattern(lane, 2), yp, yp]
 
 
 def initial_kernel(perturb_hbm, density_hbm, velocity_hbm, excitation_hbm, solid_hbm, f_out, lo_out, hi_out, s_out,
@@ -265,24 +246,11 @@
             shape = shape + 3.0 * cu + 4.5 * (cu * cu)
         if i % 3 == 0:
             chunks[i // 3].wait()
-        v = (WEIGHT[i] * rho) * shape * (1.0 + amplitude * perturb[i])
+        v = WEIGHT[i] * (rho * shape * (1.0 + amplitude * perturb[i]) - 1.0)
         put(i, v.T, f_out.at[i])
 
 
-def pack_tile(t, star_ref, flag_ref, lane, patterns, x_tmp, y_tmp):
-    at = pl.ds(pl.multiple_of(8 * t, 8), 8)
-    flag = None if flag_ref is None else flag_ref[at, :]
-    packed = pack([star_ref[i, at, :] for i in range(27)], flag, lane, patterns)
-    row = pl.ds(pl.multiple_of(8 * t - 8, 8), 8)
-    for a in range(3):
-        x_tmp[a, row, :] = packed[a]
-    y_tmp[0, row, :] = packed[3]
-    y_tmp[1, row, :] = packed[4]
-
-
-def first_kernel(f_in, s_in, lo, hi, unused, star_out, s_out, xp_out, yp_out, ym_out, xc_out, edge, x_tmp, y_tmp):
-    lane = lane_iota()
-    patterns = all_patterns(lane)
+def first_kernel(f_in, s_in, lo, hi, unused, star_out, s_out, xp_out, yp_out, ym_out, xc_out, edge):
     for i in range(28):
         below = lo[4 * i : 4 * i + 4, :]
         above = hi[4 * i : 4 * i + 4, :]
@@ -299,8 +267,8 @@
             star_out[i, at, :] = star[i]
         s_out[at, :] = load(27)
 
-    def pack_at(t):
-        pack_tile(t, star_out, s_out, lane, patterns, x_tmp, y_tmp)
+    def pack_at(m):
+        pack_pair(m, star_out, s_out, xp_out, yp_out, ym_out)
 
     def outer(k, carry):
         at = pl.ds(pl.multiple_of(8 * k, 8), 8)
@@ -308,20 +276,17 @@
         return carry
 
     def inner(k, carry):
-        t = k + 2
-        pack_at(t - 1)
-        at = pl.ds(pl.multiple_of(8 * t, 8), 8)
-        emit(t, lambda i: s_in[at, :] if i == 27 else f_in[i, at, :])
+        pack_at(jnp.maximum(k - 1, 0))
+        for t in (2 * k + 2, 2 * k + 3):
+            at = pl.ds(pl.multiple_of(8 * t, 8), 8)
+            emit(t, lambda i: s_in[at, :] if i == 27 else f_in[i, at, :])
         return carry
 
     lax.fori_loop(0, 2, outer, 0)
-    lax.fori_loop(0, 16, inner, 0)
-    pack_at(17)
-    pack_at(18)
-    xp_out[...] = x_tmp[...].astype(xp_out.dtype)
-    yp_out[...] = y_tmp[0].astype(yp_out.dtype)
-    ym_out[...] = y_tmp[1].astype(ym_out.dtype)
-    xc_out[...] = corners(y_tmp[0], y_tmp[1]).astype(xc_out.dtype)
+    lax.fori_loop(0, 8, inner, 0)
+    pack_at(7)
+    pack_at(8)
+    xc_out[...] = corners(yp_out[...].astype(F32), ym_out[...].astype(F32)).astype(xc_out.dtype)
 
 
 def patch_kernel(low, high, yp_in, ym_in, yp_out, ym_out):
@@ -351,17 +316,13 @@
         wall_ref = s_in
     xs, ys = refs[:2]
     lane = lane_iota()
-    patterns = all_patterns(lane)
     slot = lane % 16
     halo = pl.ds(8, HALO_ROWS)
 
-    def tall(v):
-        return jnp.concatenate([v] * TILES, axis=0)
-
     for a in range(3):
-        xs[a, halo, :] = xh[a].astype(F32) + tall(patterns[a])
-    ys[0, halo, :] = yph[...].astype(F32) + tall(patterns[3])
-    ys[1, halo, :] = ymh[...].astype(F32) + tall(patterns[4])
+        xs[a, halo, :] = xh[a].astype(F32)
+    ys[0, halo, :] = yph[...].astype(F32)
+    ys[1, halo, :] = ymh[...].astype(F32)
     edge_rows = (pl.ds(0, 8), pl.ds(ROWS - 8, 8))
     for at in edge_rows:
         for a in range(3):
@@ -427,32 +388,25 @@
         for a, v in enumerate(macro):
             mom_out[a, row, :] = v
 
-    if not last:
-        xs_next, ys_next = refs[2:4]
-        refs = refs[2:]
     even, odd = refs[2:4]
 
-    def pack_at(t):
+    def pack_at(m):
         if not last:
-            pack_tile(t, star_out, None, lane, patterns, xs_next, ys_next)
+            pack_pair(m, star_out, None, xp_out, yp_out, ym_out)
 
     def body(m, carry):
-        pack_at(jnp.maximum(2 * m, 1))
         collide_tile(2 * m + 1, even)
         gather_tile(2 * m + 2, odd)
-        pack_at(2 * m + 1)
+        pack_at(jnp.maximum(m - 1, 0))
         collide_tile(2 * m + 2, odd)
         gather_tile(jnp.minimum(2 * m + 3, TILES), even)
         return carry
 
     gather_tile(1, even)
     lax.fori_loop(0, TILES // 2, body, 0)
-    pack_at(TILES)
+    pack_at(TILES // 2 - 1)
     if not last:
-        xp_out[...] = xs_next[...].astype(xp_out.dtype)
-        yp_out[...] = ys_next[0].astype(yp_out.dtype)
-        ym_out[...] = ys_next[1].astype(ym_out.dtype)
-        xc_out[...] = corners(ys_next[0], ys_next[1]).astype(xc_out.dtype)
+        xc_out[...] = corners(yp_out[...].astype(F32), ym_out[...].astype(F32)).astype(xc_out.dtype)
 
 
 def prepare_kernel(capacity, owner_row, owner_col, cell, placing_out, lane_out, row_out):
@@ -530,7 +484,7 @@
         velocity_out[a] = jnp.where(wall, 0.0, mom[a + 1, 8:136, :].T)
 
 
-def observe_kernel(groups, capacity, ptile, weights_hbm, near, offset, rec, out_hbm, rest, out, sem):
+def observe_kernel(groups, capacity, ptile, weights_hbm, near, offset, rec, out, rest, sem):
     ahead = near.shape[0]
     copy = pltpu.make_async_copy(weights_hbm.at[pl.ds(ahead, 4 - ahead)], rest, sem.at[0])
     copy.start()
@@ -561,7 +515,6 @@
     devices = out.shape[0]
     count = obs // devices
     obs_tile = obs // offset.shape[1]
-    stores = []
     for h in range(2):
         acc = None
         for k in range(4):
@@ -585,11 +538,6 @@
             out[d, 0:tiles, :] = piece * down
             o = start // obs_tile
             out[d, tiles : 2 * tiles, :] = jnp.where(lane < 64, jnp.broadcast_to(offset[:, o : o + 1], (tiles, LANES)), power)
-        half = pl.ds(h * (devices // 2), devices // 2)
-        stores.append(pltpu.make_async_copy(out.at[half], out_hbm.at[half], sem.at[1 + h]))
-        stores[h].start()
-    for store in stores:
-        store.wait()
 
 
 def signal_kernel(got, out):
@@ -663,8 +611,6 @@
     x_face = jax.ShapeDtypeStruct((3, HALO_ROWS, LANES), HALO_TYPE)
     y_face = jax.ShapeDtypeStruct((HALO_ROWS, LANES), HALO_TYPE)
     x_edge = jax.ShapeDtypeStruct((FOLD, LANES), HALO_TYPE)
-    x_scratch = pltpu.VMEM((3, HALO_ROWS, LANES), F32)
-    y_scratch = pltpu.VMEM((2, HALO_ROWS, LANES), F32)
 
     f0, low_rim, high_rim, flags = call(
         initial_kernel, (block, rim, rim, one),
@@ -689,7 +635,7 @@
 
     star, walls, xp, yp, ym, xc = call(
         first_kernel, (block, one, x_face, y_face, y_face, x_edge), f0, flags, below, above, placing,
-        scratch=(pltpu.VMEM((28, 16, LANES), F32), x_scratch, y_scratch))
+        scratch=(pltpu.VMEM((28, 16, LANES), F32),))
 
     mom_shape = jax.ShapeDtypeStruct((4, HALO_ROWS, LANES), F32)
     routed = []
@@ -702,8 +648,6 @@
         if first:
             outs += [jax.ShapeDtypeStruct((9, ROWS, LANES), F32)]
         scratch = [pltpu.VMEM((3, ROWS, LANES), F32), pltpu.VMEM((2, ROWS, LANES), F32)]
-        if not last:
-            scratch += [x_scratch, y_scratch]
         scratch += [pltpu.VMEM((27, 8, LANES), F32)] * 2
         res = call(functools.partial(step_kernel, first, last), tuple(outs), star, walls, xh, yph, ymh,
                    routed[-1] if routed else placing, scratch=scratch)
@@ -738,9 +682,9 @@
         functools.partial(observe_kernel, group_count, capacity, row_count // tiles),
         out_shape=jax.ShapeDtypeStruct(out_shape, F32),
         in_specs=[pl.BlockSpec(memory_space=pltpu.HBM)] + [pl.BlockSpec(memory_space=pltpu.VMEM)] * 3,
-        out_specs=pl.BlockSpec(memory_space=pltpu.HBM),
-        scratch_shapes=[pltpu.VMEM((4 - near.shape[0],) + weights.shape[1:], weights.dtype), pltpu.VMEM(out_shape, F32),
-                        pltpu.SemaphoreType.DMA((3,))],
+        out_specs=pl.BlockSpec(memory_space=pltpu.VMEM),
+        scratch_shapes=[pltpu.VMEM((4 - near.shape[0],) + weights.shape[1:], weights.dtype),
+                        pltpu.SemaphoreType.DMA((1,))],
         compiler_params=pltpu.CompilerParams(vmem_limit_bytes=24 << 20),
     )(pltpu.with_memory_space_constraint(weights, pltpu.HBM), near, bin_offset.astype(F32), received)
     final_density, final_velocity = call(

time: 97.6 us -> 96.4 us (0.988)
  Pallas kernels: 29.7 us -> 28.5 us
where the time goes in v2:
time: 96.4 us; the launch traced here: 95.8 us
  starting transfers between devices  34.8 us (36%)
  waiting for transfers between devices  30.2 us (31%)
  Pallas kernels  28.5 us (30%)
    pallas_call x18, Pallas kernels, call(): pl.pallas_call(kernel, out_shape=outs, in_specs=[pl.BlockSpec(memory_spac...  26.5 us
    ppermute x16, starting transfers between devices, shift(): return lax.ppermute(value, axis, ring(axis, by))  24 us
    ppermute x16, waiting for transfers between devices, shift(): return lax.ppermute(value, axis, ring(axis, by))  19.2 us
    all_to_all x1, waiting for transfers between devices, shards(): lax.all_to_all(observed.astype(jnp.float16), ('gx', 'gy', 'gz'), split_ax...  5.78 us
    all_to_all x1, starting transfers between devices, shards(): lax.all_to_all(sent, ('gx', 'gy'), split_axis=0, concat_axis=0, tiled=True)  5.77 us
    all_to_all x1, waiting for transfers between devices, shards(): lax.all_to_all(sent, ('gx', 'gy'), split_axis=0, concat_axis=0, tiled=True)  4.03 us
    all_to_all x1, starting transfers between devices, shards(): lax.all_to_all(observed.astype(jnp.float16), ('gx', 'gy', 'gz'), split_ax...  2.56 us
    ppermute x1, starting transfers between devices, shards(): above = lax.ppermute(low_rim, 'gz', ring('gz', -1))  2.01 us
  transfers between devices with their start and end apart: 20, of which 13 were waited for; matrix products, arithmetic and copies ran while one was open for 1% of the time, Pallas kernels for 7%

profile of v2, /device:TPU:0, one launch (start us, length us, event | category | flops | bytes accessed | tf_op | source)
XLA Modules:
  0.0 95.8 jit_solution(3637981136402748236)
XLA Ops:
  0.7 3.1 %shard_map.121 = (f32[27,160,128]{2,1,0:T(8,128)S(1)}, f32[112,128]{1,0:T(8,128)S(1)}, f32[112,128]{1,0:T(8,128)S(1)}, f32[160,128]{1,0:T(8,128)S(1)}) custom-call(f32[27,128,128]{2,1,0:T(8,128)} %bitcast.13, f32[128,128]{1,0:T(8,128)} %bitcast.17, f32[3,128,128]{2,1,0:T(8,128)} %bitcast.16, f32[128,128]{1,0:T(8,128)} %bitcast.18, s32[128,128]{1,0:T(8,128)} %bitcast.14), custom_call_target="tpu_custom_call" | custom-call | flops 1000000 | bytes 2162688 | tf_op jit(solution)/shard_map/pallas_call | solution.py:566
  3.7 0.5 collective-permute-start
  4.3 2.0 %collective-permute-start.1 = (f32[112,128]{1,0:T(8,128)S(1)}, f32[112,128]{1,0:T(8,128)S(1)}, u32[]{:S(2)}, u32[]{:S(2)}) collective-permute-start(f32[112,128]{1,0:T(8,128)S(1)} %get-tuple-element.48), channel_id=1, source_target_pairs={{0,3},{1,0},{2,1},{3,2},{4,7},{5,4},{6,5},{7,6},{8,11},{9,8},{10,9... | collective-permute-start | bytes 172040 | tf_op jit(solution)/shard_map/ppermute | solution.py:623
  6.3 0.8 copy.13.owner_col
  7.3 0.7 collective-permute-done.lo
  8.1 0.4 collective-permute-done.1.hi
  8.5 2.1 %shard_map.123 = (f32[27,160,128]{2,1,0:T(8,128)S(1)}, f32[160,128]{1,0:T(8,128)S(1)}, bf16[3,144,128]{2,1,0:T(8,128)(2,1)S(1)}, bf16[144,128]{1,0:T(8,128)(2,1)...) custom-call(f32[27,160,128]{2,1,0:T(8,128)S(1)} %get-tuple-element.45.f_in, ...), custom_call_target="tpu_custom_call" | custom-call | flops 1000000 | bytes 2670592 | tf_op jit(solution)/shard_map/pallas_call | solution.py:566
  10.7 1.9 %collective-permute-start.2 = (bf16[3,144,128]{2,1,0:T(8,128)(2,1)S(1)}, bf16[3,144,128]{2,1,0:T(8,128)(2,1)S(1)}, u32[]{:S(2)}, u32[]{:S(2)}) collective-permute-start(bf16[3,144,128]{2,1,0:T(8,128)(2,1)S(1)} %get-tuple-element.52), channel_id=1, source_target_pairs={{0,16},{16,0},{1,17},{17,1},{2,18},{18,2},{3,19},{19,3},{4,20},{20... | collective-permute-start | bytes 331784 | tf_op jit(solution)/shard_map/ppermute | solution.py:585
  12.7 3.6 %collective-permute-done.3.low.high = bf16[48,128]{1,0:T(8,128)(2,1)S(1)} collective-permute-done((bf16[48,128]{1,0:T(8,128)(2,1)S(1)}, bf16[48,128]{1,0:T(8,128)(2,1)S(1)}, u32[]{:S(2)}, u32[]{:S(2)}) %collective-permute-start.3) | collective-permute-done | bytes 12320 | tf_op jit(solution)/shard_map/ppermute | solution.py:585
  16.5 1.8 %collective-permute-start.4 = (bf16[144,128]{1,0:T(8,128)(2,1)S(1)}, bf16[144,128]{1,0:T(8,128)(2,1)S(1)}, u32[]{:S(2)}, u32[]{:S(2)}) collective-permute-start(bf16[144,128]{1,0:T(8,128)(2,1)S(1)} %get-tuple-element.56), channel_id=1, source_target_pairs={{0,4},{4,8},{8,12},{12,0},{1,5},{5,9},{9,13},{13,1},{2,6},{6,10},{... | collective-permute-start | bytes 110600 | tf_op jit(solution)/shard_map/ppermute | solution.py:585
  18.3 2.1 %collective-permute-start.5 = (bf16[144,128]{1,0:T(8,128)(2,1)S(1)}, bf16[144,128]{1,0:T(8,128)(2,1)S(1)}, u32[]{:S(2)}, u32[]{:S(2)}) collective-permute-start(bf16[144,128]{1,0:T(8,128)(2,1)S(1)} %get-tuple-element.57), channel_id=1, source_target_pairs={{0,12},{4,0},{8,4},{12,8},{1,13},{5,1},{9,5},{13,9},{2,14},{6,2},{... | collective-permute-start | bytes 110600 | tf_op jit(solution)/shard_map/ppermute | solution.py:585
  20.4 2.1 %collective-permute-done.4.refs_3_ = bf16[144,128]{1,0:T(8,128)(2,1)S(1)} collective-permute-done((bf16[144,128]{1,0:T(8,128)(2,1)S(1)}, bf16[144,128]{1,0:T(8,128)(2,1)S(1)}, u32[]{:S(2)}, u32[]{:S(2)}) %collective-permute-start.4) | collective-permute-done | bytes 36896 | tf_op jit(solution)/shard_map/ppermute | solution.py:585
  22.5 0.3 collective-permute-done.5.refs_4_
  22.9 3.7 %shard_map.125 = (f32[4,144,128]{2,1,0:T(8,128)S(1)}, f32[27,160,128]{2,1,0:T(8,128)S(1)}, bf16[3,144,128]{2,1,0:T(8,128)(2,1)S(1)}, bf16[144,128]{1,0:T(8,128)(...) custom-call(f32[27,160,128]{2,1,0:T(8,128)S(1)} %get-tuple-element.50.refs_0_, ...), custom_call_target="tpu_custom_call" | custom-call | flops 1000000 | bytes 2740224 | tf_op jit(solution)/shard_map/pallas_call | solution.py:566
  26.6 1.5 %collective-permute-start.6 = (bf16[3,144,128]{2,1,0:T(8,128)(2,1)S(1)}, bf16[3,144,128]{2,1,0:T(8,128)(2,1)S(1)}, u32[]{:S(2)}, u32[]{:S(2)}) collective-permute-start(bf16[3,144,128]{2,1,0:T(8,128)(2,1)S(1)} %get-tuple-element.60), channel_id=1, source_target_pairs={{0,16},{16,0},{1,17},{17,1},{2,18},{18,2},{3,19},{19,3},{4,20},{20... | collective-permute-start | bytes 331784 | tf_op jit(solution)/shard_map/ppermute | solution.py:585
  28.1 0.5 collective-permute-start.7
  28.6 3.2 %collective-permute-done.7.low.high = bf16[48,128]{1,0:T(8,128)(2,1)S(1)} collective-permute-done((bf16[48,128]{1,0:T(8,128)(2,1)S(1)}, bf16[48,128]{1,0:T(8,128)(2,1)S(1)}, u32[]{:S(2)}, u32[]{:S(2)}) %collective-permute-start.7) | collective-permute-done | bytes 12320 | tf_op jit(solution)/shard_map/ppermute | solution.py:585
  31.9 1.0 %collective-permute-start.8 = (bf16[144,128]{1,0:T(8,128)(2,1)S(1)}, bf16[144,128]{1,0:T(8,128)(2,1)S(1)}, u32[]{:S(2)}, u32[]{:S(2)}) collective-permute-start(bf16[144,128]{1,0:T(8,128)(2,1)S(1)} %get-tuple-element.64), channel_id=1, source_target_pairs={{0,4},{4,8},{8,12},{12,0},{1,5},{5,9},{9,13},{13,1},{2,6},{6,10},{... | collective-permute-start | bytes 110600 | tf_op jit(solution)/shard_map/ppermute | solution.py:585
  32.9 2.8 %collective-permute-start.9 = (bf16[144,128]{1,0:T(8,128)(2,1)S(1)}, bf16[144,128]{1,0:T(8,128)(2,1)S(1)}, u32[]{:S(2)}, u32[]{:S(2)}) collective-permute-start(bf16[144,128]{1,0:T(8,128)(2,1)S(1)} %get-tuple-element.65), channel_id=1, source_target_pairs={{0,12},{4,0},{8,4},{12,8},{1,13},{5,1},{9,5},{13,9},{2,14},{6,2},{... | collective-permute-start | bytes 110600 | tf_op jit(solution)/shard_map/ppermute | solution.py:585
  35.8 0.5 shard_map.127.refs_5_.part0
  36.2 1.5 %collective-permute-done.8.refs_3_ = bf16[144,128]{1,0:T(8,128)(2,1)S(1)} collective-permute-done((bf16[144,128]{1,0:T(8,128)(2,1)S(1)}, bf16[144,128]{1,0:T(8,128)(2,1)S(1)}, u32[]{:S(2)}, u32[]{:S(2)}) %collective-permute-start.8) | collective-permute-done | bytes 36896 | tf_op jit(solution)/shard_map/ppermute | solution.py:585
  37.7 3.1 %shard_map.128 = (f32[4,144,128]{2,1,0:T(8,128)S(1)}, f32[27,160,128]{2,1,0:T(8,128)S(1)}, bf16[3,144,128]{2,1,0:T(8,128)(2,1)S(1)}, bf16[144,128]{1,0:T(8,128)(...) custom-call(f32[27,160,128]{2,1,0:T(8,128)S(1)} %get-tuple-element.58.refs_0_, ...), custom_call_target="tpu_custom_call" | custom-call | flops 1000000 | bytes 3149824 | tf_op jit(solution)/shard_map/pallas_call | solution.py:566
  40.8 1.2 %collective-permute-start.10 = (bf16[3,144,128]{2,1,0:T(8,128)(2,1)S(1)}, bf16[3,144,128]{2,1,0:T(8,128)(2,1)S(1)}, u32[]{:S(2)}, u32[]{:S(2)}) collective-permute-start(bf16[3,144,128]{2,1,0:T(8,128)(2,1)S(1)} %get-tuple-element.70), channel_id=1, source_target_pairs={{0,16},{16,0},{1,17},{17,1},{2,18},{18,2},{3,19},{19,3},{4,20},{20... | collective-permute-start | bytes 331784 | tf_op jit(solution)/shard_map/ppermute | solution.py:585
  42.1 0.8 collective-permute-start.11
  42.9 2.9 %collective-permute-done.11.low.high = bf16[48,128]{1,0:T(8,128)(2,1)S(1)} collective-permute-done((bf16[48,128]{1,0:T(8,128)(2,1)S(1)}, bf16[48,128]{1,0:T(8,128)(2,1)S(1)}, u32[]{:S(2)}, u32[]{:S(2)}) %collective-permute-start.11) | collective-permute-done | bytes 12320 | tf_op jit(solution)/shard_map/ppermute | solution.py:585
  45.9 1.0 %collective-permute-start.12 = (bf16[144,128]{1,0:T(8,128)(2,1)S(1)}, bf16[144,128]{1,0:T(8,128)(2,1)S(1)}, u32[]{:S(2)}, u32[]{:S(2)}) collective-permute-start(bf16[144,128]{1,0:T(8,128)(2,1)S(1)} %get-tuple-element.74), channel_id=1, source_target_pairs={{0,4},{4,8},{8,12},{12,0},{1,5},{5,9},{9,13},{13,1},{2,6},{6,10},{... | collective-permute-start | bytes 110600 | tf_op jit(solution)/shard_map/ppermute | solution.py:585
  46.9 2.9 %collective-permute-start.13 = (bf16[144,128]{1,0:T(8,128)(2,1)S(1)}, bf16[144,128]{1,0:T(8,128)(2,1)S(1)}, u32[]{:S(2)}, u32[]{:S(2)}) collective-permute-start(bf16[144,128]{1,0:T(8,128)(2,1)S(1)} %get-tuple-element.75), channel_id=1, source_target_pairs={{0,12},{4,0},{8,4},{12,8},{1,13},{5,1},{9,5},{13,9},{2,14},{6,2},{... | collective-permute-start | bytes 110600 | tf_op jit(solution)/shard_map/ppermute | solution.py:585
  49.8 0.5 shard_map.130.refs_5_.part1
  50.3 1.4 %collective-permute-done.12.refs_3_ = bf16[144,128]{1,0:T(8,128)(2,1)S(1)} collective-permute-done((bf16[144,128]{1,0:T(8,128)(2,1)S(1)}, bf16[144,128]{1,0:T(8,128)(2,1)S(1)}, u32[]{:S(2)}, u32[]{:S(2)}) %collective-permute-start.12) | collective-permute-done | bytes 36896 | tf_op jit(solution)/shard_map/ppermute | solution.py:585
  51.7 3.1 %shard_map.131 = (f32[4,144,128]{2,1,0:T(8,128)S(1)}, f32[27,160,128]{2,1,0:T(8,128)S(1)}, bf16[3,144,128]{2,1,0:T(8,128)(2,1)S(1)}, bf16[144,128]{1,0:T(8,128)(...) custom-call(f32[27,160,128]{2,1,0:T(8,128)S(1)} %get-tuple-element.69.refs_0_, ...), custom_call_target="tpu_custom_call" | custom-call | flops 1000000 | bytes 3149824 | tf_op jit(solution)/shard_map/pallas_call | solution.py:566
  54.8 1.2 %collective-permute-start.14 = (bf16[3,144,128]{2,1,0:T(8,128)(2,1)S(1)}, bf16[3,144,128]{2,1,0:T(8,128)(2,1)S(1)}, u32[]{:S(2)}, u32[]{:S(2)}) collective-permute-start(bf16[3,144,128]{2,1,0:T(8,128)(2,1)S(1)} %get-tuple-element.78), channel_id=1, source_target_pairs={{0,16},{16,0},{1,17},{17,1},{2,18},{18,2},{3,19},{19,3},{4,20},{20... | collective-permute-start | bytes 331784 | tf_op jit(solution)/shard_map/ppermute | solution.py:585
  56.0 0.8 collective-permute-start.15
  56.9 2.9 %collective-permute-done.15.low.high = bf16[48,128]{1,0:T(8,128)(2,1)S(1)} collective-permute-done((bf16[48,128]{1,0:T(8,128)(2,1)S(1)}, bf16[48,128]{1,0:T(8,128)(2,1)S(1)}, u32[]{:S(2)}, u32[]{:S(2)}) %collective-permute-start.15) | collective-permute-done | bytes 12320 | tf_op jit(solution)/shard_map/ppermute | solution.py:585
  59.8 1.2 %collective-permute-start.16 = (bf16[144,128]{1,0:T(8,128)(2,1)S(1)}, bf16[144,128]{1,0:T(8,128)(2,1)S(1)}, u32[]{:S(2)}, u32[]{:S(2)}) collective-permute-start(bf16[144,128]{1,0:T(8,128)(2,1)S(1)} %get-tuple-element.82), channel_id=1, source_target_pairs={{0,4},{4,8},{8,12},{12,0},{1,5},{5,9},{9,13},{13,1},{2,6},{6,10},{... | collective-permute-start | bytes 110600 | tf_op jit(solution)/shard_map/ppermute | solution.py:585
  61.0 2.8 %collective-permute-start.17 = (bf16[144,128]{1,0:T(8,128)(2,1)S(1)}, bf16[144,128]{1,0:T(8,128)(2,1)S(1)}, u32[]{:S(2)}, u32[]{:S(2)}) collective-permute-start(bf16[144,128]{1,0:T(8,128)(2,1)S(1)} %get-tuple-element.83), channel_id=1, source_target_pairs={{0,12},{4,0},{8,4},{12,8},{1,13},{5,1},{9,5},{13,9},{2,14},{6,2},{... | collective-permute-start | bytes 110600 | tf_op jit(solution)/shard_map/ppermute | solution.py:585
  63.8 0.5 shard_map.133.refs_5_.part2
  64.3 1.4 %collective-permute-done.16.refs_3_ = bf16[144,128]{1,0:T(8,128)(2,1)S(1)} collective-permute-done((bf16[144,128]{1,0:T(8,128)(2,1)S(1)}, bf16[144,128]{1,0:T(8,128)(2,1)S(1)}, u32[]{:S(2)}, u32[]{:S(2)}) %collective-permute-start.16) | collective-permute-done | bytes 36896 | tf_op jit(solution)/shard_map/ppermute | solution.py:585
  65.7 2.0 %shard_map.134.mom = f32[4,144,128]{2,1,0:T(8,128)S(1)} custom-call(f32[27,160,128]{2,1,0:T(8,128)S(1)} %get-tuple-element.77.refs_0_, f32[9,160,128]{2,1,0:T(8,128)S(1)} %get-tuple-element.59.refs_1_, bf16[3,144,128]{2,1,0:T(8,128)(2,1)S(1)} %collective-permute-done.14.refs_2_, bf16[144,128]{1,0:T(8,128)(2,1)S(1)} %collective-permute-done.16.refs_3_, ...), custom_call_target="tpu_custom_call" | custom-call | flops 1000000 | bytes 3149824 | tf_op jit(solution)/shard_map/pallas_call | solution.py:566
  67.7 1.2 %shard_map.135.unused = f32[8,8,128]{2,1,0:T(8,128)} custom-call(f32[4,144,128]{2,1,0:T(8,128)S(1)} %shard_map.134.mom, bf16[128,256]{1,0:T(8,128)(2,1)S(1)} %get-tuple-element.67.refs_1_.lane_hot, f32[128,256]{1,0:T(8,128)S(1)} %get-tuple-element.68.refs_2_.row_hot, f32[3,256]{1,0:T(4,128)S(1)} %copy-done, ...), custom_call_target="tpu_custom_call" | custom-call | flops 1000000 | bytes 805888 | tf_op jit(solution)/shard_map/pallas_call | solution.py:566
  68.9 5.8 %all-to-all-start = ((f32[8,8,128]{2,1,0:T(8,128)}), f32[8,8,128]{2,1,0:T(8,128)S(1)}, u32[]{:S(2)}, u32[]{:S(2)}) async-start(f32[8,8,128]{2,1,0:T(8,128)} %shard_map.135.unused), calls=%async_computation | async-start | bytes 65536 | tf_op jit(solution)/shard_map/all_to_all | solution.py:672
  74.6 2.7 %shard_map.137.near = bf16[3,512,1024]{2,1,0:T(8,128)(2,1)S(1)} custom-call(bf16[4,512,1024]{2,1,0:T(8,128)(2,1)} %weights_hbm.3, f32[8,8,128]{2,1,0:T(8,128)} %shard_map.135.unused), custom_call_target="tpu_custom_call" | custom-call | flops 1000000 | bytes 4227072 | tf_op jit(solution)/shard_map/pallas_call | solution.py:566
  77.3 4.0 %all-to-all-done.rec = f32[8,8,128]{2,1,0:T(8,128)S(1)} async-done(((f32[8,8,128]{2,1,0:T(8,128)}), f32[8,8,128]{2,1,0:T(8,128)S(1)}, u32[]{:S(2)}, u32[]{:S(2)}) %all-to-all-start) | async-done | bytes 32800 | tf_op jit(solution)/shard_map/all_to_all | solution.py:672
  81.4 2.0 %shard_map.138 = f32[32,16,128]{2,1,0:T(8,128)S(1)} custom-call(bf16[4,512,1024]{2,1,0:T(8,128)(2,1)} %weights_hbm.3, bf16[3,512,1024]{2,1,0:T(8,128)(2,1)S(1)} %shard_map.137.near, f32[8,8]{1,0:T(8,128)S(1)} %convert_element_type.9.offset, f32[8,8,128]{2,1,0:T(8,128)S(1)} %all-to-all-done.rec), custom_call_target="tpu_custom_call" | custom-call | tf_op jit(solution)/shard_map/pallas_call | solution.py:681
  83.3 0.7 convert_element_type.10
  84.0 2.6 %all-to-all-start.1 = ((f16[32,16,128]{2,1,0:T(8,128)(2,1)}), f16[32,16,128]{2,1,0:T(8,128)(2,1)S(1)}, u32[]{:S(2)}, u32[]{:S(2)}) async-start(f16[32,16,128]{2,1,0:T(8,128)(2,1)} %convert_element_type.10), calls=%async_computation.1 | async-start | bytes 262144 | tf_op jit(solution)/shard_map/all_to_all | solution.py:694
  86.6 2.4 %shard_map.136 = (f32[128,128]{1,0:T(8,128)}, f32[3,128,128]{2,1,0:T(8,128)}) custom-call(s32[128,128]{1,0:T(8,128)} %bitcast.15, f32[4,144,128]{2,1,0:T(8,128)S(1)} %shard_map.134.mom, f32[8,8,128]{2,1,0:T(8,128)} %shard_map.135.unused), custom_call_target="tpu_custom_call" | custom-call | flops 1000000 | bytes 393216 | tf_op jit(solution)/shard_map/pallas_call | solution.py:566
  89.0 5.8 %all-to-all-done.1 = f16[32,16,128]{2,1,0:T(8,128)(2,1)S(1)} async-done(((f16[32,16,128]{2,1,0:T(8,128)(2,1)}), f16[32,16,128]{2,1,0:T(8,128)(2,1)S(1)}, u32[]{:S(2)}, u32[]{:S(2)}) %all-to-all-start.1) | async-done | bytes 131104 | tf_op jit(solution)/shard_map/all_to_all | solution.py:694
  94.8 1.0 %shard_map.139 = f32[32,128]{1,0:T(8,128)} custom-call(f32[32,16,128]{2,1,0:T(8,128)S(1)} %convert_element_type.11.got), custom_call_target="tpu_custom_call" | custom-call | flops 1000000 | bytes 262144 | tf_op jit(solution)/shard_map/pallas_call | solution.py:566
  (23 shorter events, 0.9 us)
Async XLA Ops:
  0.6 6.5 %copy-start.1 = (s32[256]{0:T(256)S(1)}, s32[256]{0:T(256)}, u32[]{:S(2)}) copy-start(s32[256]{0:T(256)} %param.16) | copy-start | bytes 3076
  0.6 6.5 %copy-start.2 = (s32[256]{0:T(256)S(1)}, s32[256]{0:T(256)}, u32[]{:S(2)}) copy-start(s32[256]{0:T(256)} %param.15) | copy-start | bytes 3076
  3.7 4.3 %collective-permute-start = (f32[112,128]{1,0:T(8,128)S(1)}, f32[112,128]{1,0:T(8,128)S(1)}, u32[]{:S(2)}, u32[]{:S(2)}) collective-permute-start(f32[112,128]{1,0:T(8,128)S(1)} %get-tuple-element.47), channel_id=1, source_target_pairs={{0,1},{1,2},{2,3},{3,0},{4,5},{5,6},{6,7},{7,4},{8,9},{9,10},{10,1... | collective-permute-start | bytes 172040 | tf_op jit(solution)/shard_map/ppermute | solution.py:622
  4.3 4.2 %collective-permute-start.1 = (f32[112,128]{1,0:T(8,128)S(1)}, f32[112,128]{1,0:T(8,128)S(1)}, u32[]{:S(2)}, u32[]{:S(2)}) collective-permute-start(f32[112,128]{1,0:T(8,128)S(1)} %get-tuple-element.48), channel_id=1, source_target_pairs={{0,3},{1,0},{2,1},{3,2},{4,7},{5,4},{6,5},{7,6},{8,11},{9,8},{10,9... | collective-permute-start | bytes 172040 | tf_op jit(solution)/shard_map/ppermute | solution.py:623
  8.5 27.2 %copy-start = (f32[3,256]{1,0:T(4,128)S(1)}, f32[3,256]{1,0:T(4,128)}, u32[]{:S(2)}) copy-start(f32[3,256]{1,0:T(4,128)} %area.1) | copy-start | bytes 9220
  10.7 12.2 %collective-permute-start.2 = (bf16[3,144,128]{2,1,0:T(8,128)(2,1)S(1)}, bf16[3,144,128]{2,1,0:T(8,128)(2,1)S(1)}, u32[]{:S(2)}, u32[]{:S(2)}) collective-permute-start(bf16[3,144,128]{2,1,0:T(8,128)(2,1)S(1)} %get-tuple-element.52), channel_id=1, source_target_pairs={{0,16},{16,0},{1,17},{17,1},{2,18},{18,2},{3,19},{19,3},{4,20},{20... | collective-permute-start | bytes 331784 | tf_op jit(solution)/shard_map/ppermute | solution.py:585
  12.5 3.8 %collective-permute-start.3 = (bf16[48,128]{1,0:T(8,128)(2,1)S(1)}, bf16[48,128]{1,0:T(8,128)(2,1)S(1)}, u32[]{:S(2)}, u32[]{:S(2)}) collective-permute-start(bf16[48,128]{1,0:T(8,128)(2,1)S(1)} %get-tuple-element.53), channel_id=1, source_target_pairs={{0,16},{16,0},{1,17},{17,1},{2,18},{18,2},{3,19},{19,3},{4,20},{20... | collective-permute-start | bytes 36872 | tf_op jit(solution)/shard_map/ppermute | solution.py:585
  16.5 6.1 %collective-permute-start.4 = (bf16[144,128]{1,0:T(8,128)(2,1)S(1)}, bf16[144,128]{1,0:T(8,128)(2,1)S(1)}, u32[]{:S(2)}, u32[]{:S(2)}) collective-permute-start(bf16[144,128]{1,0:T(8,128)(2,1)S(1)} %get-tuple-element.56), channel_id=1, source_target_pairs={{0,4},{4,8},{8,12},{12,0},{1,5},{5,9},{9,13},{13,1},{2,6},{6,10},{... | collective-permute-start | bytes 110600 | tf_op jit(solution)/shard_map/ppermute | solution.py:585
  18.3 4.5 %collective-permute-start.5 = (bf16[144,128]{1,0:T(8,128)(2,1)S(1)}, bf16[144,128]{1,0:T(8,128)(2,1)S(1)}, u32[]{:S(2)}, u32[]{:S(2)}) collective-permute-start(bf16[144,128]{1,0:T(8,128)(2,1)S(1)} %get-tuple-element.57), channel_id=1, source_target_pairs={{0,12},{4,0},{8,4},{12,8},{1,13},{5,1},{9,5},{13,9},{2,14},{6,2},{... | collective-permute-start | bytes 110600 | tf_op jit(solution)/shard_map/ppermute | solution.py:585
  26.6 11.2 %collective-permute-start.6 = (bf16[3,144,128]{2,1,0:T(8,128)(2,1)S(1)}, bf16[3,144,128]{2,1,0:T(8,128)(2,1)S(1)}, u32[]{:S(2)}, u32[]{:S(2)}) collective-permute-start(bf16[3,144,128]{2,1,0:T(8,128)(2,1)S(1)} %get-tuple-element.60), channel_id=1, source_target_pairs={{0,16},{16,0},{1,17},{17,1},{2,18},{18,2},{3,19},{19,3},{4,20},{20... | collective-permute-start | bytes 331784 | tf_op jit(solution)/shard_map/ppermute | solution.py:585
  28.1 3.7 %collective-permute-start.7 = (bf16[48,128]{1,0:T(8,128)(2,1)S(1)}, bf16[48,128]{1,0:T(8,128)(2,1)S(1)}, u32[]{:S(2)}, u32[]{:S(2)}) collective-permute-start(bf16[48,128]{1,0:T(8,128)(2,1)S(1)} %get-tuple-element.61), channel_id=1, source_target_pairs={{0,16},{16,0},{1,17},{17,1},{2,18},{18,2},{3,19},{19,3},{4,20},{20... | collective-permute-start | bytes 36872 | tf_op jit(solution)/shard_map/ppermute | solution.py:585
  31.9 5.8 %collective-permute-start.8 = (bf16[144,128]{1,0:T(8,128)(2,1)S(1)}, bf16[144,128]{1,0:T(8,128)(2,1)S(1)}, u32[]{:S(2)}, u32[]{:S(2)}) collective-permute-start(bf16[144,128]{1,0:T(8,128)(2,1)S(1)} %get-tuple-element.64), channel_id=1, source_target_pairs={{0,4},{4,8},{8,12},{12,0},{1,5},{5,9},{9,13},{13,1},{2,6},{6,10},{... | collective-permute-start | bytes 110600 | tf_op jit(solution)/shard_map/ppermute | solution.py:585
  32.9 4.8 %collective-permute-start.9 = (bf16[144,128]{1,0:T(8,128)(2,1)S(1)}, bf16[144,128]{1,0:T(8,128)(2,1)S(1)}, u32[]{:S(2)}, u32[]{:S(2)}) collective-permute-start(bf16[144,128]{1,0:T(8,128)(2,1)S(1)} %get-tuple-element.65), channel_id=1, source_target_pairs={{0,12},{4,0},{8,4},{12,8},{1,13},{5,1},{9,5},{13,9},{2,14},{6,2},{... | collective-permute-start | bytes 110600 | tf_op jit(solution)/shard_map/ppermute | solution.py:585
  40.8 10.8 %collective-permute-start.10 = (bf16[3,144,128]{2,1,0:T(8,128)(2,1)S(1)}, bf16[3,144,128]{2,1,0:T(8,128)(2,1)S(1)}, u32[]{:S(2)}, u32[]{:S(2)}) collective-permute-start(bf16[3,144,128]{2,1,0:T(8,128)(2,1)S(1)} %get-tuple-element.70), channel_id=1, source_target_pairs={{0,16},{16,0},{1,17},{17,1},{2,18},{18,2},{3,19},{19,3},{4,20},{20... | collective-permute-start | bytes 331784 | tf_op jit(solution)/shard_map/ppermute | solution.py:585
  42.1 3.7 %collective-permute-start.11 = (bf16[48,128]{1,0:T(8,128)(2,1)S(1)}, bf16[48,128]{1,0:T(8,128)(2,1)S(1)}, u32[]{:S(2)}, u32[]{:S(2)}) collective-permute-start(bf16[48,128]{1,0:T(8,128)(2,1)S(1)} %get-tuple-element.71), channel_id=1, source_target_pairs={{0,16},{16,0},{1,17},{17,1},{2,18},{18,2},{3,19},{19,3},{4,20},{20... | collective-permute-start | bytes 36872 | tf_op jit(solution)/shard_map/ppermute | solution.py:585
  45.9 5.8 %collective-permute-start.12 = (bf16[144,128]{1,0:T(8,128)(2,1)S(1)}, bf16[144,128]{1,0:T(8,128)(2,1)S(1)}, u32[]{:S(2)}, u32[]{:S(2)}) collective-permute-start(bf16[144,128]{1,0:T(8,128)(2,1)S(1)} %get-tuple-element.74), channel_id=1, source_target_pairs={{0,4},{4,8},{8,12},{12,0},{1,5},{5,9},{9,13},{13,1},{2,6},{6,10},{... | collective-permute-start | bytes 110600 | tf_op jit(solution)/shard_map/ppermute | solution.py:585
  46.9 4.8 %collective-permute-start.13 = (bf16[144,128]{1,0:T(8,128)(2,1)S(1)}, bf16[144,128]{1,0:T(8,128)(2,1)S(1)}, u32[]{:S(2)}, u32[]{:S(2)}) collective-permute-start(bf16[144,128]{1,0:T(8,128)(2,1)S(1)} %get-tuple-element.75), channel_id=1, source_target_pairs={{0,12},{4,0},{8,4},{12,8},{1,13},{5,1},{9,5},{13,9},{2,14},{6,2},{... | collective-permute-start | bytes 110600 | tf_op jit(solution)/shard_map/ppermute | solution.py:585
  54.8 10.9 %collective-permute-start.14 = (bf16[3,144,128]{2,1,0:T(8,128)(2,1)S(1)}, bf16[3,144,128]{2,1,0:T(8,128)(2,1)S(1)}, u32[]{:S(2)}, u32[]{:S(2)}) collective-permute-start(bf16[3,144,128]{2,1,0:T(8,128)(2,1)S(1)} %get-tuple-element.78), channel_id=1, source_target_pairs={{0,16},{16,0},{1,17},{17,1},{2,18},{18,2},{3,19},{19,3},{4,20},{20... | collective-permute-start | bytes 331784 | tf_op jit(solution)/shard_map/ppermute | solution.py:585
  56.0 3.7 %collective-permute-start.15 = (bf16[48,128]{1,0:T(8,128)(2,1)S(1)}, bf16[48,128]{1,0:T(8,128)(2,1)S(1)}, u32[]{:S(2)}, u32[]{:S(2)}) collective-permute-start(bf16[48,128]{1,0:T(8,128)(2,1)S(1)} %get-tuple-element.79), channel_id=1, source_target_pairs={{0,16},{16,0},{1,17},{17,1},{2,18},{18,2},{3,19},{19,3},{4,20},{20... | collective-permute-start | bytes 36872 | tf_op jit(solution)/shard_map/ppermute | solution.py:585
  59.8 5.9 %collective-permute-start.16 = (bf16[144,128]{1,0:T(8,128)(2,1)S(1)}, bf16[144,128]{1,0:T(8,128)(2,1)S(1)}, u32[]{:S(2)}, u32[]{:S(2)}) collective-permute-start(bf16[144,128]{1,0:T(8,128)(2,1)S(1)} %get-tuple-element.82), channel_id=1, source_target_pairs={{0,4},{4,8},{8,12},{12,0},{1,5},{5,9},{9,13},{13,1},{2,6},{6,10},{... | collective-permute-start | bytes 110600 | tf_op jit(solution)/shard_map/ppermute | solution.py:585
  61.0 4.7 %collective-permute-start.17 = (bf16[144,128]{1,0:T(8,128)(2,1)S(1)}, bf16[144,128]{1,0:T(8,128)(2,1)S(1)}, u32[]{:S(2)}, u32[]{:S(2)}) collective-permute-start(bf16[144,128]{1,0:T(8,128)(2,1)S(1)} %get-tuple-element.83), channel_id=1, source_target_pairs={{0,12},{4,0},{8,4},{12,8},{1,13},{5,1},{9,5},{13,9},{2,14},{6,2},{... | collective-permute-start | bytes 110600 | tf_op jit(solution)/shard_map/ppermute | solution.py:585
  64.3 10.3 %copy-start.3 = (s32[8,8]{1,0:T(8,128)S(1)}, s32[8,8]{1,0:T(8,128)}, u32[]{:S(2)}) copy-start(s32[8,8]{1,0:T(8,128)} %param.19) | copy-start | bytes 772
  68.9 12.5 %all-to-all-start = ((f32[8,8,128]{2,1,0:T(8,128)}), f32[8,8,128]{2,1,0:T(8,128)S(1)}, u32[]{:S(2)}, u32[]{:S(2)}) async-start(f32[8,8,128]{2,1,0:T(8,128)} %shard_map.135.unused), calls=%async_computation | async-start | bytes 65536 | tf_op jit(solution)/shard_map/all_to_all | solution.py:672
  84.0 10.8 %all-to-all-start.1 = ((f16[32,16,128]{2,1,0:T(8,128)(2,1)}), f16[32,16,128]{2,1,0:T(8,128)(2,1)S(1)}, u32[]{:S(2)}, u32[]{:S(2)}) async-start(f16[32,16,128]{2,1,0:T(8,128)(2,1)} %convert_element_type.10), calls=%async_computation.1 | async-start | bytes 262144 | tf_op jit(solution)/shard_map/all_to_all | solution.py:694

commit v3 on v2

--- a/solution.py
+++ b/solution.py
@@ -208,7 +208,7 @@
 
 
 def initial_kernel(perturb_hbm, density_hbm, velocity_hbm, excitation_hbm, solid_hbm, f_out, lo_out, hi_out, s_out,
-                   perturb, density, velocity, excitation, solid, chunk_sem, sem):
+                   perturb, density, velocity, excitation, solid, lo_tmp, hi_tmp, chunk_sem, sem):
     small = [
         pltpu.make_async_copy(src, dst, sem.at[k])
         for k, (src, dst) in enumerate(((density_hbm, density), (velocity_hbm, velocity),
@@ -231,8 +231,8 @@
 
     def put(i, v, out):
         out[FIRST : FIRST + 128, :] = v
-        lo_out[4 * i : 4 * i + 4, :] = v[0:4, :]
-        hi_out[4 * i : 4 * i + 4, :] = v[124:128, :]
+        lo_tmp[4 * i : 4 * i + 4, :] = v[0:4, :]
+        hi_tmp[4 * i : 4 * i + 4, :] = v[124:128, :]
 
     put(27, solid[...].astype(F32).T, s_out)
     for i in range(27):
@@ -248,12 +248,16 @@
             chunks[i // 3].wait()
         v = WEIGHT[i] * (rho * shape * (1.0 + amplitude * perturb[i]) - 1.0)
         put(i, v.T, f_out.at[i])
-
-
-def first_kernel(f_in, s_in, lo, hi, unused, star_out, s_out, xp_out, yp_out, ym_out, xc_out, edge):
+    lo_out[...] = lo_tmp[...].astype(lo_out.dtype)
+    hi_out[...] = hi_tmp[...].astype(hi_out.dtype)
+
+
+def first_kernel(f_in, s_in, lo, hi, unused, star_out, s_out, xp_out, yp_out, ym_out, xc_out, edge, lo_tmp, hi_tmp):
+    lo_tmp[...] = lo[...].astype(F32)
+    hi_tmp[...] = hi[...].astype(F32)
     for i in range(28):
-        below = lo[4 * i : 4 * i + 4, :]
-        above = hi[4 * i : 4 * i + 4, :]
+        below = lo_tmp[4 * i : 4 * i + 4, :]
+        above = hi_tmp[4 * i : 4 * i + 4, :]
         edge[i, 0:4, :] = below
         edge[i, 4:8, :] = below
         edge[i, 8:12, :] = above
@@ -607,7 +611,7 @@
     solid = solid_flag.reshape(flat)
     block = jax.ShapeDtypeStruct((27, ROWS, LANES), F32)
     one = jax.ShapeDtypeStruct((ROWS, LANES), F32)
-    rim = jax.ShapeDtypeStruct((28 * 4, LANES), F32)
+    rim = jax.ShapeDtypeStruct((28 * 4, LANES), HALO_TYPE)
     x_face = jax.ShapeDtypeStruct((3, HALO_ROWS, LANES), HALO_TYPE)
     y_face = jax.ShapeDtypeStruct((HALO_ROWS, LANES), HALO_TYPE)
     x_edge = jax.ShapeDtypeStruct((FOLD, LANES), HALO_TYPE)
@@ -618,7 +622,7 @@
         excitation.reshape(flat), solid,
         far=range(5),
         scratch=(pltpu.VMEM((27,) + flat, F32), pltpu.VMEM(flat, F32), pltpu.VMEM((3,) + flat, F32), pltpu.VMEM(flat, F32),
-                 pltpu.VMEM(flat, jnp.int32), pltpu.SemaphoreType.DMA((9,)), pltpu.SemaphoreType.DMA((4,))))
+                 pltpu.VMEM(flat, jnp.int32), pltpu.VMEM((112, LANES), F32), pltpu.VMEM((112, LANES), F32), pltpu.SemaphoreType.DMA((9,)), pltpu.SemaphoreType.DMA((4,))))
     below = lax.ppermute(high_rim, "gz", ring("gz", 1))
     above = lax.ppermute(low_rim, "gz", ring("gz", -1))
 
@@ -635,7 +639,7 @@
 
     star, walls, xp, yp, ym, xc = call(
         first_kernel, (block, one, x_face, y_face, y_face, x_edge), f0, flags, below, above, placing,
-        scratch=(pltpu.VMEM((28, 16, LANES), F32),))
+        scratch=(pltpu.VMEM((28, 16, LANES), F32), pltpu.VMEM((112, LANES), F32), pltpu.VMEM((112, LANES), F32)))
 
     mom_shape = jax.ShapeDtypeStruct((4, HALO_ROWS, LANES), F32)
     routed = []

time: 96.4 us -> 96.1 us (level)
  no operation moved by 1% of the time
where the time goes in v3:
time: 96.1 us; the launch traced here: 95.6 us
  starting transfers between devices  35.1 us (37%)
  waiting for transfers between devices  29.7 us (31%)
  Pallas kernels  28.5 us (30%)
    pallas_call x18, Pallas kernels, call(): pl.pallas_call(kernel, out_shape=outs, in_specs=[pl.BlockSpec(memory_spac...  26.5 us
    ppermute x16, starting transfers between devices, shift(): return lax.ppermute(value, axis, ring(axis, by))  24.2 us
    ppermute x16, waiting for transfers between devices, shift(): return lax.ppermute(value, axis, ring(axis, by))  19.3 us
    all_to_all x1, waiting for transfers between devices, shards(): lax.all_to_all(observed.astype(jnp.float16), ('gx', 'gy', 'gz'), split_ax...  5.78 us
    all_to_all x1, starting transfers between devices, shards(): lax.all_to_all(sent, ('gx', 'gy'), split_axis=0, concat_axis=0, tiled=True)  5.77 us
    all_to_all x1, waiting for transfers between devices, shards(): lax.all_to_all(sent, ('gx', 'gy'), split_axis=0, concat_axis=0, tiled=True)  4.03 us
    all_to_all x1, starting transfers between devices, shards(): lax.all_to_all(observed.astype(jnp.float16), ('gx', 'gy', 'gz'), split_ax...  2.56 us
    ppermute x1, starting transfers between devices, shards(): above = lax.ppermute(low_rim, 'gz', ring('gz', -1))  2.01 us
  transfers between devices with their start and end apart: 20, of which 13 were waited for; matrix products, arithmetic and copies ran while one was open for 1% of the time, Pallas kernels for 7%

profile of v3, /device:TPU:0, one launch (start us, length us, event | category | flops | bytes accessed | tf_op | source)
XLA Modules:
  0.0 95.6 jit_solution(11882088418508725485)
XLA Ops:
  0.7 3.1 %shard_map.121 = (f32[27,160,128]{2,1,0:T(8,128)S(1)}, bf16[112,128]{1,0:T(8,128)(2,1)S(1)}, bf16[112,128]{1,0:T(8,128)(2,1)S(1)}, f32[160,128]{1,0:T(8,128)S(1)}) custom-call(f32[27,128,128]{2,1,0:T(8,128)} %bitcast.13, f32[128,128]{1,0:T(8,128)} %bitcast.17, f32[3,128,128]{2,1,0:T(8,128)} %bitcast.16, f32[128,128]{1,0:T(8,128)} %bitcast.18, ...), custom_call_target="tpu_custom_call" | custom-call | flops 1000000 | bytes 2162688 | tf_op jit(solution)/shard_map/pallas_call | solution.py:570
  3.8 0.5 collective-permute-start
  4.3 2.0 %collective-permute-start.1 = (bf16[112,128]{1,0:T(8,128)(2,1)S(1)}, bf16[112,128]{1,0:T(8,128)(2,1)S(1)}, u32[]{:S(2)}, u32[]{:S(2)}) collective-permute-start(bf16[112,128]{1,0:T(8,128)(2,1)S(1)} %get-tuple-element.48), channel_id=1, source_target_pairs={{0,3},{1,0},{2,1},{3,2},{4,7},{5,4},{6,5},{7,6},{8,11},{9,8},{10,9... | collective-permute-start | bytes 86024 | tf_op jit(solution)/shard_map/ppermute | solution.py:627
  6.3 0.8 copy.13.owner_col
  7.1 0.2 shard_map.122
  7.4 0.4 collective-permute-done.lo
  7.9 2.1 %shard_map.123 = (f32[27,160,128]{2,1,0:T(8,128)S(1)}, f32[160,128]{1,0:T(8,128)S(1)}, bf16[3,144,128]{2,1,0:T(8,128)(2,1)S(1)}, bf16[144,128]{1,0:T(8,128)(2,1)...) custom-call(f32[27,160,128]{2,1,0:T(8,128)S(1)} %get-tuple-element.45.f_in, ...), custom_call_target="tpu_custom_call" | custom-call | flops 1000000 | bytes 2613248 | tf_op jit(solution)/shard_map/pallas_call | solution.py:570
  10.1 2.2 %collective-permute-start.2 = (bf16[3,144,128]{2,1,0:T(8,128)(2,1)S(1)}, bf16[3,144,128]{2,1,0:T(8,128)(2,1)S(1)}, u32[]{:S(2)}, u32[]{:S(2)}) collective-permute-start(bf16[3,144,128]{2,1,0:T(8,128)(2,1)S(1)} %get-tuple-element.52), channel_id=1, source_target_pairs={{0,16},{16,0},{1,17},{17,1},{2,18},{18,2},{3,19},{19,3},{4,20},{20... | collective-permute-start | bytes 331784 | tf_op jit(solution)/shard_map/ppermute | solution.py:589
  12.3 3.7 %collective-permute-done.3.low.high = bf16[48,128]{1,0:T(8,128)(2,1)S(1)} collective-permute-done((bf16[48,128]{1,0:T(8,128)(2,1)S(1)}, bf16[48,128]{1,0:T(8,128)(2,1)S(1)}, u32[]{:S(2)}, u32[]{:S(2)}) %collective-permute-start.3) | collective-permute-done | bytes 12320 | tf_op jit(solution)/shard_map/ppermute | solution.py:589
  16.2 1.9 %collective-permute-start.4 = (bf16[144,128]{1,0:T(8,128)(2,1)S(1)}, bf16[144,128]{1,0:T(8,128)(2,1)S(1)}, u32[]{:S(2)}, u32[]{:S(2)}) collective-permute-start(bf16[144,128]{1,0:T(8,128)(2,1)S(1)} %get-tuple-element.56), channel_id=1, source_target_pairs={{0,4},{4,8},{8,12},{12,0},{1,5},{5,9},{9,13},{13,1},{2,6},{6,10},{... | collective-permute-start | bytes 110600 | tf_op jit(solution)/shard_map/ppermute | solution.py:589
  18.0 2.1 %collective-permute-start.5 = (bf16[144,128]{1,0:T(8,128)(2,1)S(1)}, bf16[144,128]{1,0:T(8,128)(2,1)S(1)}, u32[]{:S(2)}, u32[]{:S(2)}) collective-permute-start(bf16[144,128]{1,0:T(8,128)(2,1)S(1)} %get-tuple-element.57), channel_id=1, source_target_pairs={{0,12},{4,0},{8,4},{12,8},{1,13},{5,1},{9,5},{13,9},{2,14},{6,2},{... | collective-permute-start | bytes 110600 | tf_op jit(solution)/shard_map/ppermute | solution.py:589
  20.1 2.1 %collective-permute-done.4.refs_3_ = bf16[144,128]{1,0:T(8,128)(2,1)S(1)} collective-permute-done((bf16[144,128]{1,0:T(8,128)(2,1)S(1)}, bf16[144,128]{1,0:T(8,128)(2,1)S(1)}, u32[]{:S(2)}, u32[]{:S(2)}) %collective-permute-start.4) | collective-permute-done | bytes 36896 | tf_op jit(solution)/shard_map/ppermute | solution.py:589
  22.2 0.3 collective-permute-done.5.refs_4_
  22.6 3.7 %shard_map.125 = (f32[4,144,128]{2,1,0:T(8,128)S(1)}, f32[27,160,128]{2,1,0:T(8,128)S(1)}, bf16[3,144,128]{2,1,0:T(8,128)(2,1)S(1)}, bf16[144,128]{1,0:T(8,128)(...) custom-call(f32[27,160,128]{2,1,0:T(8,128)S(1)} %get-tuple-element.50.refs_0_, ...), custom_call_target="tpu_custom_call" | custom-call | flops 1000000 | bytes 2740224 | tf_op jit(solution)/shard_map/pallas_call | solution.py:570
  26.3 1.5 %collective-permute-start.6 = (bf16[3,144,128]{2,1,0:T(8,128)(2,1)S(1)}, bf16[3,144,128]{2,1,0:T(8,128)(2,1)S(1)}, u32[]{:S(2)}, u32[]{:S(2)}) collective-permute-start(bf16[3,144,128]{2,1,0:T(8,128)(2,1)S(1)} %get-tuple-element.60), channel_id=1, source_target_pairs={{0,16},{16,0},{1,17},{17,1},{2,18},{18,2},{3,19},{19,3},{4,20},{20... | collective-permute-start | bytes 331784 | tf_op jit(solution)/shard_map/ppermute | solution.py:589
  27.8 0.5 collective-permute-start.7
  28.3 3.2 %collective-permute-done.7.low.high = bf16[48,128]{1,0:T(8,128)(2,1)S(1)} collective-permute-done((bf16[48,128]{1,0:T(8,128)(2,1)S(1)}, bf16[48,128]{1,0:T(8,128)(2,1)S(1)}, u32[]{:S(2)}, u32[]{:S(2)}) %collective-permute-start.7) | collective-permute-done | bytes 12320 | tf_op jit(solution)/shard_map/ppermute | solution.py:589
  31.6 1.0 %collective-permute-start.8 = (bf16[144,128]{1,0:T(8,128)(2,1)S(1)}, bf16[144,128]{1,0:T(8,128)(2,1)S(1)}, u32[]{:S(2)}, u32[]{:S(2)}) collective-permute-start(bf16[144,128]{1,0:T(8,128)(2,1)S(1)} %get-tuple-element.64), channel_id=1, source_target_pairs={{0,4},{4,8},{8,12},{12,0},{1,5},{5,9},{9,13},{13,1},{2,6},{6,10},{... | collective-permute-start | bytes 110600 | tf_op jit(solution)/shard_map/ppermute | solution.py:589
  32.6 2.8 %collective-permute-start.9 = (bf16[144,128]{1,0:T(8,128)(2,1)S(1)}, bf16[144,128]{1,0:T(8,128)(2,1)S(1)}, u32[]{:S(2)}, u32[]{:S(2)}) collective-permute-start(bf16[144,128]{1,0:T(8,128)(2,1)S(1)} %get-tuple-element.65), channel_id=1, source_target_pairs={{0,12},{4,0},{8,4},{12,8},{1,13},{5,1},{9,5},{13,9},{2,14},{6,2},{... | collective-permute-start | bytes 110600 | tf_op jit(solution)/shard_map/ppermute | solution.py:589
  35.5 0.5 shard_map.127.refs_5_.part0
  36.0 1.5 %collective-permute-done.8.refs_3_ = bf16[144,128]{1,0:T(8,128)(2,1)S(1)} collective-permute-done((bf16[144,128]{1,0:T(8,128)(2,1)S(1)}, bf16[144,128]{1,0:T(8,128)(2,1)S(1)}, u32[]{:S(2)}, u32[]{:S(2)}) %collective-permute-start.8) | collective-permute-done | bytes 36896 | tf_op jit(solution)/shard_map/ppermute | solution.py:589
  37.4 3.1 %shard_map.128 = (f32[4,144,128]{2,1,0:T(8,128)S(1)}, f32[27,160,128]{2,1,0:T(8,128)S(1)}, bf16[3,144,128]{2,1,0:T(8,128)(2,1)S(1)}, bf16[144,128]{1,0:T(8,128)(...) custom-call(f32[27,160,128]{2,1,0:T(8,128)S(1)} %get-tuple-element.58.refs_0_, ...), custom_call_target="tpu_custom_call" | custom-call | flops 1000000 | bytes 3149824 | tf_op jit(solution)/shard_map/pallas_call | solution.py:570
  40.6 1.2 %collective-permute-start.10 = (bf16[3,144,128]{2,1,0:T(8,128)(2,1)S(1)}, bf16[3,144,128]{2,1,0:T(8,128)(2,1)S(1)}, u32[]{:S(2)}, u32[]{:S(2)}) collective-permute-start(bf16[3,144,128]{2,1,0:T(8,128)(2,1)S(1)} %get-tuple-element.70), channel_id=1, source_target_pairs={{0,16},{16,0},{1,17},{17,1},{2,18},{18,2},{3,19},{19,3},{4,20},{20... | collective-permute-start | bytes 331784 | tf_op jit(solution)/shard_map/ppermute | solution.py:589
  41.8 0.8 collective-permute-start.11
  42.6 2.9 %collective-permute-done.11.low.high = bf16[48,128]{1,0:T(8,128)(2,1)S(1)} collective-permute-done((bf16[48,128]{1,0:T(8,128)(2,1)S(1)}, bf16[48,128]{1,0:T(8,128)(2,1)S(1)}, u32[]{:S(2)}, u32[]{:S(2)}) %collective-permute-start.11) | collective-permute-done | bytes 12320 | tf_op jit(solution)/shard_map/ppermute | solution.py:589
  45.6 1.0 %collective-permute-start.12 = (bf16[144,128]{1,0:T(8,128)(2,1)S(1)}, bf16[144,128]{1,0:T(8,128)(2,1)S(1)}, u32[]{:S(2)}, u32[]{:S(2)}) collective-permute-start(bf16[144,128]{1,0:T(8,128)(2,1)S(1)} %get-tuple-element.74), channel_id=1, source_target_pairs={{0,4},{4,8},{8,12},{12,0},{1,5},{5,9},{9,13},{13,1},{2,6},{6,10},{... | collective-permute-start | bytes 110600 | tf_op jit(solution)/shard_map/ppermute | solution.py:589
  46.6 2.9 %collective-permute-start.13 = (bf16[144,128]{1,0:T(8,128)(2,1)S(1)}, bf16[144,128]{1,0:T(8,128)(2,1)S(1)}, u32[]{:S(2)}, u32[]{:S(2)}) collective-permute-start(bf16[144,128]{1,0:T(8,128)(2,1)S(1)} %get-tuple-element.75), channel_id=1, source_target_pairs={{0,12},{4,0},{8,4},{12,8},{1,13},{5,1},{9,5},{13,9},{2,14},{6,2},{... | collective-permute-start | bytes 110600 | tf_op jit(solution)/shard_map/ppermute | solution.py:589
  49.5 0.5 shard_map.130.refs_5_.part1
  50.0 1.4 %collective-permute-done.12.refs_3_ = bf16[144,128]{1,0:T(8,128)(2,1)S(1)} collective-permute-done((bf16[144,128]{1,0:T(8,128)(2,1)S(1)}, bf16[144,128]{1,0:T(8,128)(2,1)S(1)}, u32[]{:S(2)}, u32[]{:S(2)}) %collective-permute-start.12) | collective-permute-done | bytes 36896 | tf_op jit(solution)/shard_map/ppermute | solution.py:589
  51.4 3.1 %shard_map.131 = (f32[4,144,128]{2,1,0:T(8,128)S(1)}, f32[27,160,128]{2,1,0:T(8,128)S(1)}, bf16[3,144,128]{2,1,0:T(8,128)(2,1)S(1)}, bf16[144,128]{1,0:T(8,128)(...) custom-call(f32[27,160,128]{2,1,0:T(8,128)S(1)} %get-tuple-element.69.refs_0_, ...), custom_call_target="tpu_custom_call" | custom-call | flops 1000000 | bytes 3149824 | tf_op jit(solution)/shard_map/pallas_call | solution.py:570
  54.5 1.2 %collective-permute-start.14 = (bf16[3,144,128]{2,1,0:T(8,128)(2,1)S(1)}, bf16[3,144,128]{2,1,0:T(8,128)(2,1)S(1)}, u32[]{:S(2)}, u32[]{:S(2)}) collective-permute-start(bf16[3,144,128]{2,1,0:T(8,128)(2,1)S(1)} %get-tuple-element.78), channel_id=1, source_target_pairs={{0,16},{16,0},{1,17},{17,1},{2,18},{18,2},{3,19},{19,3},{4,20},{20... | collective-permute-start | bytes 331784 | tf_op jit(solution)/shard_map/ppermute | solution.py:589
  55.7 0.8 collective-permute-start.15
  56.6 2.9 %collective-permute-done.15.low.high = bf16[48,128]{1,0:T(8,128)(2,1)S(1)} collective-permute-done((bf16[48,128]{1,0:T(8,128)(2,1)S(1)}, bf16[48,128]{1,0:T(8,128)(2,1)S(1)}, u32[]{:S(2)}, u32[]{:S(2)}) %collective-permute-start.15) | collective-permute-done | bytes 12320 | tf_op jit(solution)/shard_map/ppermute | solution.py:589
  59.5 1.2 %collective-permute-start.16 = (bf16[144,128]{1,0:T(8,128)(2,1)S(1)}, bf16[144,128]{1,0:T(8,128)(2,1)S(1)}, u32[]{:S(2)}, u32[]{:S(2)}) collective-permute-start(bf16[144,128]{1,0:T(8,128)(2,1)S(1)} %get-tuple-element.82), channel_id=1, source_target_pairs={{0,4},{4,8},{8,12},{12,0},{1,5},{5,9},{9,13},{13,1},{2,6},{6,10},{... | collective-permute-start | bytes 110600 | tf_op jit(solution)/shard_map/ppermute | solution.py:589
  60.7 2.8 %collective-permute-start.17 = (bf16[144,128]{1,0:T(8,128)(2,1)S(1)}, bf16[144,128]{1,0:T(8,128)(2,1)S(1)}, u32[]{:S(2)}, u32[]{:S(2)}) collective-permute-start(bf16[144,128]{1,0:T(8,128)(2,1)S(1)} %get-tuple-element.83), channel_id=1, source_target_pairs={{0,12},{4,0},{8,4},{12,8},{1,13},{5,1},{9,5},{13,9},{2,14},{6,2},{... | collective-permute-start | bytes 110600 | tf_op jit(solution)/shard_map/ppermute | solution.py:589
  63.5 0.5 shard_map.133.refs_5_.part2
  64.0 1.4 %collective-permute-done.16.refs_3_ = bf16[144,128]{1,0:T(8,128)(2,1)S(1)} collective-permute-done((bf16[144,128]{1,0:T(8,128)(2,1)S(1)}, bf16[144,128]{1,0:T(8,128)(2,1)S(1)}, u32[]{:S(2)}, u32[]{:S(2)}) %collective-permute-start.16) | collective-permute-done | bytes 36896 | tf_op jit(solution)/shard_map/ppermute | solution.py:589
  65.4 2.0 %shard_map.134.mom = f32[4,144,128]{2,1,0:T(8,128)S(1)} custom-call(f32[27,160,128]{2,1,0:T(8,128)S(1)} %get-tuple-element.77.refs_0_, f32[9,160,128]{2,1,0:T(8,128)S(1)} %get-tuple-element.59.refs_1_, bf16[3,144,128]{2,1,0:T(8,128)(2,1)S(1)} %collective-permute-done.14.refs_2_, bf16[144,128]{1,0:T(8,128)(2,1)S(1)} %collective-permute-done.16.refs_3_, ...), custom_call_target="tpu_custom_call" | custom-call | flops 1000000 | bytes 3149824 | tf_op jit(solution)/shard_map/pallas_call | solution.py:570
  67.4 1.2 %shard_map.135.unused = f32[8,8,128]{2,1,0:T(8,128)} custom-call(f32[4,144,128]{2,1,0:T(8,128)S(1)} %shard_map.134.mom, bf16[128,256]{1,0:T(8,128)(2,1)S(1)} %get-tuple-element.67.refs_1_.lane_hot, f32[128,256]{1,0:T(8,128)S(1)} %get-tuple-element.68.refs_2_.row_hot, f32[3,256]{1,0:T(4,128)S(1)} %copy-done, ...), custom_call_target="tpu_custom_call" | custom-call | flops 1000000 | bytes 805888 | tf_op jit(solution)/shard_map/pallas_call | solution.py:570
  68.6 5.8 %all-to-all-start = ((f32[8,8,128]{2,1,0:T(8,128)}), f32[8,8,128]{2,1,0:T(8,128)S(1)}, u32[]{:S(2)}, u32[]{:S(2)}) async-start(f32[8,8,128]{2,1,0:T(8,128)} %shard_map.135.unused), calls=%async_computation | async-start | bytes 65536 | tf_op jit(solution)/shard_map/all_to_all | solution.py:676
  74.4 2.7 %shard_map.137.near = bf16[3,512,1024]{2,1,0:T(8,128)(2,1)S(1)} custom-call(bf16[4,512,1024]{2,1,0:T(8,128)(2,1)} %weights_hbm.3, f32[8,8,128]{2,1,0:T(8,128)} %shard_map.135.unused), custom_call_target="tpu_custom_call" | custom-call | flops 1000000 | bytes 4227072 | tf_op jit(solution)/shard_map/pallas_call | solution.py:570
  77.0 4.0 %all-to-all-done.rec = f32[8,8,128]{2,1,0:T(8,128)S(1)} async-done(((f32[8,8,128]{2,1,0:T(8,128)}), f32[8,8,128]{2,1,0:T(8,128)S(1)}, u32[]{:S(2)}, u32[]{:S(2)}) %all-to-all-start) | async-done | bytes 32800 | tf_op jit(solution)/shard_map/all_to_all | solution.py:676
  81.1 2.0 %shard_map.138 = f32[32,16,128]{2,1,0:T(8,128)S(1)} custom-call(bf16[4,512,1024]{2,1,0:T(8,128)(2,1)} %weights_hbm.3, bf16[3,512,1024]{2,1,0:T(8,128)(2,1)S(1)} %shard_map.137.near, f32[8,8]{1,0:T(8,128)S(1)} %convert_element_type.9.offset, f32[8,8,128]{2,1,0:T(8,128)S(1)} %all-to-all-done.rec), custom_call_target="tpu_custom_call" | custom-call | tf_op jit(solution)/shard_map/pallas_call | solution.py:685
  83.1 0.7 convert_element_type.10
  83.7 2.6 %all-to-all-start.1 = ((f16[32,16,128]{2,1,0:T(8,128)(2,1)}), f16[32,16,128]{2,1,0:T(8,128)(2,1)S(1)}, u32[]{:S(2)}, u32[]{:S(2)}) async-start(f16[32,16,128]{2,1,0:T(8,128)(2,1)} %convert_element_type.10), calls=%async_computation.1 | async-start | bytes 262144 | tf_op jit(solution)/shard_map/all_to_all | solution.py:698
  86.3 2.4 %shard_map.136 = (f32[128,128]{1,0:T(8,128)}, f32[3,128,128]{2,1,0:T(8,128)}) custom-call(s32[128,128]{1,0:T(8,128)} %bitcast.15, f32[4,144,128]{2,1,0:T(8,128)S(1)} %shard_map.134.mom, f32[8,8,128]{2,1,0:T(8,128)} %shard_map.135.unused), custom_call_target="tpu_custom_call" | custom-call | flops 1000000 | bytes 393216 | tf_op jit(solution)/shard_map/pallas_call | solution.py:570
  88.7 5.8 %all-to-all-done.1 = f16[32,16,128]{2,1,0:T(8,128)(2,1)S(1)} async-done(((f16[32,16,128]{2,1,0:T(8,128)(2,1)}), f16[32,16,128]{2,1,0:T(8,128)(2,1)S(1)}, u32[]{:S(2)}, u32[]{:S(2)}) %all-to-all-start.1) | async-done | bytes 131104 | tf_op jit(solution)/shard_map/all_to_all | solution.py:698
  94.5 1.0 %shard_map.139 = f32[32,128]{1,0:T(8,128)} custom-call(f32[32,16,128]{2,1,0:T(8,128)S(1)} %convert_element_type.11.got), custom_call_target="tpu_custom_call" | custom-call | flops 1000000 | bytes 262144 | tf_op jit(solution)/shard_map/pallas_call | solution.py:570
  (23 shorter events, 0.7 us)
Async XLA Ops:
  0.6 6.5 %copy-start.1 = (s32[256]{0:T(256)S(1)}, s32[256]{0:T(256)}, u32[]{:S(2)}) copy-start(s32[256]{0:T(256)} %param.16) | copy-start | bytes 3076
  0.6 6.5 %copy-start.2 = (s32[256]{0:T(256)S(1)}, s32[256]{0:T(256)}, u32[]{:S(2)}) copy-start(s32[256]{0:T(256)} %param.15) | copy-start | bytes 3076
  3.8 4.0 %collective-permute-start = (bf16[112,128]{1,0:T(8,128)(2,1)S(1)}, bf16[112,128]{1,0:T(8,128)(2,1)S(1)}, u32[]{:S(2)}, u32[]{:S(2)}) collective-permute-start(bf16[112,128]{1,0:T(8,128)(2,1)S(1)} %get-tuple-element.47), channel_id=1, source_target_pairs={{0,1},{1,2},{2,3},{3,0},{4,5},{5,6},{6,7},{7,4},{8,9},{9,10},{10,1... | collective-permute-start | bytes 86024 | tf_op jit(solution)/shard_map/ppermute | solution.py:626
  4.3 3.6 %collective-permute-start.1 = (bf16[112,128]{1,0:T(8,128)(2,1)S(1)}, bf16[112,128]{1,0:T(8,128)(2,1)S(1)}, u32[]{:S(2)}, u32[]{:S(2)}) collective-permute-start(bf16[112,128]{1,0:T(8,128)(2,1)S(1)} %get-tuple-element.48), channel_id=1, source_target_pairs={{0,3},{1,0},{2,1},{3,2},{4,7},{5,4},{6,5},{7,6},{8,11},{9,8},{10,9... | collective-permute-start | bytes 86024 | tf_op jit(solution)/shard_map/ppermute | solution.py:627
  7.9 27.6 %copy-start = (f32[3,256]{1,0:T(4,128)S(1)}, f32[3,256]{1,0:T(4,128)}, u32[]{:S(2)}) copy-start(f32[3,256]{1,0:T(4,128)} %area.1) | copy-start | bytes 9220
  10.1 12.5 %collective-permute-start.2 = (bf16[3,144,128]{2,1,0:T(8,128)(2,1)S(1)}, bf16[3,144,128]{2,1,0:T(8,128)(2,1)S(1)}, u32[]{:S(2)}, u32[]{:S(2)}) collective-permute-start(bf16[3,144,128]{2,1,0:T(8,128)(2,1)S(1)} %get-tuple-element.52), channel_id=1, source_target_pairs={{0,16},{16,0},{1,17},{17,1},{2,18},{18,2},{3,19},{19,3},{4,20},{20... | collective-permute-start | bytes 331784 | tf_op jit(solution)/shard_map/ppermute | solution.py:589
  12.3 3.8 %collective-permute-start.3 = (bf16[48,128]{1,0:T(8,128)(2,1)S(1)}, bf16[48,128]{1,0:T(8,128)(2,1)S(1)}, u32[]{:S(2)}, u32[]{:S(2)}) collective-permute-start(bf16[48,128]{1,0:T(8,128)(2,1)S(1)} %get-tuple-element.53), channel_id=1, source_target_pairs={{0,16},{16,0},{1,17},{17,1},{2,18},{18,2},{3,19},{19,3},{4,20},{20... | collective-permute-start | bytes 36872 | tf_op jit(solution)/shard_map/ppermute | solution.py:589
  16.2 6.1 %collective-permute-start.4 = (bf16[144,128]{1,0:T(8,128)(2,1)S(1)}, bf16[144,128]{1,0:T(8,128)(2,1)S(1)}, u32[]{:S(2)}, u32[]{:S(2)}) collective-permute-start(bf16[144,128]{1,0:T(8,128)(2,1)S(1)} %get-tuple-element.56), channel_id=1, source_target_pairs={{0,4},{4,8},{8,12},{12,0},{1,5},{5,9},{9,13},{13,1},{2,6},{6,10},{... | collective-permute-start | bytes 110600 | tf_op jit(solution)/shard_map/ppermute | solution.py:589
  18.0 4.5 %collective-permute-start.5 = (bf16[144,128]{1,0:T(8,128)(2,1)S(1)}, bf16[144,128]{1,0:T(8,128)(2,1)S(1)}, u32[]{:S(2)}, u32[]{:S(2)}) collective-permute-start(bf16[144,128]{1,0:T(8,128)(2,1)S(1)} %get-tuple-element.57), channel_id=1, source_target_pairs={{0,12},{4,0},{8,4},{12,8},{1,13},{5,1},{9,5},{13,9},{2,14},{6,2},{... | collective-permute-start | bytes 110600 | tf_op jit(solution)/shard_map/ppermute | solution.py:589
  26.3 11.2 %collective-permute-start.6 = (bf16[3,144,128]{2,1,0:T(8,128)(2,1)S(1)}, bf16[3,144,128]{2,1,0:T(8,128)(2,1)S(1)}, u32[]{:S(2)}, u32[]{:S(2)}) collective-permute-start(bf16[3,144,128]{2,1,0:T(8,128)(2,1)S(1)} %get-tuple-element.60), channel_id=1, source_target_pairs={{0,16},{16,0},{1,17},{17,1},{2,18},{18,2},{3,19},{19,3},{4,20},{20... | collective-permute-start | bytes 331784 | tf_op jit(solution)/shard_map/ppermute | solution.py:589
  27.8 3.7 %collective-permute-start.7 = (bf16[48,128]{1,0:T(8,128)(2,1)S(1)}, bf16[48,128]{1,0:T(8,128)(2,1)S(1)}, u32[]{:S(2)}, u32[]{:S(2)}) collective-permute-start(bf16[48,128]{1,0:T(8,128)(2,1)S(1)} %get-tuple-element.61), channel_id=1, source_target_pairs={{0,16},{16,0},{1,17},{17,1},{2,18},{18,2},{3,19},{19,3},{4,20},{20... | collective-permute-start | bytes 36872 | tf_op jit(solution)/shard_map/ppermute | solution.py:589
  31.6 5.8 %collective-permute-start.8 = (bf16[144,128]{1,0:T(8,128)(2,1)S(1)}, bf16[144,128]{1,0:T(8,128)(2,1)S(1)}, u32[]{:S(2)}, u32[]{:S(2)}) collective-permute-start(bf16[144,128]{1,0:T(8,128)(2,1)S(1)} %get-tuple-element.64), channel_id=1, source_target_pairs={{0,4},{4,8},{8,12},{12,0},{1,5},{5,9},{9,13},{13,1},{2,6},{6,10},{... | collective-permute-start | bytes 110600 | tf_op jit(solution)/shard_map/ppermute | solution.py:589
  32.6 4.8 %collective-permute-start.9 = (bf16[144,128]{1,0:T(8,128)(2,1)S(1)}, bf16[144,128]{1,0:T(8,128)(2,1)S(1)}, u32[]{:S(2)}, u32[]{:S(2)}) collective-permute-start(bf16[144,128]{1,0:T(8,128)(2,1)S(1)} %get-tuple-element.65), channel_id=1, source_target_pairs={{0,12},{4,0},{8,4},{12,8},{1,13},{5,1},{9,5},{13,9},{2,14},{6,2},{... | collective-permute-start | bytes 110600 | tf_op jit(solution)/shard_map/ppermute | solution.py:589
  40.6 10.8 %collective-permute-start.10 = (bf16[3,144,128]{2,1,0:T(8,128)(2,1)S(1)}, bf16[3,144,128]{2,1,0:T(8,128)(2,1)S(1)}, u32[]{:S(2)}, u32[]{:S(2)}) collective-permute-start(bf16[3,144,128]{2,1,0:T(8,128)(2,1)S(1)} %get-tuple-element.70), channel_id=1, source_target_pairs={{0,16},{16,0},{1,17},{17,1},{2,18},{18,2},{3,19},{19,3},{4,20},{20... | collective-permute-start | bytes 331784 | tf_op jit(solution)/shard_map/ppermute | solution.py:589
  41.8 3.7 %collective-permute-start.11 = (bf16[48,128]{1,0:T(8,128)(2,1)S(1)}, bf16[48,128]{1,0:T(8,128)(2,1)S(1)}, u32[]{:S(2)}, u32[]{:S(2)}) collective-permute-start(bf16[48,128]{1,0:T(8,128)(2,1)S(1)} %get-tuple-element.71), channel_id=1, source_target_pairs={{0,16},{16,0},{1,17},{17,1},{2,18},{18,2},{3,19},{19,3},{4,20},{20... | collective-permute-start | bytes 36872 | tf_op jit(solution)/shard_map/ppermute | solution.py:589
  45.6 5.8 %collective-permute-start.12 = (bf16[144,128]{1,0:T(8,128)(2,1)S(1)}, bf16[144,128]{1,0:T(8,128)(2,1)S(1)}, u32[]{:S(2)}, u32[]{:S(2)}) collective-permute-start(bf16[144,128]{1,0:T(8,128)(2,1)S(1)} %get-tuple-element.74), channel_id=1, source_target_pairs={{0,4},{4,8},{8,12},{12,0},{1,5},{5,9},{9,13},{13,1},{2,6},{6,10},{... | collective-permute-start | bytes 110600 | tf_op jit(solution)/shard_map/ppermute | solution.py:589
  46.6 4.8 %collective-permute-start.13 = (bf16[144,128]{1,0:T(8,128)(2,1)S(1)}, bf16[144,128]{1,0:T(8,128)(2,1)S(1)}, u32[]{:S(2)}, u32[]{:S(2)}) collective-permute-start(bf16[144,128]{1,0:T(8,128)(2,1)S(1)} %get-tuple-element.75), channel_id=1, source_target_pairs={{0,12},{4,0},{8,4},{12,8},{1,13},{5,1},{9,5},{13,9},{2,14},{6,2},{... | collective-permute-start | bytes 110600 | tf_op jit(solution)/shard_map/ppermute | solution.py:589
  54.5 10.9 %collective-permute-start.14 = (bf16[3,144,128]{2,1,0:T(8,128)(2,1)S(1)}, bf16[3,144,128]{2,1,0:T(8,128)(2,1)S(1)}, u32[]{:S(2)}, u32[]{:S(2)}) collective-permute-start(bf16[3,144,128]{2,1,0:T(8,128)(2,1)S(1)} %get-tuple-element.78), channel_id=1, source_target_pairs={{0,16},{16,0},{1,17},{17,1},{2,18},{18,2},{3,19},{19,3},{4,20},{20... | collective-permute-start | bytes 331784 | tf_op jit(solution)/shard_map/ppermute | solution.py:589
  55.7 3.7 %collective-permute-start.15 = (bf16[48,128]{1,0:T(8,128)(2,1)S(1)}, bf16[48,128]{1,0:T(8,128)(2,1)S(1)}, u32[]{:S(2)}, u32[]{:S(2)}) collective-permute-start(bf16[48,128]{1,0:T(8,128)(2,1)S(1)} %get-tuple-element.79), channel_id=1, source_target_pairs={{0,16},{16,0},{1,17},{17,1},{2,18},{18,2},{3,19},{19,3},{4,20},{20... | collective-permute-start | bytes 36872 | tf_op jit(solution)/shard_map/ppermute | solution.py:589
  59.5 5.9 %collective-permute-start.16 = (bf16[144,128]{1,0:T(8,128)(2,1)S(1)}, bf16[144,128]{1,0:T(8,128)(2,1)S(1)}, u32[]{:S(2)}, u32[]{:S(2)}) collective-permute-start(bf16[144,128]{1,0:T(8,128)(2,1)S(1)} %get-tuple-element.82), channel_id=1, source_target_pairs={{0,4},{4,8},{8,12},{12,0},{1,5},{5,9},{9,13},{13,1},{2,6},{6,10},{... | collective-permute-start | bytes 110600 | tf_op jit(solution)/shard_map/ppermute | solution.py:589
  60.7 4.7 %collective-permute-start.17 = (bf16[144,128]{1,0:T(8,128)(2,1)S(1)}, bf16[144,128]{1,0:T(8,128)(2,1)S(1)}, u32[]{:S(2)}, u32[]{:S(2)}) collective-permute-start(bf16[144,128]{1,0:T(8,128)(2,1)S(1)} %get-tuple-element.83), channel_id=1, source_target_pairs={{0,12},{4,0},{8,4},{12,8},{1,13},{5,1},{9,5},{13,9},{2,14},{6,2},{... | collective-permute-start | bytes 110600 | tf_op jit(solution)/shard_map/ppermute | solution.py:589
  64.0 10.3 %copy-start.3 = (s32[8,8]{1,0:T(8,128)S(1)}, s32[8,8]{1,0:T(8,128)}, u32[]{:S(2)}) copy-start(s32[8,8]{1,0:T(8,128)} %param.19) | copy-start | bytes 772
  68.6 12.5 %all-to-all-start = ((f32[8,8,128]{2,1,0:T(8,128)}), f32[8,8,128]{2,1,0:T(8,128)S(1)}, u32[]{:S(2)}, u32[]{:S(2)}) async-start(f32[8,8,128]{2,1,0:T(8,128)} %shard_map.135.unused), calls=%async_computation | async-start | bytes 65536 | tf_op jit(solution)/shard_map/all_to_all | solution.py:676
  83.7 10.8 %all-to-all-start.1 = ((f16[32,16,128]{2,1,0:T(8,128)(2,1)}), f16[32,16,128]{2,1,0:T(8,128)(2,1)S(1)}, u32[]{:S(2)}, u32[]{:S(2)}) async-start(f16[32,16,128]{2,1,0:T(8,128)(2,1)} %convert_element_type.10), calls=%async_computation.1 | async-start | bytes 262144 | tf_op jit(solution)/shard_map/all_to_all | solution.py:698
